TPU v7x, 32 devices: a whole 2x2x4 slice. The times are simulated.
32 devices in a mesh: tm: 2 (over x), lat: 16 (over z, y, core).
Axes of the slice: x: 2, y: 2, z: 4, core: 2. Of those that a mesh axis runs over, the one named last changes fastest.
Arguments:
- starts: float32 [2, 3, 8, 256, 512], P('tm', None, None, 'lat'), may hold values from -1.2 to 1.2
- coarse_old: float32 [2, 3, 8, 128, 256], P('tm', None, None, 'lat'), may hold values from -1.2 to 1.2
- mean_depth: float32 [8], replicated, may hold values from 0.5 to 2
- coupling: float32 [8, 8], replicated, may hold values from 0 to 1, as said below
- wet_cells: int32 [256, 512], P('lat'), may hold values 0 or 1
Outputs:
- new_ends: float32 [2, 3, 8, 256, 512], P('tm', None, None, 'lat')
- coarse_new: float32 [2, 3, 8, 128, 256], P('tm', None, None, 'lat')
Inputs may be any that keep to these rules, and one draw needn't show every extreme that they name: `coupling`: symmetric; each diagonal entry is at least 0.6 and exceeds the sum of magnitudes of the other entries of its row.
All inputs are finite; a program needn't handle non-finite values. No bound on the sum of `wet_cells` on one device may be relied on, other than what follows from the above.
Results may differ from a plain program's by a relative error of at most 0.00012.
Values sent between devices are 32-bit elements; how exact they have to be, the bound alone decides.
No kernel may reach another device: no remote copies, remote signals or barrier semaphores. Data moves between devices by JAX's collectives and lax.ppermute only.
A program may use at most 128 MiB of HBM per device.

v0:
```python
import functools

import jax
import jax.numpy as jnp
from jax import lax
from jax.experimental import pallas as pl
from jax.experimental.pallas import tpu as pltpu
from jax.sharding import PartitionSpec as P

STEPS = 4
HALO = 3 * STEPS

time_step = 0.15
viscosity = 0.02
rotation = 0.3

STAGE_WEIGHTS = (1.0, 0.25, 2.0 / 3.0)
PRESSURE_ROWS = 8
f32, bf16 = jnp.float32, jnp.bfloat16


def split_two(x):
    high = x.astype(bf16)
    return high, (x - high.astype(f32)).astype(bf16)


def split_three(x):
    high = x.astype(bf16)
    rest = x - high.astype(f32)
    middle = rest.astype(bf16)
    return high, middle, (rest - middle.astype(f32)).astype(bf16)


def tiles_of(x):
    fields, layers, rows, width = x.shape
    x = x.reshape(fields, layers, rows // 8, 8, width // 128, 128).transpose(0, 1, 2, 4, 3, 5)
    return x.reshape(fields, layers * rows * width // 128, 128)


def from_tiles(x, layers, rows, width):
    fields = x.shape[0]
    x = x.reshape(fields, layers, rows // 8, width // 128, 8, 128).transpose(0, 1, 2, 4, 3, 5)
    return x.reshape(fields, layers, rows, width)


def tile_slices(rows, width, r):
    blocks = width // 128
    return [pl.ds(((r // 8) * blocks + c) * 8 + r % 8, 8, stride=rows * blocks) for c in range(blocks)]


def load_row(tiles, field, rows, width, r):
    return jnp.concatenate([tiles[field, part, :] for part in tile_slices(rows, width, r)], axis=1)


def store_row(tiles, field, rows, width, r, value):
    for c, part in enumerate(tile_slices(rows, width, r)):
        tiles[field, part, :] = value[:, c * 128 : (c + 1) * 128]


def dot(a, b):
    return lax.dot_general(a, b, (((1,), (0,)), ((), ())), preferred_element_type=f32)


def east_west(x):
    width = x.shape[-1]
    return pltpu.roll(x, width - 1, 1), pltpu.roll(x, 1, 1)


def row_tendency(source, hv, press, r, depth, twice_viscosity, coriolis):
    e, u, v = source[0, r], source[1, r], source[2, r]
    u_north, u_south = source[1, r + 1], source[1, r - 1]
    v_north, v_south = source[2, r + 1], source[2, r - 1]
    hu_east, hu_west = east_west((depth + e) * u)
    divergence = (hu_east - hu_west) + (hv[r + 1] - hv[r - 1])
    u_east, u_west = east_west(u)
    v_east, v_west = east_west(v)
    p_east, p_west = east_west(press[r])
    to_east, to_west = twice_viscosity - u, twice_viscosity + u
    to_north, to_south = twice_viscosity - v, twice_viscosity + v
    centre = 4.0 * twice_viscosity
    zonal = (to_east * u_east + to_west * u_west) + (to_north * u_north + to_south * u_south)
    zonal = (zonal - (p_east - p_west)) + (coriolis * v - centre * u)
    merid = (to_east * v_east + to_west * v_west) + (to_north * v_north + to_south * v_south)
    merid = (merid - (press[r + 1] - press[r - 1])) - (coriolis * u + centre * v)
    return (e, u, v), (divergence, zonal, merid)


def pressure_rows(source, hv, press, start, count, kron_parts, depth):
    e = source[0, pl.ds(start, count)]
    v = source[2, pl.ds(start, count)]
    hv[pl.ds(start, count)] = (depth + e) * v
    layers, width = e.shape[1:]
    high, low = split_two(e.reshape(count * layers, width))
    kron_high, kron_low = kron_parts
    p = dot(kron_high, high) + dot(kron_high, low) + dot(kron_low, high)
    press[pl.ds(start, count)] = p.reshape(count, layers, width)


def pair_matrix(width, value):
    rows = lax.broadcasted_iota(jnp.int32, (width, width // 2), 0)
    columns = lax.broadcasted_iota(jnp.int32, (width, width // 2), 1)
    return jnp.where((rows >> 1) == columns, value, 0.0).astype(bf16)


def spread_matrix(width):
    rows = lax.broadcasted_iota(jnp.int32, (width // 2, width), 0)
    columns = lax.broadcasted_iota(jnp.int32, (width // 2, width), 1)
    return jnp.where((columns >> 1) == rows, 1.0, 0.0).astype(bf16)


def restrict_rows(state, field, first, count, pairs):
    fine = state[field, first : first + 2 * count]
    layers, width = fine.shape[1:]
    fine = fine.reshape(count, 2, layers, width)
    both = (fine[:, 0] + fine[:, 1]).reshape(count * layers, width)
    high, middle, low = split_three(both)
    coarse = dot(high, pairs) + dot(middle, pairs) + dot(low, pairs)
    return coarse.reshape(count, layers, width // 2)


def coarse_update(state, hv, press, wet, rows, depth, kron_parts, first_coriolis, coriolis_step, emit):
    scale = STEPS * time_step / 4.0
    pressure_rows(state, hv, press, 0, rows + 2, kron_parts, depth)
    for i in range(rows):
        coriolis = first_coriolis + coriolis_step * i
        (e, u, v), (de, du, dv) = row_tendency(state, hv, press, i + 1, depth, viscosity, coriolis)
        mask = wet[i] * scale
        emit(i, (e - scale * de, u + mask * du, v + mask * dv))


def pack_kernel(rows, starts, wet_cells, to_next, to_previous):
    wet = wet_cells[...].astype(f32)
    width = wet.shape[-1]
    planes = 3 * HALO
    for field in range(3):
        for i in range(HALO):
            to_next[field * HALO + i] = load_row(starts, field, rows, width, rows - HALO + i)
            to_previous[field * HALO + i] = load_row(starts, field, rows, width, i)
    to_next[planes] = wet[rows - HALO : rows - HALO + 8]
    to_next[planes + 1] = wet[rows - 8 :]
    to_previous[planes] = wet[:8]
    to_previous[planes + 1] = wet[HALO - 8 : HALO]


def main_kernel(
    rows, scalars, starts, before, after, wet_cells, coarse_old, mean_depth, fine_kron, coarse_kron,
    fine_end, delta, outcome, passed, coarse_wet,
    y, a, b, hv, press, wet, first, chv, cpress,
):
    total = rows + 2 * HALO
    width = wet_cells.shape[-1]
    coarse_rows = rows // 2
    planes = 3 * HALO
    first_coriolis, coriolis_step = scalars[0], scalars[1]
    top, bottom = scalars[2], scalars[3]
    depth = jnp.broadcast_to(mean_depth[...], (8, width))
    coarse_depth = jnp.broadcast_to(mean_depth[...], (8, width // 2))

    for field in range(3):
        y[field, 0:HALO] = before[field * HALO : (field + 1) * HALO]
        y[field, HALO + rows :] = after[field * HALO : (field + 1) * HALO]
        for i in range(rows):
            y[field, HALO + i] = load_row(starts, field, rows, width, i)
    own_wet = wet_cells[...].astype(f32)
    full = time_step / 2.0
    for i in range(HALO):
        place = (i // 8, i % 8) if i < 8 else (1, i - HALO + 8)
        wet[i] = jnp.broadcast_to(before[planes + place[0], place[1]][None] * full, (8, width))
        wet[HALO + rows + i] = jnp.broadcast_to(after[planes + place[0], place[1]][None] * full, (8, width))
    for i in range(rows):
        wet[HALO + i] = jnp.broadcast_to(own_wet[i][None] * full, (8, width))

    pairs = pair_matrix(width, 0.25)
    ones = pair_matrix(width, 1.0)
    for field in range(3):
        first[field] = restrict_rows(y, field, HALO - 2, coarse_rows + 2, pairs)
    for i in range(coarse_rows):
        north = wet[HALO + 2 * i]
        south = wet[HALO + 2 * i + 1]
        both = jnp.where((north > 0.5 * full) & (south > 0.5 * full), 1.0, 0.0).astype(bf16)
        coarse_wet[i] = jnp.maximum(dot(both, ones) - 1.0, 0.0)

    def emit(i, values):
        for field in range(3):
            outcome[field, i] = values[field]

    coarse_update(
        first, chv, cpress, coarse_wet, coarse_rows, coarse_depth, split_two(coarse_kron[...]),
        scalars[4], scalars[5], emit,
    )

    kron_parts = split_two(fine_kron[...])

    def stage(source, target, number, weights, which):
        low, high = number, total - number

        def fill(k, unused):
            start = jnp.minimum(low - 1 + k * PRESSURE_ROWS, high + 1 - PRESSURE_ROWS)
            pressure_rows(source, hv, press, start, PRESSURE_ROWS, kron_parts, depth)
            return unused

        lax.fori_loop(0, (high - low + 2 + PRESSURE_ROWS - 1) // PRESSURE_ROWS, fill, 0)

        factor = STAGE_WEIGHTS[which] * time_step / 2.0

        def one(r):
            coriolis = first_coriolis + coriolis_step * r.astype(f32)
            here, rates = row_tendency(source, hv, press, r, depth, 2.0 * viscosity, coriolis)
            mask = wet[r] * STAGE_WEIGHTS[which]
            inside = jnp.where(r < HALO, top, jnp.where(r >= HALO + rows, bottom, 1.0))
            scales = (-factor * inside, mask, mask)
            for field in range(3):
                value = here[field]
                if weights is not None:
                    value = weights[0] * y[field, r] + weights[1] * value
                target[field, r] = value + scales[field] * rates[field]

        def two(k, unused):
            one(low + 2 * k)
            one(low + 2 * k + 1)
            return unused

        lax.fori_loop(0, (high - low) // 2, two, 0)

    def step(k, unused):
        stage(y, a, 3 * k + 1, None, 0)
        stage(a, b, 3 * k + 2, (0.75, 0.25), 1)
        stage(b, y, 3 * k + 3, (1.0 / 3.0, 2.0 / 3.0), 2)
        return unused

    lax.fori_loop(0, STEPS, step, 0)

    for field in range(3):
        coarse = restrict_rows(y, field, HALO, coarse_rows, pairs)
        for i in range(coarse_rows):
            difference = coarse[i] - load_row(coarse_old, field, coarse_rows, width // 2, i)
            delta[field, i] = difference
            passed[field, i] = difference + outcome[field, i]
        fine_end[field] = y[field, HALO : HALO + rows]


def final_kernel(
    rows, scalars, incoming, before, after, previous, coarse_wet, coarse_old, mean_depth, coarse_kron, fine_end,
    new_ends, coarse_new,
    state, chv, cpress, change,
):
    coarse_rows = rows // 2
    width = fine_end.shape[-1]
    coarse_depth = jnp.broadcast_to(mean_depth[...], (8, width // 2))
    for field in range(3):
        state[field, 0] = before[field]
        state[field, coarse_rows + 1] = after[field]
        state[field, 1 : coarse_rows + 1] = incoming[field]
    last = scalars[6] > 0.5

    def emit(i, values):
        for field in range(3):
            value = jnp.where(last, values[field], previous[field, i])
            store_row(coarse_new, field, coarse_rows, width // 2, i, value)
            change[field, i] = value - load_row(coarse_old, field, coarse_rows, width // 2, i)

    coarse_update(
        state, chv, cpress, coarse_wet, coarse_rows, coarse_depth, split_two(coarse_kron[...]),
        scalars[4], scalars[5], emit,
    )
    spread = spread_matrix(width)
    for field in range(3):
        high, low = split_two(change[field].reshape(coarse_rows * 8, width // 2))
        fine = (dot(high, spread) + dot(low, spread)).reshape(coarse_rows, 8, width)
        for i in range(rows):
            store_row(new_ends, field, rows, width, i, fine_end[field, i] + fine[i // 2])


def middle_turn(incoming, before, after, coarse_wet, mean_depth, coupling, first_coriolis, coriolis_step):
    state = jnp.concatenate([before[:, None], incoming, after[:, None]], axis=1)
    e, u, v = state
    rows = incoming.shape[1]
    p = jnp.einsum("kl,rlc->rkc", coupling, e, precision=lax.Precision.HIGHEST)
    h = mean_depth[None, :, None] + e

    def dx(q):
        return (jnp.roll(q, -1, -1) - jnp.roll(q, 1, -1))[1:-1] / 4.0

    def dy(q):
        return (q[2:] - q[:-2]) / 4.0

    def lap(q):
        return (q[2:] + q[:-2] + (jnp.roll(q, -1, -1) + jnp.roll(q, 1, -1) - 4.0 * q)[1:-1]) / 4.0

    um, vm = u[1:-1], v[1:-1]
    f = (first_coriolis + coriolis_step * jnp.arange(rows, dtype=f32))[:, None, None] / 4.0
    de = -(dx(h * u) + dy(h * v))
    du = coarse_wet * (-(um * dx(u) + vm * dy(u)) + f * vm - dx(p) + viscosity * lap(u))
    dv = coarse_wet * (-(um * dx(v) + vm * dy(v)) - f * um - dy(p) + viscosity * lap(v))
    return incoming + STEPS * time_step * jnp.stack([de, du, dv])


def local(starts, coarse_old, mean_depth, coupling, wet_cells):
    layers, rows, width = starts.shape[2:]
    coarse_rows, half = rows // 2, width // 2
    assert layers == 8 and rows >= HALO
    tm, tm_size = lax.axis_index("tm"), lax.axis_size("tm")
    lat, lat_size = lax.axis_index("lat"), lax.axis_size("lat")
    total_rows = rows * lat_size
    starts = tiles_of(starts[0])
    coarse_old = tiles_of(coarse_old[0])
    vmem = pl.BlockSpec(memory_space=pltpu.VMEM)
    smem = pl.BlockSpec(memory_space=pltpu.SMEM)
    planes = 3 * HALO + 2

    to_next, to_previous = pl.pallas_call(
        functools.partial(pack_kernel, rows),
        out_shape=[jax.ShapeDtypeStruct((planes, 8, width), f32)] * 2,
        in_specs=[vmem] * 2,
        out_specs=[vmem] * 2,
    )(starts, wet_cells)
    up = [(i, i + 1) for i in range(lat_size - 1)]
    down = [(j, i) for i, j in up]
    before = lax.ppermute(to_next, "lat", up)
    after = lax.ppermute(to_previous, "lat", down)

    lat_f = lat.astype(f32)
    slope = 4.0 * rotation / total_rows
    coarse_slope = 16.0 * rotation / total_rows
    scalars = jnp.stack([
        slope * (lat_f * rows - HALO + 0.5) - 2.0 * rotation,
        jnp.asarray(slope, f32),
        (lat > 0).astype(f32),
        (lat < lat_size - 1).astype(f32),
        coarse_slope * (lat_f * coarse_rows + 0.5) - 4.0 * rotation,
        jnp.asarray(coarse_slope, f32),
        (tm == tm_size - 1).astype(f32),
    ])
    depth = mean_depth.reshape(layers, 1)


    def kron(count):
        return (jnp.eye(count, dtype=f32)[:, None, :, None] * coupling[None, :, None, :]).reshape(count * 8, count * 8)

    fine_kron, coarse_kron = kron(PRESSURE_ROWS), kron(coarse_rows + 2)
    coarse_shape = jax.ShapeDtypeStruct((3, coarse_rows, 8, half), f32)
    total = rows + 2 * HALO
    fine_end, delta, outcome, passed, coarse_wet = pl.pallas_call(
        functools.partial(main_kernel, rows),
        out_shape=[
            jax.ShapeDtypeStruct((3, rows, 8, width), f32),
            coarse_shape,
            coarse_shape,
            coarse_shape,
            jax.ShapeDtypeStruct((coarse_rows, 8, half), f32),
        ],
        in_specs=[smem] + [vmem] * 8,
        out_specs=[vmem] * 5,
        scratch_shapes=[pltpu.VMEM((3, total, 8, width), f32)] * 3
        + [pltpu.VMEM((total, 8, width), f32)] * 2
        + [pltpu.VMEM((total, 8, width), f32)]
        + [pltpu.VMEM((3, coarse_rows + 2, 8, half), f32)]
        + [pltpu.VMEM((coarse_rows + 2, 8, half), f32)] * 2,
    )(scalars, starts, before, after, wet_cells, coarse_old, depth, fine_kron, coarse_kron)

    both = ("tm", "lat")

    def hand_on(current):
        def moved(values, shift):
            pairs = [
                (t * lat_size + i, (t + 1) * lat_size + i + shift)
                for t in range(tm_size - 1)
                for i in range(lat_size)
                if 0 <= i + shift < lat_size
            ]
            return lax.ppermute(values, both, pairs)

        return moved(current, 0), moved(current[:, -1], 1), moved(current[:, 0], -1)

    previous = outcome
    incoming = hand_on(passed)
    for turn in range(1, tm_size - 1):
        outcome = middle_turn(*incoming, coarse_wet, mean_depth, coupling, scalars[4], scalars[5])
        previous = jnp.where(tm == turn, outcome, previous)
        incoming = hand_on(delta + outcome)

    new_ends, coarse_new = pl.pallas_call(
        functools.partial(final_kernel, rows),
        out_shape=[
            jax.ShapeDtypeStruct(starts.shape, f32),
            jax.ShapeDtypeStruct(coarse_old.shape, f32),
        ],
        in_specs=[smem] + [vmem] * 9,
        out_specs=[vmem] * 2,
        scratch_shapes=[pltpu.VMEM((3, coarse_rows + 2, 8, half), f32)]
        + [pltpu.VMEM((coarse_rows + 2, 8, half), f32)] * 2
        + [pltpu.VMEM((3, coarse_rows, 8, half), f32)],
    )(scalars, *incoming, previous, coarse_wet, coarse_old, depth, coarse_kron, fine_end)
    return (
        from_tiles(new_ends, layers, rows, width)[None],
        from_tiles(coarse_new, layers, coarse_rows, half)[None],
    )


def solution(mesh):
    in_specs = (
        P("tm", None, None, "lat", None),
        P("tm", None, None, "lat", None),
        P(),
        P(),
        P("lat", None),
    )
    out_specs = (P("tm", None, None, "lat", None), P("tm", None, None, "lat", None))
    return jax.shard_map(local, mesh=mesh, in_specs=in_specs, out_specs=out_specs, check_vma=False)
```

profile of v0, /device:TPU:1, one launch (start us, length us, event | category | flops | bytes accessed | tf_op | source)
XLA Modules:
  0.0 74.5 jit_solution(8023763694437672776)
XLA Ops:
  0.6 2.9 %shard_map.68 = (f32[38,8,512]{2,1,0:T(8,128)}, f32[38,8,512]{2,1,0:T(8,128)}) custom-call(f32[3,512,128]{2,1,0:T(8,128)} %bitcast.32, s32[16,512]{1,0:T(8,128)} %wet_cells.3), custom_call_target="tpu_custom_call" | custom-call | tf_op jit(solution)/shard_map/pallas_call | solution.py:311
  3.5 4.5 %collective-permute-start = (f32[38,8,512]{2,1,0:T(8,128)}, f32[38,8,512]{2,1,0:T(8,128)S(1)}, u32[]{:S(2)}, u32[]{:S(2)}) collective-permute-start(f32[38,8,512]{2,1,0:T(8,128)} %get-tuple-element.10), channel_id=1, source_target_pairs={{0,1},{1,2},{2,3},{3,4},{4,5},{5,6},{6,7},{7,8},{8,9},{9,10},{10,1... | collective-permute-start | bytes 1867784 | tf_op jit(solution)/shard_map/ppermute | solution.py:319
  8.0 1.9 %collective-permute-start.1 = (f32[38,8,512]{2,1,0:T(8,128)}, f32[38,8,512]{2,1,0:T(8,128)S(1)}, u32[]{:S(2)}, u32[]{:S(2)}) collective-permute-start(f32[38,8,512]{2,1,0:T(8,128)} %get-tuple-element.11), channel_id=1, source_target_pairs={{1,0},{2,1},{3,2},{4,3},{5,4},{6,5},{7,6},{8,7},{9,8},{10,9},{11,1... | collective-permute-start | bytes 1867784 | tf_op jit(solution)/shard_map/ppermute | solution.py:320
  10.0 0.0 copy-start.6
  10.0 0.0 copy-start.5
  10.0 0.6 copy-done.6
  10.6 0.7 copy.11.mean_depth
  11.3 0.0 copy-done.5
  11.3 0.1 broadcast_multiply_fusion.1
  11.4 0.7 mul.53.fine_kron
  12.1 0.1 broadcast_multiply_fusion
  12.2 0.8 %mul.57.coarse_kron = f32[80,80]{1,0:T(8,128)} reshape(f32[10,8,10,8]{3,2,1,0:T(8,128)S(1)} %broadcast_multiply_fusion) | data formatting | bytes 51200 | tf_op jit(solution)/shard_map/mul | solution.py:338
  13.1 0.7 stack.35.scalars
  13.7 8.4 %collective-permute-done.before = f32[38,8,512]{2,1,0:T(8,128)S(1)} collective-permute-done((f32[38,8,512]{2,1,0:T(8,128)}, f32[38,8,512]{2,1,0:T(8,128)S(1)}, u32[]{:S(2)}, u32[]{:S(2)}) %collective-permute-start) | collective-permute-done | bytes 622624 | tf_op jit(solution)/shard_map/ppermute | solution.py:319
  22.2 0.0 copy-start
  22.2 0.0 collective-permute-done.1.after
  22.2 0.0 copy-start.1
  22.2 0.8 %copy-done = f32[38,8,512]{2,1,0:T(8,128)} copy-done((f32[38,8,512]{2,1,0:T(8,128)}, f32[38,8,512]{2,1,0:T(8,128)S(1)}, u32[]{:S(2)}) %copy-start) | copy-done | bytes 622616
  23.0 0.2 copy-done.1
  23.2 37.7 %shard_map.69 = (f32[3,16,8,512]{3,2,1,0:T(8,128)}, f32[3,8,8,256]{3,2,1,0:T(8,128)}, f32[3,8,8,256]{3,2,1,0:T(8,128)}, f32[3,8,8,256]{3,2,1,0:T(8,128)}, f32[8,8,256]{2,1,0:T(8,128)}) custom-call(f32[7]{0:T(128)} %stack.35.scalars, f32[3,512,128]{2,1,0:T(8,128)} %bitcast.33, f32[38,8,512]{2,1,0:T(8,128)} %copy-done, f32[38,8,512]{2,1,0:T(8,128)} %copy-done.1, ...), custom_call_target="tpu_custom_call" | custom-call | tf_op jit(solution)/shard_map/pallas_call | solution.py:343
  60.9 3.1 %collective-permute-start.2 = (f32[3,8,8,256]{3,2,1,0:T(8,128)}, f32[3,8,8,256]{3,2,1,0:T(8,128)S(1)}, u32[]{:S(2)}, u32[]{:S(2)}) collective-permute-start(f32[3,8,8,256]{3,2,1,0:T(8,128)} %get-tuple-element.12), channel_id=1, source_target_pairs={{0,16},{1,17},{2,18},{3,19},{4,20},{5,21},{6,22},{7,23},{8,24},{9,... | collective-permute-start | bytes 589832 | tf_op jit(solution)/shard_map/ppermute | solution.py:371
  64.0 0.8 %slice_bitcast_fusion = (f32[3,8,256]{2,1,0:T(8,128)S(1)}, f32[3,8,256]{2,1,0:T(8,128)S(1)}) fusion(f32[3,8,8,256]{3,2,1,0:T(8,128)} %get-tuple-element.12), kind=kLoop, calls=%fused_computation.2 | loop fusion | bytes 98304 | tf_op jit(solution)/shard_map/squeeze | solution.py:373
  64.8 1.3 %collective-permute-start.4 = (f32[3,8,256]{2,1,0:T(8,128)S(1)}, f32[3,8,256]{2,1,0:T(8,128)S(1)}, u32[]{:S(2)}, u32[]{:S(2)}) collective-permute-start(f32[3,8,256]{2,1,0:T(8,128)S(1)} %get-tuple-element.18), channel_id=1, source_target_pairs={{1,16},{2,17},{3,18},{4,19},{5,20},{6,21},{7,22},{8,23},{9,24},{10... | collective-permute-start | bytes 73736 | tf_op jit(solution)/shard_map/ppermute | solution.py:371
  66.1 3.4 %collective-permute-start.3 = (f32[3,8,256]{2,1,0:T(8,128)S(1)}, f32[3,8,256]{2,1,0:T(8,128)S(1)}, u32[]{:S(2)}, u32[]{:S(2)}) collective-permute-start(f32[3,8,256]{2,1,0:T(8,128)S(1)} %get-tuple-element.19), channel_id=1, source_target_pairs={{0,17},{1,18},{2,19},{3,20},{4,21},{5,22},{6,23},{7,24},{8,25},{9,... | collective-permute-start | bytes 73736 | tf_op jit(solution)/shard_map/ppermute | solution.py:371
  69.5 0.0 collective-permute-done.4.after
  69.5 0.0 copy-start.3
  69.5 0.9 %collective-permute-done.3.before = f32[3,8,256]{2,1,0:T(8,128)S(1)} collective-permute-done((f32[3,8,256]{2,1,0:T(8,128)S(1)}, f32[3,8,256]{2,1,0:T(8,128)S(1)}, u32[]{:S(2)}, u32[]{:S(2)}) %collective-permute-start.3) | collective-permute-done | bytes 24608 | tf_op jit(solution)/shard_map/ppermute | solution.py:371
  70.4 0.0 copy-start.4
  70.4 0.0 collective-permute-done.2.incoming
  70.4 0.0 copy-start.2
  70.4 0.0 copy-done.3
  70.4 0.6 copy-done.4
  71.0 0.1 copy-done.2
  71.1 3.3 %shard_map.70 = (f32[3,512,128]{2,1,0:T(8,128)}, f32[3,128,128]{2,1,0:T(8,128)}) custom-call(f32[7]{0:T(128)} %stack.35.scalars, f32[3,8,8,256]{3,2,1,0:T(8,128)} %copy-done.2, f32[3,8,256]{2,1,0:T(8,128)} %copy-done.4, f32[3,8,256]{2,1,0:T(8,128)} %copy-done.3, f32[3,8,8,256]{3,2,1,0:T(8,128)} %get-tuple-element.13.previous, ...), custom_call_target="tpu_custom_call" | custom-call | tf_op jit(solution)/shard_map/pallas_call | solution.py:382
  (2 shorter events, 0.0 us)
Async XLA Ops:
  3.5 18.7 %collective-permute-start = (f32[38,8,512]{2,1,0:T(8,128)}, f32[38,8,512]{2,1,0:T(8,128)S(1)}, u32[]{:S(2)}, u32[]{:S(2)}) collective-permute-start(f32[38,8,512]{2,1,0:T(8,128)} %get-tuple-element.10), channel_id=1, source_target_pairs={{0,1},{1,2},{2,3},{3,4},{4,5},{5,6},{6,7},{7,8},{8,9},{9,10},{10,1... | collective-permute-start | bytes 1867784 | tf_op jit(solution)/shard_map/ppermute | solution.py:319
  8.0 14.1 %collective-permute-start.1 = (f32[38,8,512]{2,1,0:T(8,128)}, f32[38,8,512]{2,1,0:T(8,128)S(1)}, u32[]{:S(2)}, u32[]{:S(2)}) collective-permute-start(f32[38,8,512]{2,1,0:T(8,128)} %get-tuple-element.11), channel_id=1, source_target_pairs={{1,0},{2,1},{3,2},{4,3},{5,4},{6,5},{7,6},{8,7},{9,8},{10,9},{11,1... | collective-permute-start | bytes 1867784 | tf_op jit(solution)/shard_map/ppermute | solution.py:320
  10.0 0.7 copy-start.6
  10.0 1.3 %copy-start.5 = (f32[8,8]{1,0:T(8,128)S(1)}, f32[8,8]{1,0:T(8,128)}, u32[]{:S(2)}) copy-start(f32[8,8]{1,0:T(8,128)} %param.8) | copy-start | bytes 772
  22.2 0.8 %copy-start = (f32[38,8,512]{2,1,0:T(8,128)}, f32[38,8,512]{2,1,0:T(8,128)S(1)}, u32[]{:S(2)}) copy-start(f32[38,8,512]{2,1,0:T(8,128)S(1)} %collective-permute-done.before) | copy-start | bytes 1867780
  22.2 1.0 %copy-start.1 = (f32[38,8,512]{2,1,0:T(8,128)}, f32[38,8,512]{2,1,0:T(8,128)S(1)}, u32[]{:S(2)}) copy-start(f32[38,8,512]{2,1,0:T(8,128)S(1)} %collective-permute-done.1.after) | copy-start | bytes 1867780
  60.9 9.5 %collective-permute-start.2 = (f32[3,8,8,256]{3,2,1,0:T(8,128)}, f32[3,8,8,256]{3,2,1,0:T(8,128)S(1)}, u32[]{:S(2)}, u32[]{:S(2)}) collective-permute-start(f32[3,8,8,256]{3,2,1,0:T(8,128)} %get-tuple-element.12), channel_id=1, source_target_pairs={{0,16},{1,17},{2,18},{3,19},{4,20},{5,21},{6,22},{7,23},{8,24},{9,... | collective-permute-start | bytes 589832 | tf_op jit(solution)/shard_map/ppermute | solution.py:371
  64.8 4.7 %collective-permute-start.4 = (f32[3,8,256]{2,1,0:T(8,128)S(1)}, f32[3,8,256]{2,1,0:T(8,128)S(1)}, u32[]{:S(2)}, u32[]{:S(2)}) collective-permute-start(f32[3,8,256]{2,1,0:T(8,128)S(1)} %get-tuple-element.18), channel_id=1, source_target_pairs={{1,16},{2,17},{3,18},{4,19},{5,20},{6,21},{7,22},{8,23},{9,24},{10... | collective-permute-start | bytes 73736 | tf_op jit(solution)/shard_map/ppermute | solution.py:371
  66.1 4.3 %collective-permute-start.3 = (f32[3,8,256]{2,1,0:T(8,128)S(1)}, f32[3,8,256]{2,1,0:T(8,128)S(1)}, u32[]{:S(2)}, u32[]{:S(2)}) collective-permute-start(f32[3,8,256]{2,1,0:T(8,128)S(1)} %get-tuple-element.19), channel_id=1, source_target_pairs={{0,17},{1,18},{2,19},{3,20},{4,21},{5,22},{6,23},{7,24},{8,25},{9,... | collective-permute-start | bytes 73736 | tf_op jit(solution)/shard_map/ppermute | solution.py:371
  69.5 0.9 %copy-start.3 = (f32[3,8,256]{2,1,0:T(8,128)}, f32[3,8,256]{2,1,0:T(8,128)S(1)}, u32[]{:S(2)}) copy-start(f32[3,8,256]{2,1,0:T(8,128)S(1)} %collective-permute-done.4.after) | copy-start | bytes 73732
  70.4 0.6 copy-start.4
  70.4 0.7 copy-start.2
where the time goes:
time: 74.8 us; the launch traced here: 74.5 us
  Pallas kernels  43.9 us (59%)
  starting transfers between devices  14.2 us (19%)
  waiting for transfers between devices  9.35 us (12%)
  local copies, waits for them, and re-layouts  6.04 us (8%)
  between operations  0.75 us (1%)
    pallas_call x1, Pallas kernels, local(): pl.pallas_call(functools.partial(main_kernel, rows), out_shape=[jax.Shape...  37.7 us
    ppermute x1, waiting for transfers between devices, local(): before = lax.ppermute(to_next, 'lat', up)  8.43 us
    ppermute x3, starting transfers between devices, moved(): return lax.ppermute(values, both, pairs)  7.75 us
    ppermute x1, starting transfers between devices, local(): before = lax.ppermute(to_next, 'lat', up)  4.51 us
    pallas_call x1, Pallas kernels, local(): pl.pallas_call(functools.partial(final_kernel, rows), out_shape=[jax.Shap...  3.35 us
    pallas_call x1, Pallas kernels, local(): pl.pallas_call(functools.partial(pack_kernel, rows), out_shape=[jax.Shape...  2.86 us
    unnamed x14, local copies, waits for them, and re-layouts  2.37 us
    ppermute x1, starting transfers between devices, local(): after = lax.ppermute(to_previous, 'lat', down)  1.92 us
  transfers between devices with their start and end apart: 5, of which 2 were waited for; matrix products, arithmetic and copies ran while one was open for 5% of the time, Pallas kernels for 0%

commit v1 on v0

v1 whole, which is shorter than its diff:
```python
import functools

import jax
import jax.numpy as jnp
import numpy as np
from jax import lax
from jax.experimental import pallas as pl
from jax.experimental.pallas import tpu as pltpu
from jax.sharding import PartitionSpec as P

STEPS = 4
HALO = 3 * STEPS
CHUNK = 8
LANES = 128

time_step = 0.15
viscosity = 0.02
rotation = 0.3

STAGE_WEIGHTS = (1.0, 0.25, 2.0 / 3.0)
STAGE_MIX = (None, (0.75, 0.25), (1.0 / 3.0, 2.0 / 3.0))
f32, bf16 = jnp.float32, jnp.bfloat16


def interleave_matrix(width):
    blocks = width // LANES
    place = np.arange(width)
    columns = blocks * (place % LANES) + place // LANES
    return (np.arange(width)[:, None] == columns[None, :]).astype(np.float32)


def prolong_matrix(width):
    half = width // 2
    blocks = half // LANES
    place = np.arange(half)
    columns = blocks * (place % LANES) + place // LANES
    return (columns[:, None] == np.arange(width)[None, :] // 2).astype(np.float32)


def tiles_of(x):
    fields, layers, rows, width = x.shape
    x = x.reshape(fields, layers, rows // 8, 8, width // LANES, LANES).transpose(0, 1, 2, 4, 3, 5)
    return x.reshape(fields, layers * rows * width // LANES, LANES)


def from_tiles(x, layers, rows, width):
    fields = x.shape[0]
    x = x.reshape(fields, layers, rows // 8, width // LANES, 8, LANES).transpose(0, 1, 2, 4, 3, 5)
    return x.reshape(fields, layers, rows, width)


def tile_slices(rows, width, r):
    blocks = width // LANES
    return [pl.ds(((r // 8) * blocks + c) * 8 + r % 8, 8, stride=rows * blocks) for c in range(blocks)]


def load_row(tiles, field, rows, width, r):
    return jnp.concatenate([tiles[field, part, :] for part in tile_slices(rows, width, r)], axis=1)


def store_row(tiles, field, rows, width, r, value):
    for c, part in enumerate(tile_slices(rows, width, r)):
        tiles[field, part, :] = value[:, c * LANES : (c + 1) * LANES]


def blocks_of(x):
    return [x[:, c : c + LANES] for c in range(0, x.shape[1], LANES)]


def east_west(x):
    blocks = blocks_of(x)
    east = jnp.concatenate(blocks[1:] + [pltpu.roll(blocks[0], LANES - 1, 1)], axis=1)
    west = jnp.concatenate([pltpu.roll(blocks[-1], 1, 1)] + blocks[:-1], axis=1)
    return east, west


def restrict_pair(north, south):
    blocks = blocks_of(north + south)
    return 0.25 * jnp.concatenate([a + b for a, b in zip(blocks[0::2], blocks[1::2])], axis=1)


def split(x, parts):
    found = []
    for _ in range(parts - 1):
        found.append(x.astype(bf16))
        x = x - found[-1].astype(f32)
    return found + [x.astype(bf16)]


def dot(a, b):
    return lax.dot_general(a, b, (((1,), (0,)), ((), ())), preferred_element_type=f32)


def select(x, matrix, parts):
    return sum(dot(part, matrix) for part in split(x, parts))


def coupling_parts(tripled):
    high = tripled.astype(bf16).astype(f32)
    lane = lax.broadcasted_iota(jnp.int32, tripled.shape, 1)
    return jnp.where(lane < 2 * tripled.shape[0], high, tripled - high).astype(bf16)


def pressure_rows(source, hv, press, start, count, kron_parts, depth):
    e = source[0, pl.ds(start, count)]
    v = source[2, pl.ds(start, count)]
    hv[pl.ds(start, count)] = (depth + e) * v
    layers, width = e.shape[1:]
    high, low = split(e.reshape(count * layers, width), 2)
    p = dot(kron_parts, jnp.concatenate([high, low, high], axis=0))
    press[pl.ds(start, count)] = p.reshape(count, layers, width)


def row_tendency(source, hv, press, r, depth, twice_viscosity, coriolis):
    e, u, v = source[0, r], source[1, r], source[2, r]
    u_north, u_south = source[1, r + 1], source[1, r - 1]
    v_north, v_south = source[2, r + 1], source[2, r - 1]
    hu_east, hu_west = east_west((depth + e) * u)
    divergence = (hu_east - hu_west) + (hv[r + 1] - hv[r - 1])
    u_east, u_west = east_west(u)
    v_east, v_west = east_west(v)
    p_east, p_west = east_west(press[r])
    to_east, to_west = twice_viscosity - u, twice_viscosity + u
    to_north, to_south = twice_viscosity - v, twice_viscosity + v
    centre = 4.0 * twice_viscosity
    zonal = (to_east * u_east + to_west * u_west) + (to_north * u_north + to_south * u_south)
    zonal = (zonal - (p_east - p_west)) + (coriolis * v - centre * u)
    merid = (to_east * v_east + to_west * v_west) + (to_north * v_north + to_south * v_south)
    merid = (merid - (press[r + 1] - press[r - 1])) - (coriolis * u + centre * v)
    return (e, u, v), (divergence, zonal, merid)


def run_stage(source, target, base, hv, press, wet, low, high, which, kron_parts, depth, coriolis_of, inside_of):
    count = jnp.maximum(high - low, 0)

    def fill(k, unused):
        start = jnp.minimum(low - 1 + k * CHUNK, high + 1 - CHUNK)
        pressure_rows(source, hv, press, start, CHUNK, kron_parts[...], depth)
        return unused

    chunks = jnp.where(count > 0, (count + 2 + CHUNK - 1) // CHUNK, 0)
    lax.fori_loop(0, chunks, fill, 0)
    factor = STAGE_WEIGHTS[which] * time_step / 2.0
    mix = STAGE_MIX[which]

    def one(r):
        here, rates = row_tendency(source, hv, press, r, depth, 2.0 * viscosity, coriolis_of(r))
        mask = wet[r] * factor
        scales = (-factor * inside_of(r), mask, mask)
        for field in range(3):
            value = here[field]
            if mix is not None:
                value = mix[0] * base[field, r] + mix[1] * value
            target[field, r] = value + scales[field] * rates[field]

    def two(k, unused):
        one(low + 2 * k)
        one(low + 2 * k + 1)
        return unused

    lax.fori_loop(0, count // 2, two, 0)


def coarse_update(state, hv, press, wet, rows, depth, kron_parts, first_coriolis, coriolis_step, emit):
    scale = STEPS * time_step / 4.0
    start = 0
    while start < rows + 2:
        pressure_rows(state, hv, press, min(start, rows + 2 - CHUNK), CHUNK, kron_parts, depth)
        start += CHUNK
    for i in range(rows):
        coriolis = first_coriolis + coriolis_step * i
        (e, u, v), (de, du, dv) = row_tendency(state, hv, press, i + 1, depth, viscosity, coriolis)
        mask = wet[i] * scale
        emit(i, (e - scale * de, u + mask * du, v + mask * dv))


class Fetch:
    def __init__(self, semaphores):
        self.semaphores, self.copies = semaphores, []

    def __call__(self, source, target):
        copy = pltpu.make_async_copy(source, target, self.semaphores.at[len(self.copies)])
        copy.start()
        self.copies.append(copy)

    def wait(self):
        for copy in self.copies:
            copy.wait()


def wet_row(halo, i):
    plane, row = (0, i) if i < 8 else (1, i - HALO + 8)
    return halo[3 * HALO + plane, pl.ds(row, 1), :]


def pack_kernel(rows, starts, wet_cells, matrix, to_next, to_previous):
    width = wet_cells.shape[-1]
    order = matrix[...]
    for field in range(3):
        state = jnp.concatenate([load_row(starts, field, rows, width, i) for i in range(rows)], axis=0)
        state = select(state, order, 2).reshape(rows, 8, width)
        to_next[field * HALO : (field + 1) * HALO] = state[rows - HALO :]
        to_previous[field * HALO : (field + 1) * HALO] = state[:HALO]
    wet = dot(wet_cells[...].astype(f32).astype(bf16), order)
    planes = 3 * HALO
    to_next[planes] = wet[rows - HALO : rows - HALO + 8]
    to_next[planes + 1] = wet[rows - 8 :]
    to_previous[planes] = wet[:8]
    to_previous[planes + 1] = wet[HALO - 8 : HALO]


def inner_kernel(
    rows, scalars, to_next, to_previous, coarse_old, mean_depth, tripled, matrix,
    north_strips, south_strips, coarse_before, first, coarse_wet,
    y, a, b, hv, press, wet, kron_parts,
):
    width = to_next.shape[-1]
    depth = jnp.broadcast_to(mean_depth[...], (8, width))
    kron_parts[...] = coupling_parts(tripled[...])
    for i in range(rows):
        halo, at = (to_previous, i) if i < HALO else (to_next, i - rows + HALO)
        for field in range(3):
            y[field, i] = halo[field * HALO + at]
        wet[i] = jnp.broadcast_to(wet_row(halo, at), (8, width))

    def coriolis_of(r):
        return scalars[0] + scalars[1] * r.astype(f32)

    def keep(state, t):
        for field in range(3):
            north_strips[t, field] = state[field, pl.ds(t, 3)]
            south_strips[t, field] = state[field, pl.ds(rows - 3 - t, 3)]

    keep(y, 0)

    def step(k, unused):
        for which, (source, target) in enumerate(((y, a), (a, b), (b, y))):
            s = 3 * k + which + 1
            run_stage(
                source, target, y, hv, press, wet, s, rows - s, which, kron_parts, depth, coriolis_of, lambda r: 1.0
            )

            @pl.when(s < rows // 2)
            def _():
                keep(target, s)

        return unused

    coarse_rows = rows // 2
    for i in range(coarse_rows):
        both = wet[2 * i] * wet[2 * i + 1]
        blocks = blocks_of(both)
        coarse_wet[i] = jnp.concatenate([p * q for p, q in zip(blocks[0::2], blocks[1::2])], axis=1)
        for field in range(3):
            first[field, i] = restrict_pair(y[field, 2 * i], y[field, 2 * i + 1])
    order = matrix[...]
    for field in range(3):
        old = [load_row(coarse_old, field, coarse_rows, width // 2, i) for i in range(coarse_rows)]
        old = select(jnp.concatenate(old, axis=0), order, 3)
        coarse_before[field] = old.reshape(coarse_rows, 8, width // 2)
    lax.fori_loop(0, (rows // 2 + 1) // 3, step, 0)


def north_kernel(
    rows, scalars, before, to_previous, strips, mean_depth, tripled,
    end_rows, south_strips,
    y, a, b, hv, press, wet, kron_parts, strip, masks, semaphores,
):
    width = y.shape[-1]
    half = rows // 2
    fetch = Fetch(semaphores)
    for field in range(3):
        fetch(before.at[pl.ds(field * HALO, HALO)], y.at[field, pl.ds(0, HALO)])
    fetch(strips, strip)
    fetch(before.at[pl.ds(3 * HALO, 2)], masks.at[0])
    fetch(to_previous.at[pl.ds(3 * HALO, 2)], masks.at[1])
    depth = jnp.broadcast_to(mean_depth[...], (8, width))
    kron_parts[...] = coupling_parts(tripled[...])
    fetch.wait()
    for i in range(HALO + half):
        side, at = (0, i) if i < HALO else (1, i - HALO)
        plane, row = (0, at) if at < 8 else (1, at - HALO + 8)
        wet[i] = jnp.broadcast_to(masks[side, plane, pl.ds(row, 1), :], (8, width))

    def coriolis_of(r):
        return scalars[0] + scalars[1] * (r - HALO).astype(f32)

    def inside_of(r):
        return jnp.where(r < HALO, scalars[2], 1.0)

    def step(k, unused):
        for which, (source, target) in enumerate(((y, a), (a, b), (b, y))):
            t = 3 * k + which
            s = t + 1

            @pl.when(t < half)
            def _():
                for field in range(3):
                    for i in range(3 if which == 0 else 2):
                        source[field, HALO + t + i] = strip[t, field, i]

            high = HALO + jnp.minimum(s, rows - s)
            run_stage(
                source, target, y, hv, press, wet, s, high, which, kron_parts, depth, coriolis_of, inside_of
            )

            @pl.when((s >= half) & (s < HALO))
            def _():
                for field in range(3):
                    south_strips[s - half, field] = target[field, pl.ds(HALO + rows - 3 - s, 3)]

        return unused

    lax.fori_loop(0, STEPS, step, 0)
    for field in range(3):
        end_rows[field] = y[field, HALO : HALO + rows - HALO]


def south_kernel(
    rows, scalars, after, to_next, before, inner_strips, north_strips, first_rows, first, coarse_before, coarse_wet,
    mean_depth, tripled,
    end_rows, delta, outcome, passed,
    y, a, b, hv, press, wet, kron_parts, inner_strip, north_strip, masks, state, edge, old, semaphores,
):
    width = y.shape[-1]
    half = rows // 2
    origin = rows - HALO - 1
    own = rows - origin
    coarse_rows = rows // 2
    fetch = Fetch(semaphores)
    for field in range(3):
        fetch(after.at[pl.ds(field * HALO, HALO)], y.at[field, pl.ds(own, HALO)])
        fetch(before.at[pl.ds(field * HALO + HALO - 2, 2)], edge.at[field])
        fetch(first.at[field], state.at[field, pl.ds(1, coarse_rows)])
    fetch(inner_strips, inner_strip)
    fetch(north_strips, north_strip)
    fetch(after.at[pl.ds(3 * HALO, 2)], masks.at[0])
    fetch(to_next.at[pl.ds(3 * HALO, 2)], masks.at[1])
    fetch(coarse_before, old)
    depth = jnp.broadcast_to(mean_depth[...], (8, width))
    coarse_depth = jnp.broadcast_to(mean_depth[...], (8, width // 2))
    kron_parts[...] = coupling_parts(tripled[...])
    fetch.wait()
    for i in range(HALO):
        plane, row = (0, i) if i < 8 else (1, i - HALO + 8)
        wet[own + i] = jnp.broadcast_to(masks[0, plane, pl.ds(row, 1), :], (8, width))
        wet[own - HALO + i] = jnp.broadcast_to(masks[1, plane, pl.ds(row, 1), :], (8, width))

    for field in range(3):
        state[field, 0] = restrict_pair(edge[field, 0], edge[field, 1])
        state[field, coarse_rows + 1] = restrict_pair(y[field, own], y[field, own + 1])

    def emit(i, values):
        for field in range(3):
            outcome[field, i] = values[field]

    coarse_update(
        state, hv.at[:, :, pl.ds(0, width // 2)], press.at[:, :, pl.ds(0, width // 2)], coarse_wet, coarse_rows,
        coarse_depth, kron_parts[...], scalars[4], scalars[5], emit,
    )

    def coriolis_of(r):
        return scalars[0] + scalars[1] * (r + origin).astype(f32)

    def inside_of(r):
        return jnp.where(r < own, 1.0, scalars[3])

    def step(k, unused):
        for which, (source, target) in enumerate(((y, a), (a, b), (b, y))):
            t = 3 * k + which
            s = t + 1
            skip = 0 if which == 0 else 1

            def insert(strip, index):
                for field in range(3):
                    for i in range(skip, 3):
                        source[field, own - 3 - t + i] = strip[index, field, i]

            @pl.when(t < half)
            def _():
                insert(inner_strip, t)

            @pl.when(t >= half)
            def _():
                insert(north_strip, t - half)

            low = own - s
            run_stage(
                source, target, y, hv, press, wet, low, low + HALO, which, kron_parts, depth, coriolis_of, inside_of
            )
        return unused

    lax.fori_loop(0, STEPS, step, 0)
    early = rows - HALO
    for field in range(3):
        end_rows[field] = y[field, own - HALO : own]
        for i in range(coarse_rows):
            if 2 * i < early:
                pair = first_rows[field, 2 * i], first_rows[field, 2 * i + 1]
            else:
                pair = y[field, 2 * i - origin], y[field, 2 * i + 1 - origin]
            difference = restrict_pair(*pair) - old[field, i]
            delta[field, i] = difference
            passed[field, i] = difference + outcome[field, i]


def natural_kernel(rows, early_rows, late_rows, matrix, natural):
    width = late_rows.shape[-1]
    order = matrix[...]
    for field in range(3):
        for part, first in ((early_rows, 0), (late_rows, rows - HALO)):
            count = part.shape[1]
            value = select(part[field].reshape(count * 8, width), order, 3).reshape(count, 8, width)
            for i in range(count):
                store_row(natural, field, rows, width, first + i, value[i])


def final_kernel(
    rows, scalars, incoming, before, after, previous, coarse_wet, coarse_before, mean_depth, tripled, natural, order,
    spread,
    new_ends, coarse_new,
    state, hv, press, result, semaphores,
):
    coarse_rows = rows // 2
    half = incoming.shape[-1]
    width = 2 * half
    fetch = Fetch(semaphores)
    for field in range(3):
        fetch(before.at[field], state.at[field, 0])
        fetch(after.at[field], state.at[field, coarse_rows + 1])
        fetch(incoming.at[field], state.at[field, pl.ds(1, coarse_rows)])
    coarse_depth = jnp.broadcast_to(mean_depth[...], (8, half))
    kron_parts = coupling_parts(tripled[...])
    last = scalars[6] > 0.5
    fetch.wait()

    def emit(i, values):
        for field in range(3):
            result[field, i] = jnp.where(last, values[field], previous[field, i])

    coarse_update(
        state, hv, press, coarse_wet, coarse_rows, coarse_depth, kron_parts, scalars[4], scalars[5], emit
    )
    to_natural, to_fine = order[...], spread[...]
    for field in range(3):
        value = result[field].reshape(coarse_rows * 8, half)
        change = value - coarse_before[field].reshape(coarse_rows * 8, half)
        fine = select(change, to_fine, 2).reshape(coarse_rows, 8, width)
        value = select(value, to_natural, 2).reshape(coarse_rows, 8, half)
        for i in range(coarse_rows):
            store_row(coarse_new, field, coarse_rows, half, i, value[i])
            for r in (2 * i, 2 * i + 1):
                for c, part in enumerate(tile_slices(rows, width, r)):
                    new_ends[field, part, :] = natural[field, part, :] + fine[i, :, c * LANES : (c + 1) * LANES]


def middle_turn(incoming, before, after, coarse_wet, mean_depth, coupling, first_coriolis, coriolis_step):
    state = jnp.concatenate([before[:, None], incoming, after[:, None]], axis=1)
    e, u, v = state
    rows, layers, half = incoming.shape[1:]
    blocks = half // LANES
    p = jnp.einsum("kl,rlc->rkc", coupling, e, precision=lax.Precision.HIGHEST)
    h = mean_depth[None, :, None] + e

    def dx_parts(q):
        q = q.reshape(q.shape[0], layers, blocks, LANES)
        east = jnp.concatenate([q[:, :, 1:], jnp.roll(q[:, :, :1], -1, -1)], axis=2)
        west = jnp.concatenate([jnp.roll(q[:, :, -1:], 1, -1), q[:, :, :-1]], axis=2)
        return east.reshape(-1, layers, half)[1:-1], west.reshape(-1, layers, half)[1:-1]

    def dx(q):
        east, west = dx_parts(q)
        return (east - west) / 4.0

    def dy(q):
        return (q[2:] - q[:-2]) / 4.0

    def lap(q):
        east, west = dx_parts(q)
        return (q[2:] + q[:-2] + east + west - 4.0 * q[1:-1]) / 4.0

    um, vm = u[1:-1], v[1:-1]
    f = (first_coriolis + coriolis_step * jnp.arange(rows, dtype=f32))[:, None, None] / 4.0
    de = -(dx(h * u) + dy(h * v))
    du = coarse_wet * (-(um * dx(u) + vm * dy(u)) + f * vm - dx(p) + viscosity * lap(u))
    dv = coarse_wet * (-(um * dx(v) + vm * dy(v)) - f * um - dy(p) + viscosity * lap(v))
    return incoming + STEPS * time_step * jnp.stack([de, du, dv])


def local(starts, coarse_old, mean_depth, coupling, wet_cells):
    layers, rows, width = starts.shape[2:]
    coarse_rows, half = rows // 2, width // 2
    assert layers == 8 and rows % 8 == 0 and HALO < rows <= 2 * HALO
    tm, tm_size = lax.axis_index("tm"), lax.axis_size("tm")
    lat, lat_size = lax.axis_index("lat"), lax.axis_size("lat")
    total_rows = rows * lat_size
    starts = tiles_of(starts[0])
    coarse_old = tiles_of(coarse_old[0])
    vmem = pl.BlockSpec(memory_space=pltpu.VMEM)
    smem = pl.BlockSpec(memory_space=pltpu.SMEM)
    anywhere = pl.BlockSpec(memory_space=pl.ANY)
    fine_order = interleave_matrix(width)
    coarse_order = interleave_matrix(half)
    planes = 3 * HALO + 2

    def array(*shape):
        return jax.ShapeDtypeStruct(shape, f32)

    def buffer(*shape):
        return pltpu.VMEM(shape, f32)

    def call(kernel, outs, in_specs, scratch=()):
        return pl.pallas_call(
            functools.partial(kernel, rows),
            out_shape=outs,
            in_specs=in_specs,
            out_specs=[vmem] * len(outs),
            scratch_shapes=list(scratch),
            name=kernel.__name__,
            compiler_params=pltpu.CompilerParams(vmem_limit_bytes=16 * 2**20),
        )

    to_next, to_previous = call(pack_kernel, [array(planes, 8, width)] * 2, [vmem] * 3)(
        starts, wet_cells, jnp.asarray(fine_order, bf16)
    )
    up = [(i, i + 1) for i in range(lat_size - 1)]
    down = [(j, i) for i, j in up]
    before = lax.ppermute(to_next, "lat", up)

    lat_f = lat.astype(f32)
    slope = 4.0 * rotation / total_rows
    coarse_slope = 16.0 * rotation / total_rows
    scalars = jnp.stack([
        slope * (lat_f * rows + 0.5) - 2.0 * rotation,
        jnp.asarray(slope, f32),
        (lat > 0).astype(f32),
        (lat < lat_size - 1).astype(f32),
        coarse_slope * (lat_f * coarse_rows + 0.5) - 4.0 * rotation,
        jnp.asarray(coarse_slope, f32),
        (tm == tm_size - 1).astype(f32),
    ])
    depth = mean_depth.reshape(layers, 1)
    same_row = np.kron(np.eye(CHUNK), np.ones((8, 8))).astype(np.float32)
    tripled = jnp.tile(jnp.tile(coupling, (CHUNK, CHUNK)) * same_row, (1, 3))

    def stage_scratch(count):
        return [buffer(3, count, 8, width)] * 3 + [buffer(count, 8, width)] * 3 + [
            pltpu.VMEM((CHUNK * 8, 3 * CHUNK * 8), bf16)
        ]

    north_strips, south_strips, coarse_before, first, coarse_wet = call(
        inner_kernel,
        [array(rows // 2, 3, 3, 8, width)] * 2
        + [array(3, coarse_rows, 8, half)] * 2
        + [array(coarse_rows, 8, half)],
        [smem] + [vmem] * 6,
        stage_scratch(rows),
    )(scalars, to_next, to_previous, coarse_old, depth, tripled, jnp.asarray(coarse_order, bf16))
    to_previous, south_strips = lax.optimization_barrier((to_previous, south_strips))
    after = lax.ppermute(to_previous, "lat", down)

    early_rows, late_strips = call(
        north_kernel,
        [array(3, rows - HALO, 8, width), array(HALO - rows // 2, 3, 3, 8, width)],
        [smem] + [anywhere] * 3 + [vmem] * 2,
        stage_scratch(HALO + rows)
        + [buffer(rows // 2, 3, 3, 8, width), buffer(2, 2, 8, width), pltpu.SemaphoreType.DMA((6,))],
    )(scalars, before, to_previous, north_strips, depth, tripled)

    late_rows, delta, outcome, passed = call(
        south_kernel,
        [array(3, HALO, 8, width)] + [array(3, coarse_rows, 8, half)] * 3,
        [smem] + [anywhere] * 5 + [vmem] + [anywhere] * 2 + [vmem] * 3,
        stage_scratch(2 * HALO + 1)
        + [buffer(rows // 2, 3, 3, 8, width), buffer(HALO - rows // 2, 3, 3, 8, width), buffer(2, 2, 8, width)]
        + [buffer(3, coarse_rows + 2, 8, half), buffer(3, 2, 8, width), buffer(3, coarse_rows, 8, half)]
        + [pltpu.SemaphoreType.DMA((14,))],
    )(
        scalars, after, to_next, before, south_strips, late_strips, early_rows, first, coarse_before, coarse_wet,
        depth, tripled,
    )

    both = ("tm", "lat")

    def hand_on(current):
        def moved(values, shift):
            pairs = [
                (t * lat_size + i, (t + 1) * lat_size + i + shift)
                for t in range(tm_size - 1)
                for i in range(lat_size)
                if 0 <= i + shift < lat_size
            ]
            return lax.ppermute(values, both, pairs)

        return moved(current, 0), moved(current[:, -1], 1), moved(current[:, 0], -1)

    previous = outcome
    incoming = hand_on(passed)
    (natural,) = call(natural_kernel, [array(*starts.shape)], [vmem] * 3)(
        early_rows, late_rows, jnp.asarray(fine_order.T, bf16)
    )
    for turn in range(1, tm_size - 1):
        outcome = middle_turn(*incoming, coarse_wet, mean_depth, coupling, scalars[4], scalars[5])
        previous = jnp.where(tm == turn, outcome, previous)
        incoming = hand_on(delta + outcome)

    new_ends, coarse_new = call(
        final_kernel,
        [array(*starts.shape), array(*coarse_old.shape)],
        [smem] + [anywhere] * 3 + [vmem] * 8,
        [buffer(3, coarse_rows + 2, 8, half)]
        + [buffer(coarse_rows + 2, 8, half)] * 2
        + [buffer(3, coarse_rows, 8, half), pltpu.SemaphoreType.DMA((9,))],
    )(
        scalars, *incoming, previous, coarse_wet, coarse_before, depth, tripled, natural,
        jnp.asarray(coarse_order.T, bf16), jnp.asarray(prolong_matrix(width), bf16),
    )
    return (
        from_tiles(new_ends, layers, rows, width)[None],
        from_tiles(coarse_new, layers, coarse_rows, half)[None],
    )


def solution(mesh):
    in_specs = (
        P("tm", None, None, "lat", None),
        P("tm", None, None, "lat", None),
        P(),
        P(),
        P("lat", None),
    )
    out_specs = (P("tm", None, None, "lat", None), P("tm", None, None, "lat", None))
    return jax.shard_map(local, mesh=mesh, in_specs=in_specs, out_specs=out_specs, check_vma=False)
```

time: 74.8 us -> 56.7 us (0.76)
  waiting for transfers between devices: 9.35 us -> 0.01 us
  Pallas kernels: 43.9 us -> 37.9 us
  local copies, waits for them, and re-layouts: 6.04 us -> 3.43 us
    ppermute x1, waiting for transfers between devices: 8.43 us -> 0.01 us  [local(): before = lax.ppermute(to_next, 'lat', up)]
    pallas_call x3 -> x6, Pallas kernels: 43.9 us -> 37.9 us  [the longest x1 14.4 us: local(): call(south_kernel, [array(3, HALO, 8, width)] + [array(3, coarse_rows, 8,...]
    mul x2 -> x1, local copies, waits for them, and re-layouts: 1.57 us -> 0.12 us  [local(): tripled = jnp.tile(jnp.tile(coupling, (CHUNK, CHUNK)) * same_row, (1, 3))]
    ppermute x3, waiting for transfers between devices: 0.91 us -> 0.01 us  [moved(): return lax.ppermute(values, both, pairs)]
    squeeze x1, local copies, waits for them, and re-layouts: 0.78 us -> 0.01 us  [hand_on(): current[:, 0]]
    unnamed x14 -> x23, local copies, waits for them, and re-layouts: 2.37 us -> 3.04 us
  transfers between devices with their start and end apart: 5 -> 5, of which waited for: 2 -> 0; matrix products, arithmetic and copies ran while one was open for 5% -> 1% of each run, Pallas kernels for 0% -> 34%
where the time goes in v1:
time: 56.7 us; the launch traced here: 55.9 us
  Pallas kernels  37.9 us (67%)
  starting transfers between devices  13.7 us (24%)
  local copies, waits for them, and re-layouts  3.43 us (6%)
  between operations  0.89 us (2%)
    pallas_call x1, Pallas kernels, local(): call(south_kernel, [array(3, HALO, 8, width)] + [array(3, coarse_rows, 8,...  14.4 us
    pallas_call x1, Pallas kernels, local(): call(north_kernel, [array(3, rows - HALO, 8, width), array(HALO - rows //...  11.5 us
    ppermute x3, starting transfers between devices, moved(): return lax.ppermute(values, both, pairs)  7.28 us
    pallas_call x1, Pallas kernels, local(): call(inner_kernel, [array(rows // 2, 3, 3, 8, width)] * 2 + [array(3, coa...  5.7 us
    ppermute x1, starting transfers between devices, local(): before = lax.ppermute(to_next, 'lat', up)  4.51 us
    pallas_call x1, Pallas kernels, local(): call(final_kernel, [array(*starts.shape), array(*coarse_old.shape)], [sme...  3.34 us
    unnamed x23, local copies, waits for them, and re-layouts  3.04 us
    pallas_call x1, Pallas kernels, local(): call(natural_kernel, [array(*starts.shape)], [vmem] * 3)  2.01 us
  transfers between devices with their start and end apart: 5, of which 0 were waited for; matrix products, arithmetic and copies ran while one was open for 1% of the time, Pallas kernels for 34%

profile of v1, /device:TPU:1, one launch (start us, length us, event | category | flops | bytes accessed | tf_op | source)
XLA Modules:
  0.0 55.9 jit_solution(14746883342949468307)
XLA Ops:
  0.6 0.0 copy-start.10
  0.6 0.0 copy-start
  0.7 1.1 %copy-done = f32[1,3,8,16,512]{4,3,2,1,0:T(8,128)S(1)} copy-done((f32[1,3,8,16,512]{4,3,2,1,0:T(8,128)S(1)}, f32[1,3,8,16,512]{4,3,2,1,0:T(8,128)}, u32[]{:S(2)}) %copy-start) | copy-done | bytes 786456
  1.8 0.0 copy-start.2
  1.8 1.0 %copy-done.2 = bf16[512,512]{1,0:T(8,128)(2,1)S(1)} copy-done((bf16[512,512]{1,0:T(8,128)(2,1)S(1)}, bf16[512,512]{1,0:T(8,128)(2,1)}, u32[]{:S(2)}) %copy-start.2) | copy-done | bytes 524312
  2.8 0.0 copy-start.7
  2.8 0.8 %copy-done.7 = s32[16,512]{1,0:T(8,128)S(1)} copy-done((s32[16,512]{1,0:T(8,128)S(1)}, s32[16,512]{1,0:T(8,128)}, u32[]{:S(2)}) %copy-start.7) | copy-done | bytes 32792
  3.6 0.0 copy-start.9
  3.6 0.0 copy-start.8
  3.6 0.0 copy-start.4
  3.6 0.0 copy-start.6
  3.6 1.0 %pack_kernel.1 = (f32[38,8,512]{2,1,0:T(8,128)S(1)}, f32[38,8,512]{2,1,0:T(8,128)S(1)}) custom-call(f32[3,512,128]{2,1,0:T(8,128)S(1)} %bitcast.35, s32[16,512]{1,0:T(8,128)S(1)} %copy-done.7, bf16[512,512]{1,0:T(8,128)(2,1)S(1)} %copy-done.2), custom_call_target="tpu_custom_call" | custom-call | tf_op jit(solution)/shard_map/pack_kernel/pallas_call | solution.py:523
  4.5 4.5 %collective-permute-start.1 = (f32[38,8,512]{2,1,0:T(8,128)S(1)}, f32[38,8,512]{2,1,0:T(8,128)S(1)}, u32[]{:S(2)}, u32[]{:S(2)}) collective-permute-start(f32[38,8,512]{2,1,0:T(8,128)S(1)} %get-tuple-element.19.to_next), channel_id=1, source_target_pairs={{0,1},{1,2},{2,3},{3,4},{4,5},{5,6},{6,7},{7,8},{8,9},{9,10},{10,1... | collective-permute-start | bytes 1867784 | tf_op jit(solution)/shard_map/ppermute | solution.py:528
  9.1 0.0 copy-done.10
  9.1 0.1 copy.20.mean_depth
  9.2 0.0 copy-done.9
  9.2 0.1 copy.19
  9.2 0.0 copy-done.8
  9.3 0.1 reshape.33
  9.4 0.1 copy.21.tripled
  9.5 0.1 stack.35.scalars
  9.6 0.0 copy-done.4
  9.6 0.0 copy-done.6
  9.6 5.7 %inner_kernel.1 = (f32[8,3,3,8,512]{4,3,2,1,0:T(8,128)S(1)}, f32[8,3,3,8,512]{4,3,2,1,0:T(8,128)S(1)}, f32[3,8,8,256]{3,2,1,0:T(8,128)S(1)}, f32[3,8,8,256]{3,2,1,0:T(8,128)S(1)}, f32[8,8,256]{2,1,0:T(8,128)S(1)}) custom-call(f32[7]{0:T(128)S(1)} %stack.35.scalars, f32[38,8,512]{2,1,0:T(8,128)S(1)} %get-tuple-element.19.to_next, ...), custom_call_target="tpu_custom_call" | custom-call | tf_op jit(solution)/shard_map/inner_kernel/pallas_call | solution.py:551
  15.3 1.9 %collective-permute-start = (f32[38,8,512]{2,1,0:T(8,128)S(1)}, f32[38,8,512]{2,1,0:T(8,128)S(1)}, u32[]{:S(2)}, u32[]{:S(2)}) collective-permute-start(f32[38,8,512]{2,1,0:T(8,128)S(1)} %get-tuple-element.21.to_previous), channel_id=1, source_target_pairs={{1,0},{2,1},{3,2},{4,3},{5,4},{6,5},{7,6},{8,7},{9,8},{10,9},{11,1... | collective-permute-start | bytes 1867784 | tf_op jit(solution)/shard_map/ppermute | solution.py:560
  17.3 0.0 collective-permute-done.1.before
  17.3 11.5 %north_kernel.1 = (f32[3,4,8,512]{3,2,1,0:T(8,128)S(1)}, f32[4,3,3,8,512]{4,3,2,1,0:T(8,128)S(1)}) custom-call(f32[7]{0:T(128)S(1)} %stack.35.scalars, f32[38,8,512]{2,1,0:T(8,128)S(1)} %collective-permute-done.1.before, f32[38,8,512]{2,1,0:T(8,128)S(1)} %get-tuple-element.21.to_previous, f32[8,3,3,8,512]{4,3,2,1,0:T(8,128)S(1)} %get-tuple-element.23.strips, ...), custom_call_target="tpu_custom_call" | custom-call | tf_op jit(solution)/shard_map/north_kernel/pallas_call | solution.py:562
  28.8 0.0 collective-permute-done.after
  28.8 0.0 copy-start.1
  28.8 14.4 %south_kernel.1 = (f32[3,12,8,512]{3,2,1,0:T(8,128)S(1)}, f32[3,8,8,256]{3,2,1,0:T(8,128)}, f32[3,8,8,256]{3,2,1,0:T(8,128)S(1)}, f32[3,8,8,256]{3,2,1,0:T(8,128)S(1)}) custom-call(f32[7]{0:T(128)S(1)} %stack.35.scalars, f32[38,8,512]{2,1,0:T(8,128)S(1)} %collective-permute-done.after, f32[38,8,512]{2,1,0:T(8,128)S(1)} %get-tuple-element.19.to_next, ...), custom_call_target="tpu_custom_call" | custom-call | tf_op jit(solution)/shard_map/south_kernel/pallas_call | solution.py:570
  43.2 0.0 copy-start.3
  43.2 0.0 copy-start.5
  43.2 3.3 %collective-permute-start.2 = (f32[3,8,8,256]{3,2,1,0:T(8,128)S(1)}, f32[3,8,8,256]{3,2,1,0:T(8,128)S(1)}, u32[]{:S(2)}, u32[]{:S(2)}) collective-permute-start(f32[3,8,8,256]{3,2,1,0:T(8,128)S(1)} %get-tuple-element.29), channel_id=1, source_target_pairs={{0,16},{1,17},{2,18},{3,19},{4,20},{5,21},{6,22},{7,23},{8,24},{9,... | collective-permute-start | bytes 589832 | tf_op jit(solution)/shard_map/ppermute | solution.py:593
  46.5 1.3 %collective-permute-start.4 = (f32[3,8,256]{2,1,0:T(8,128)S(1)}, f32[3,8,256]{2,1,0:T(8,128)S(1)}, u32[]{:S(2)}, u32[]{:S(2)}) collective-permute-start(f32[3,8,256]{2,1,0:T(8,128)S(1)} %get-tuple-element.34), channel_id=1, source_target_pairs={{1,16},{2,17},{3,18},{4,19},{5,20},{6,21},{7,22},{8,23},{9,24},{10... | collective-permute-start | bytes 73736 | tf_op jit(solution)/shard_map/ppermute | solution.py:593
  47.8 2.7 %collective-permute-start.3 = (f32[3,8,256]{2,1,0:T(8,128)S(1)}, f32[3,8,256]{2,1,0:T(8,128)S(1)}, u32[]{:S(2)}, u32[]{:S(2)}) collective-permute-start(f32[3,8,256]{2,1,0:T(8,128)S(1)} %get-tuple-element.35), channel_id=1, source_target_pairs={{0,17},{1,18},{2,19},{3,20},{4,21},{5,22},{6,23},{7,24},{8,25},{9,... | collective-permute-start | bytes 73736 | tf_op jit(solution)/shard_map/ppermute | solution.py:593
  50.5 0.0 copy-done.1
  50.5 2.0 %natural_kernel.1.natural = f32[3,512,128]{2,1,0:T(8,128)S(1)} custom-call(f32[3,4,8,512]{3,2,1,0:T(8,128)S(1)} %get-tuple-element.25.first_rows.early_rows, f32[3,12,8,512]{3,2,1,0:T(8,128)S(1)} %get-tuple-element.31.late_rows, bf16[512,512]{1,0:T(8,128)(2,1)S(1)} %copy-done.1), custom_call_target="tpu_custom_call" | custom-call | tf_op jit(solution)/shard_map/natural_kernel/pallas_call | solution.py:599
  52.6 0.0 collective-permute-done.4.after
  52.6 0.0 collective-permute-done.3.before
  52.6 0.0 collective-permute-done.2.incoming
  52.6 0.0 copy-done.3
  52.6 0.0 copy-done.5
  52.6 3.3 %final_kernel.1 = (f32[3,512,128]{2,1,0:T(8,128)}, f32[3,128,128]{2,1,0:T(8,128)}) custom-call(f32[7]{0:T(128)S(1)} %stack.35.scalars, f32[3,8,8,256]{3,2,1,0:T(8,128)S(1)} %collective-permute-done.2.incoming, f32[3,8,256]{2,1,0:T(8,128)S(1)} %collective-permute-done.3.before, f32[3,8,256]{2,1,0:T(8,128)S(1)} %collective-permute-done.4.after, ...), custom_call_target="tpu_custom_call" | custom-call | tf_op jit(solution)/shard_map/final_kernel/pallas_call | solution.py:607
  (3 shorter events, 0.0 us)
Async XLA Ops:
  0.6 8.5 %copy-start.10 = (f32[8]{0:T(128)S(1)}, f32[8]{0:T(128)}, u32[]{:S(2)}) copy-start(f32[8]{0:T(128)} %param.13) | copy-start | bytes 100
  0.6 1.1 %copy-start = (f32[1,3,8,16,512]{4,3,2,1,0:T(8,128)S(1)}, f32[1,3,8,16,512]{4,3,2,1,0:T(8,128)}, u32[]{:S(2)}) copy-start(f32[1,3,8,16,512]{4,3,2,1,0:T(8,128)} %param.11) | copy-start | bytes 2359300
  1.8 1.0 %copy-start.2 = (bf16[512,512]{1,0:T(8,128)(2,1)S(1)}, bf16[512,512]{1,0:T(8,128)(2,1)}, u32[]{:S(2)}) copy-start(bf16[512,512]{1,0:T(8,128)(2,1)} %constant.47.clone.matrix) | copy-start | bytes 1572868
  2.8 0.8 %copy-start.7 = (s32[16,512]{1,0:T(8,128)S(1)}, s32[16,512]{1,0:T(8,128)}, u32[]{:S(2)}) copy-start(s32[16,512]{1,0:T(8,128)} %wet_cells.1) | copy-start | bytes 98308
  3.6 5.6 %copy-start.9 = (f32[8,8]{1,0:T(8,128)S(1)}, f32[8,8]{1,0:T(8,128)}, u32[]{:S(2)}) copy-start(f32[8,8]{1,0:T(8,128)} %param.14) | copy-start | bytes 772
  3.6 5.7 %copy-start.8 = (f32[8,8,8,8]{1,0,3,2:T(8,128)S(1)}, f32[8,8,8,8]{1,0,3,2:T(8,128)}, u32[]{:S(2)}) copy-start(f32[8,8,8,8]{1,0,3,2:T(8,128)} %constant.55) | copy-start | bytes 49156
  3.6 6.0 %copy-start.4 = (f32[1,3,8,8,256]{4,3,2,1,0:T(8,128)S(1)}, f32[1,3,8,8,256]{4,3,2,1,0:T(8,128)}, u32[]{:S(2)}) copy-start(f32[1,3,8,8,256]{4,3,2,1,0:T(8,128)} %param.12) | copy-start | bytes 589828
  3.6 6.0 %copy-start.6 = (bf16[256,256]{1,0:T(8,128)(2,1)S(1)}, bf16[256,256]{1,0:T(8,128)(2,1)}, u32[]{:S(2)}) copy-start(bf16[256,256]{1,0:T(8,128)(2,1)} %constant.49.clone.matrix) | copy-start | bytes 393220
  4.5 12.7 %collective-permute-start.1 = (f32[38,8,512]{2,1,0:T(8,128)S(1)}, f32[38,8,512]{2,1,0:T(8,128)S(1)}, u32[]{:S(2)}, u32[]{:S(2)}) collective-permute-start(f32[38,8,512]{2,1,0:T(8,128)S(1)} %get-tuple-element.19.to_next), channel_id=1, source_target_pairs={{0,1},{1,2},{2,3},{3,4},{4,5},{5,6},{6,7},{7,8},{8,9},{9,10},{10,1... | collective-permute-start | bytes 1867784 | tf_op jit(solution)/shard_map/ppermute | solution.py:528
  15.3 13.4 %collective-permute-start = (f32[38,8,512]{2,1,0:T(8,128)S(1)}, f32[38,8,512]{2,1,0:T(8,128)S(1)}, u32[]{:S(2)}, u32[]{:S(2)}) collective-permute-start(f32[38,8,512]{2,1,0:T(8,128)S(1)} %get-tuple-element.21.to_previous), channel_id=1, source_target_pairs={{1,0},{2,1},{3,2},{4,3},{5,4},{6,5},{7,6},{8,7},{9,8},{10,9},{11,1... | collective-permute-start | bytes 1867784 | tf_op jit(solution)/shard_map/ppermute | solution.py:560
  28.8 21.8 %copy-start.1 = (bf16[512,512]{1,0:T(8,128)(2,1)S(1)}, bf16[512,512]{1,0:T(8,128)(2,1)}, u32[]{:S(2)}) copy-start(bf16[512,512]{1,0:T(8,128)(2,1)} %constant.50.clone.matrix) | copy-start | bytes 1572868
  43.2 9.4 %copy-start.3 = (bf16[256,512]{1,0:T(8,128)(2,1)S(1)}, bf16[256,512]{1,0:T(8,128)(2,1)}, u32[]{:S(2)}) copy-start(bf16[256,512]{1,0:T(8,128)(2,1)} %constant.52.clone.spread) | copy-start | bytes 786436
  43.2 9.4 %copy-start.5 = (bf16[256,256]{1,0:T(8,128)(2,1)S(1)}, bf16[256,256]{1,0:T(8,128)(2,1)}, u32[]{:S(2)}) copy-start(bf16[256,256]{1,0:T(8,128)(2,1)} %constant.51.clone.order) | copy-start | bytes 393220
  43.2 9.4 %collective-permute-start.2 = (f32[3,8,8,256]{3,2,1,0:T(8,128)S(1)}, f32[3,8,8,256]{3,2,1,0:T(8,128)S(1)}, u32[]{:S(2)}, u32[]{:S(2)}) collective-permute-start(f32[3,8,8,256]{3,2,1,0:T(8,128)S(1)} %get-tuple-element.29), channel_id=1, source_target_pairs={{0,16},{1,17},{2,18},{3,19},{4,20},{5,21},{6,22},{7,23},{8,24},{9,... | collective-permute-start | bytes 589832 | tf_op jit(solution)/shard_map/ppermute | solution.py:593
  46.5 6.1 %collective-permute-start.4 = (f32[3,8,256]{2,1,0:T(8,128)S(1)}, f32[3,8,256]{2,1,0:T(8,128)S(1)}, u32[]{:S(2)}, u32[]{:S(2)}) collective-permute-start(f32[3,8,256]{2,1,0:T(8,128)S(1)} %get-tuple-element.34), channel_id=1, source_target_pairs={{1,16},{2,17},{3,18},{4,19},{5,20},{6,21},{7,22},{8,23},{9,24},{10... | collective-permute-start | bytes 73736 | tf_op jit(solution)/shard_map/ppermute | solution.py:593
  47.8 4.8 %collective-permute-start.3 = (f32[3,8,256]{2,1,0:T(8,128)S(1)}, f32[3,8,256]{2,1,0:T(8,128)S(1)}, u32[]{:S(2)}, u32[]{:S(2)}) collective-permute-start(f32[3,8,256]{2,1,0:T(8,128)S(1)} %get-tuple-element.35), channel_id=1, source_target_pairs={{0,17},{1,18},{2,19},{3,20},{4,21},{5,22},{6,23},{7,24},{8,25},{9,... | collective-permute-start | bytes 73736 | tf_op jit(solution)/shard_map/ppermute | solution.py:593

commit v2 on v1

v2 whole, which is shorter than its diff:
```python
import functools

import jax
import jax.numpy as jnp
import numpy as np
from jax import lax
from jax.experimental import pallas as pl
from jax.experimental.pallas import tpu as pltpu
from jax.sharding import PartitionSpec as P


STEPS = 4
HALO = 3 * STEPS
GROUP = 6
CHUNK = GROUP + 2
LANES = 128

time_step = 0.15
viscosity = 0.02
rotation = 0.3

STAGE_WEIGHTS = (1.0, 0.25, 2.0 / 3.0)
STAGE_MIX = (None, (0.75, 0.25), (1.0 / 3.0, 2.0 / 3.0))
f32, bf16 = jnp.float32, jnp.bfloat16


def interleave_matrix(width):
    blocks = width // LANES
    place = np.arange(width)
    columns = blocks * (place % LANES) + place // LANES
    return (np.arange(width)[:, None] == columns[None, :]).astype(np.float32)


def prolong_matrix(width):
    half = width // 2
    blocks = half // LANES
    place = np.arange(half)
    columns = blocks * (place % LANES) + place // LANES
    return (columns[:, None] == np.arange(width)[None, :] // 2).astype(np.float32)


def tiles_of(x):
    fields, layers, rows, width = x.shape
    x = x.reshape(fields, layers, rows // 8, 8, width // LANES, LANES).transpose(0, 1, 2, 4, 3, 5)
    return x.reshape(fields, layers * rows * width // LANES, LANES)


def from_tiles(x, layers, rows, width):
    fields = x.shape[0]
    x = x.reshape(fields, layers, rows // 8, width // LANES, 8, LANES).transpose(0, 1, 2, 4, 3, 5)
    return x.reshape(fields, layers, rows, width)


def tile_slices(rows, width, r):
    blocks = width // LANES
    if not isinstance(r, int):
        start = lax.div(r, 8) * (8 * blocks) + lax.rem(r, 8)
    else:
        start = (r // 8) * (8 * blocks) + r % 8
    return [pl.ds(start + 8 * c, 8, stride=rows * blocks) for c in range(blocks)]


def load_row(tiles, field, rows, width, r):
    return jnp.concatenate([tiles[field, part, :] for part in tile_slices(rows, width, r)], axis=1)


def store_row(tiles, field, rows, width, r, value):
    for c, part in enumerate(tile_slices(rows, width, r)):
        tiles[field, part, :] = value[:, c * LANES : (c + 1) * LANES]


def blocks_of(x):
    return [x[:, c : c + LANES] for c in range(0, x.shape[1], LANES)]


def east_west(x):
    blocks = blocks_of(x)
    east = jnp.concatenate(blocks[1:] + [pltpu.roll(blocks[0], LANES - 1, 1)], axis=1)
    west = jnp.concatenate([pltpu.roll(blocks[-1], 1, 1)] + blocks[:-1], axis=1)
    return east, west


def restrict_pair(north, south):
    blocks = blocks_of(north + south)
    return 0.25 * jnp.concatenate([a + b for a, b in zip(blocks[0::2], blocks[1::2])], axis=1)


def split(x, parts):
    found = []
    for _ in range(parts - 1):
        found.append(x.astype(bf16))
        x = x - found[-1].astype(f32)
    return found + [x.astype(bf16)]


def dot(a, b):
    return lax.dot_general(a, b, (((1,), (0,)), ((), ())), preferred_element_type=f32)


def select(x, matrix, parts):
    return sum(dot(part, matrix) for part in split(x, parts))


def coupling_parts(coupling, count):
    size = 8 * count
    high, low = split(jnp.concatenate([coupling] * count, axis=0), 2)
    layer = lax.broadcasted_iota(jnp.int32, (8, 3 * size), 0)
    column = lax.broadcasted_iota(jnp.int32, (8, 3 * size), 1)
    spread = jnp.where((column & 7) == layer, 1.0, 0.0).astype(bf16)
    row = lax.broadcasted_iota(jnp.int32, (size, 3 * size), 0)
    column = lax.broadcasted_iota(jnp.int32, (size, 3 * size), 1)
    third = jnp.where(column >= 2 * size, 2, jnp.where(column >= size, 1, 0))
    parts = jnp.where(third == 2, dot(low, spread), dot(high, spread))
    return jnp.where(((column - size * third) >> 3) == (row >> 3), parts, 0.0).astype(bf16)


def depth_of(mean_depth, width):
    row = lax.broadcasted_iota(jnp.int32, (8, 8), 0)
    column = lax.broadcasted_iota(jnp.int32, (8, 8), 1)
    diagonal = jnp.where(row == column, jnp.broadcast_to(mean_depth[...], (8, 8)), 0.0)
    return select(diagonal, jnp.ones((8, width), bf16), 3)


class Place:
    def __init__(self, rows):
        lat, lat_size = lax.axis_index("lat"), lax.axis_size("lat")
        tm, tm_size = lax.axis_index("tm"), lax.axis_size("tm")
        total = rows * lat_size
        self.even = lax.rem(lat, 2) == 0
        self.last = tm == tm_size - 1
        self.sign = jnp.where(self.even, -1.0, 1.0).astype(f32)
        low, high = (lat > 0).astype(f32), (lat < lat_size - 1).astype(f32)
        self.near_inside = jnp.where(self.even, high, low)
        self.far_inside = jnp.where(self.even, low, high)
        lat_f = lat.astype(f32)
        self.step = 4.0 * rotation / total
        self.coarse_step = 16.0 * rotation / total
        first = self.step * (lat_f * rows + 0.5) - 2.0 * rotation
        coarse = self.coarse_step * (lat_f * (rows // 2) + 0.5) - 4.0 * rotation
        self.first = jnp.where(self.even, -(first + self.step * (rows - 1)), first)
        self.coarse_first = jnp.where(self.even, -(coarse + self.coarse_step * (rows // 2 - 1)), coarse)

    def own_row(self, rows, i):
        return jnp.where(self.even, rows - 1 - i, i)


def pressure_rows(source, hv, press, start, count, kron_parts):
    h = source[0, pl.ds(start, count)]
    hv[pl.ds(start, count)] = h * source[2, pl.ds(start, count)]
    layers, width = h.shape[1:]
    high, low = split(h.reshape(count * layers, width), 2)
    p = dot(kron_parts[count][...], jnp.concatenate([high, low, high], axis=0))
    press[pl.ds(start, count)] = p.reshape(count, layers, width)


def row_tendency(source, hv, press, r, twice_viscosity, coriolis):
    h, u, v = source[0, r], source[1, r], source[2, r]
    u_north, u_south = source[1, r + 1], source[1, r - 1]
    v_north, v_south = source[2, r + 1], source[2, r - 1]
    hu_east, hu_west = east_west(h * u)
    divergence = (hu_east - hu_west) + (hv[r + 1] - hv[r - 1])
    u_east, u_west = east_west(u)
    v_east, v_west = east_west(v)
    p_east, p_west = east_west(press[r])
    to_east, to_west = twice_viscosity - u, twice_viscosity + u
    to_north, to_south = twice_viscosity - v, twice_viscosity + v
    zonal = (to_east * u_east + to_west * u_west) + (to_north * u_north + to_south * u_south)
    zonal = (zonal - (p_east - p_west)) + coriolis * v
    merid = (to_east * v_east + to_west * v_west) + (to_north * v_north + to_south * v_south)
    merid = (merid - (press[r + 1] - press[r - 1])) - coriolis * u
    return (h, u, v), (divergence, zonal, merid)


def run_stage(
    source, target, base, hv, press, wet, low, high, count, which, kron_parts, coriolis_of, inside_of
):
    factor = STAGE_WEIGHTS[which] * time_step / 2.0
    mix = STAGE_MIX[which]

    def one(r):
        here, rates = row_tendency(source, hv, press, r, 2.0 * viscosity, coriolis_of(r))
        mask, keep = wet[which, r], wet[3 + which, r]
        values = [here[0] if mix is None else mix[1] * here[0], keep * here[1], keep * here[2]]
        scales = (-factor * inside_of(r), mask, mask)
        for field in range(3):
            value = values[field]
            if mix is not None:
                value = value + mix[0] * base[field, r]
            target[field, r] = value + scales[field] * rates[field]

    def group(first):
        for i in range(GROUP):
            one(first + i)

    def fill(start, count):
        pressure_rows(source, hv, press, start, count, kron_parts)

    if isinstance(count, int):
        fill(low - 1, GROUP + 2)
        for first in range(0, count, GROUP):
            if first + GROUP < count:
                fill(low + first + GROUP + 1, GROUP)
            group(low + first)
        return

    def turn(k, unused):
        first = low + GROUP * k
        group(first)
        fill(jnp.minimum(first + GROUP + 1, high + 1 - GROUP), GROUP)
        return unused

    def two(k, unused):
        first = high - 2 * (rest - k)
        one(first)
        one(first + 1)
        return unused

    turns = lax.div(count, GROUP)
    rest = lax.div(count - GROUP * turns, 2)
    fill(jnp.minimum(low - 1, high - 1 - GROUP), GROUP + 2)
    lax.fori_loop(0, turns, turn, 0)
    lax.fori_loop(0, rest, two, 0)


def coarse_update(state, hv, press, wet, rows, kron_parts, first_coriolis, coriolis_step, emit):
    scale = STEPS * time_step / 4.0
    start = 0
    while start < rows + 2:
        pressure_rows(state, hv, press, min(start, rows + 2 - CHUNK), CHUNK, kron_parts)
        start += CHUNK
    for i in range(rows):
        coriolis = first_coriolis + coriolis_step * i
        (h, u, v), (dh, du, dv) = row_tendency(state, hv, press, i + 1, viscosity, coriolis)
        mask = wet[i] * scale
        keep = 1.0 - 4.0 * viscosity * mask
        emit(i, (h - scale * dh, keep * u + mask * du, keep * v + mask * dv))


def wet_row(halo, i):
    plane, row = (0, i) if i < 8 else (1, i - HALO + 8)
    return halo[3 * HALO + plane, pl.ds(row, 1), :]


def set_masks(wet, i, mask):
    for which, weight in enumerate(STAGE_WEIGHTS):
        scaled = mask * (weight * time_step / 2.0)
        wet[which, i] = scaled
        wet[3 + which, i] = weight - 8.0 * viscosity * scaled


def turned(x, field):
    return -x if field == 2 else x


def pack_kernel(rows, starts_hbm, wet_hbm, to_near, to_far, starts, wet_cells, wet, semaphores):
    width = wet_cells.shape[-1]
    blocks = width // LANES
    copies = [
        pltpu.make_async_copy(source, target, semaphores.at[n])
        for n, (source, target) in enumerate(
            [(starts_hbm.at[field], starts.at[field]) for field in range(3)] + [(wet_hbm, wet_cells)]
        )
    ]
    for copy in copies:
        copy.start()
    place = Place(rows)
    column = lax.broadcasted_iota(jnp.int32, (width, LANES), 0)
    column = column - blocks * lax.broadcasted_iota(jnp.int32, (width, LANES), 1)
    order = jnp.concatenate([jnp.where(column == c, 1.0, 0.0).astype(bf16) for c in range(blocks)], axis=1)
    for field in range(3):
        copies[field].wait()
        state = [load_row(starts, field, rows, width, place.own_row(rows, i)) for i in range(rows)]
        state = jnp.concatenate(state, axis=0)
        state = select(state * place.sign if field == 2 else state, order, 2).reshape(rows, 8, width)
        to_near[field * HALO : (field + 1) * HALO] = state[:HALO]
        to_far[field * HALO : (field + 1) * HALO] = state[rows - HALO :]
    copies[3].wait()
    wet[...] = dot(wet_cells[...].astype(f32).astype(bf16), order)
    for plane, skip in ((0, 0), (1, HALO - 8)):
        for i in range(8):
            for packed, first in ((to_near, 0), (to_far, rows - HALO)):
                row = place.own_row(rows, first + skip + i)
                packed[3 * HALO + plane, pl.ds(i, 1), :] = wet[pl.ds(row, 1), :]


def near_kernel(
    rows, near, to_near, to_far, coarse_old, mean_depth, coupling, matrix,
    early_rows, strips, coarse_before, first, coarse_wet,
    y, a, b, hv, press, wet, short_parts, long_parts,
):
    width = y.shape[-1]
    coarse_rows = rows // 2
    place = Place(rows)
    depth = depth_of(mean_depth, width)
    kron_parts = {}
    for count, parts in ((GROUP, short_parts), (CHUNK, long_parts)):
        parts[...] = coupling_parts(coupling[...], count)
        kron_parts[count] = parts
    for i in range(HALO):
        for field in range(3):
            value = turned(near[field * HALO + i], field)
            y[field, HALO - 1 - i] = value + depth if field == 0 else value
        set_masks(wet, HALO - 1 - i, jnp.broadcast_to(wet_row(near, i), (8, width)))
    for i in range(rows):
        sent, at = (to_near, i) if i < HALO else (to_far, i - rows + HALO)
        for field in range(3):
            value = sent[field * HALO + at]
            y[field, HALO + i] = value + depth if field == 0 else value
        set_masks(wet, HALO + i, jnp.broadcast_to(wet_row(sent, at), (8, width)))

    def coriolis_of(r):
        return place.first + place.step * (r - HALO).astype(f32)

    def inside_of(r):
        return jnp.where(r < HALO, place.near_inside, 1.0)

    def keep(state, t):
        for field in range(3):
            strips[t, field] = state[field, pl.ds(HALO + rows - 3 - t, 3)]

    keep(y, 0)
    for i in range(coarse_rows):
        both = wet[0, HALO + 2 * i] * wet[0, HALO + 2 * i + 1]
        blocks = blocks_of(jnp.where(both > 0.0, 1.0, 0.0))
        coarse_wet[i] = jnp.concatenate([p * q for p, q in zip(blocks[0::2], blocks[1::2])], axis=1)
        for field in range(3):
            first[field, i] = restrict_pair(y[field, HALO + 2 * i], y[field, HALO + 2 * i + 1])
    order = matrix[...]
    for field in range(3):
        old = [
            load_row(coarse_old, field, coarse_rows, width // 2, place.own_row(coarse_rows, i))
            for i in range(coarse_rows)
        ]
        old = select(jnp.concatenate(old, axis=0), order, 2).reshape(coarse_rows, 8, width // 2)
        if field == 0:
            old = old + depth[:, : width // 2]
        coarse_before[field] = old * place.sign if field == 2 else old

    def step(k, unused):
        for which, (source, target) in enumerate(((y, a), (a, b), (b, y))):
            s = 3 * k + which + 1
            run_stage(
                source, target, y, hv, press, wet, s, HALO + rows - s, HALO + rows - 2 * s, which, kron_parts, coriolis_of, inside_of
            )

            @pl.when(s < HALO)
            def _():
                keep(target, s)

        return unused

    lax.fori_loop(0, STEPS, step, 0)
    for field in range(3):
        early_rows[field] = y[field, HALO : HALO + rows - HALO]


def far_kernel(
    rows, far, to_far, near, strips, early_rows, first, coarse_before, coarse_wet,
    mean_depth, coupling,
    late_rows, delta, outcome, passed,
    y, a, b, hv, press, wet, short_parts, long_parts, state,
):
    width = y.shape[-1]
    origin = rows - HALO - 1
    own = rows - origin
    coarse_rows = rows // 2
    place = Place(rows)
    depth = depth_of(mean_depth, width)
    kron_parts = {}
    for count, parts in ((GROUP, short_parts), (CHUNK, long_parts)):
        parts[...] = coupling_parts(coupling[...], count)
        kron_parts[count] = parts
    for field in range(3):
        for i in range(HALO):
            value = turned(far[(field + 1) * HALO - 1 - i], field)
            y[field, own + i] = value + depth if field == 0 else value
        state[field, 1 : coarse_rows + 1] = first[field]
    for i in range(HALO):
        set_masks(wet, own + i, jnp.broadcast_to(wet_row(far, HALO - 1 - i), (8, width)))
        set_masks(wet, own - HALO + i, jnp.broadcast_to(wet_row(to_far, i), (8, width)))

    for field in range(3):
        edge = turned(restrict_pair(near[field * HALO], near[field * HALO + 1]), field)
        state[field, 0] = edge + depth[:, : width // 2] if field == 0 else edge
        state[field, coarse_rows + 1] = restrict_pair(y[field, own], y[field, own + 1])

    def emit(i, values):
        for field in range(3):
            outcome[field, i] = values[field]

    coarse_update(
        state, hv.at[:, :, pl.ds(0, width // 2)], press.at[:, :, pl.ds(0, width // 2)], coarse_wet, coarse_rows,
        kron_parts, place.coarse_first, place.coarse_step, emit,
    )

    def coriolis_of(r):
        return place.first + place.step * (r + origin).astype(f32)

    def inside_of(r):
        return jnp.where(r < own, 1.0, place.far_inside)

    def step(k, unused):
        for which, (source, target) in enumerate(((y, a), (a, b), (b, y))):
            t = 3 * k + which
            s = t + 1
            for field in range(3):
                for i in range(0 if which == 0 else 1, 3):
                    source[field, own - 3 - t + i] = strips[t, field, i]
            low = own - s
            run_stage(
                source, target, y, hv, press, wet, low, low + HALO, HALO, which, kron_parts, coriolis_of, inside_of
            )
        return unused

    lax.fori_loop(0, STEPS, step, 0)
    early = rows - HALO
    for field in range(3):
        late_rows[field] = y[field, own - HALO : own]
        for i in range(coarse_rows):
            if 2 * i < early:
                pair = early_rows[field, 2 * i], early_rows[field, 2 * i + 1]
            else:
                pair = y[field, 2 * i - origin], y[field, 2 * i + 1 - origin]
            difference = restrict_pair(*pair) - coarse_before[field, i]
            delta[field, i] = difference
            passed[field, i] = difference + outcome[field, i]


def natural_kernel(rows, early_rows, late_rows, mean_depth, matrix, natural):
    width = late_rows.shape[-1]
    order = matrix[...]
    place = Place(rows)
    depth = depth_of(mean_depth, width)
    for field in range(3):
        for part, first in ((early_rows, 0), (late_rows, rows - HALO)):
            count = part.shape[1]
            value = part[field] - depth if field == 0 else part[field]
            if field == 2:
                value = value * place.sign
            value = select(value.reshape(count * 8, width), order, 3).reshape(count, 8, width)
            for i in range(count):
                store_row(natural, field, rows, width, place.own_row(rows, first + i), value[i])


def final_kernel(
    rows, incoming, near_edge, far_edge, previous, coarse_wet, coarse_before, mean_depth, coupling, natural, order,
    spread,
    new_ends, coarse_new,
    state, hv, press, result,
):
    coarse_rows = rows // 2
    half = incoming.shape[-1]
    width = 2 * half
    place = Place(rows)
    depth = depth_of(mean_depth, half)
    for field in range(3):
        state[field, 0] = turned(near_edge[field], field)
        state[field, coarse_rows + 1] = turned(far_edge[field], field)
        state[field, 1 : coarse_rows + 1] = incoming[field]
    state[0, 0] += (1.0 - place.near_inside) * depth
    state[0, coarse_rows + 1] += (1.0 - place.far_inside) * depth
    kron_parts = {CHUNK: coupling_parts(coupling[...], CHUNK)}

    def emit(i, values):
        for field in range(3):
            result[field, i] = jnp.where(place.last, values[field], previous[field, i])

    coarse_update(
        state, hv, press, coarse_wet, coarse_rows, kron_parts, place.coarse_first, place.coarse_step, emit
    )
    to_natural, to_fine = order[...], spread[...]
    for field in range(3):
        value = result[field].reshape(coarse_rows * 8, half)
        change = value - coarse_before[field].reshape(coarse_rows * 8, half)
        if field == 0:
            value = (result[0] - depth).reshape(coarse_rows * 8, half)
        if field == 2:
            value, change = value * place.sign, change * place.sign
        fine = select(change, to_fine, 2).reshape(coarse_rows, 8, width)
        value = select(value, to_natural, 2).reshape(coarse_rows, 8, half)
        for i in range(coarse_rows):
            store_row(coarse_new, field, coarse_rows, half, place.own_row(coarse_rows, i), value[i])
            for r in (2 * i, 2 * i + 1):
                for c, part in enumerate(tile_slices(rows, width, place.own_row(rows, r))):
                    new_ends[field, part, :] = natural[field, part, :] + fine[i, :, c * LANES : (c + 1) * LANES]


def middle_turn(incoming, near_edge, far_edge, coarse_wet, mean_depth, coupling, place):
    signs = jnp.asarray([1.0, 1.0, -1.0], f32)[:, None, None]
    before = (near_edge * signs).at[0].add((1.0 - place.near_inside) * mean_depth[:, None])
    after = (far_edge * signs).at[0].add((1.0 - place.far_inside) * mean_depth[:, None])
    state = jnp.concatenate([before[:, None], incoming, after[:, None]], axis=1)
    h, u, v = state
    e = h - mean_depth[None, :, None]
    rows, layers, half = incoming.shape[1:]
    blocks = half // LANES
    p = jnp.einsum("kl,rlc->rkc", coupling, e, precision=lax.Precision.HIGHEST)

    def dx_parts(q):
        q = q.reshape(q.shape[0], layers, blocks, LANES)
        east = jnp.concatenate([q[:, :, 1:], jnp.roll(q[:, :, :1], -1, -1)], axis=2)
        west = jnp.concatenate([jnp.roll(q[:, :, -1:], 1, -1), q[:, :, :-1]], axis=2)
        return east.reshape(-1, layers, half)[1:-1], west.reshape(-1, layers, half)[1:-1]

    def dx(q):
        east, west = dx_parts(q)
        return (east - west) / 4.0

    def dy(q):
        return (q[2:] - q[:-2]) / 4.0

    def lap(q):
        east, west = dx_parts(q)
        return (q[2:] + q[:-2] + east + west - 4.0 * q[1:-1]) / 4.0

    um, vm = u[1:-1], v[1:-1]
    f = (place.coarse_first + place.coarse_step * jnp.arange(rows, dtype=f32))[:, None, None] / 4.0
    de = -(dx(h * u) + dy(h * v))
    du = coarse_wet * (-(um * dx(u) + vm * dy(u)) + f * vm - dx(p) + viscosity * lap(u))
    dv = coarse_wet * (-(um * dx(v) + vm * dy(v)) - f * um - dy(p) + viscosity * lap(v))
    return incoming + STEPS * time_step * jnp.stack([de, du, dv])


def local(starts, coarse_old, mean_depth, coupling, wet_cells):
    layers, rows, width = starts.shape[2:]
    coarse_rows, half = rows // 2, width // 2
    assert layers == 8 and rows % 8 == 0 and HALO < rows <= 2 * HALO
    tm, tm_size = lax.axis_index("tm"), lax.axis_size("tm")
    lat_size = lax.axis_size("lat")
    starts = tiles_of(starts[0])
    coarse_old = tiles_of(coarse_old[0])
    vmem = pl.BlockSpec(memory_space=pltpu.VMEM)
    hbm = pl.BlockSpec(memory_space=pltpu.HBM)
    fine_order = interleave_matrix(width)
    coarse_order = interleave_matrix(half)
    planes = 3 * HALO + 2

    def array(*shape):
        return jax.ShapeDtypeStruct(shape, f32)

    def buffer(*shape):
        return pltpu.VMEM(shape, f32)

    def call(kernel, outs, in_specs, scratch=()):
        return pl.pallas_call(
            functools.partial(kernel, rows),
            out_shape=outs,
            in_specs=in_specs,
            out_specs=[vmem] * len(outs),
            scratch_shapes=list(scratch),
            compiler_params=pltpu.CompilerParams(vmem_limit_bytes=16 * 2**20),
        )

    near_of = [i + 1 if i % 2 == 0 else i - 1 for i in range(lat_size)]
    far_of = [i - 1 if i % 2 == 0 else i + 1 for i in range(lat_size)]

    def neighbours(of):
        return [(i, j) for i, j in enumerate(of) if 0 <= j < lat_size]

    to_near, to_far = call(
        pack_kernel,
        [array(planes, 8, width)] * 2,
        [hbm] * 2,
        [
            buffer(*starts.shape),
            pltpu.VMEM((rows, width), jnp.int32),
            buffer(rows, width),
            pltpu.SemaphoreType.DMA((4,)),
        ],
    )(*[pltpu.with_memory_space_constraint(x, pltpu.HBM) for x in (starts, wet_cells)])
    far = lax.ppermute(to_far, "lat", neighbours(far_of))
    near = lax.ppermute(to_near, "lat", neighbours(near_of))
    mean_depths = mean_depth.reshape(1, layers)

    def stage_scratch(count):
        return [buffer(3, count, 8, width)] * 3 + [buffer(count, 8, width)] * 2 + [
            buffer(6, count, 8, width),
            *[pltpu.VMEM((n * 8, 3 * n * 8), bf16) for n in (GROUP, CHUNK)],
        ]

    early_rows, strips, coarse_before, first, coarse_wet = call(
        near_kernel,
        [array(3, rows - HALO, 8, width), array(HALO, 3, 3, 8, width)]
        + [array(3, coarse_rows, 8, half)] * 2
        + [array(coarse_rows, 8, half)],
        [vmem] * 7,
        stage_scratch(HALO + rows),
    )(near, to_near, to_far, coarse_old, mean_depths, coupling, jnp.asarray(coarse_order, bf16))

    late_rows, delta, outcome, passed = call(
        far_kernel,
        [array(3, HALO, 8, width)] + [array(3, coarse_rows, 8, half)] * 3,
        [vmem] * 10,
        stage_scratch(2 * HALO + 1) + [buffer(3, coarse_rows + 2, 8, half)],
    )(far, to_far, near, strips, early_rows, first, coarse_before, coarse_wet, mean_depths, coupling)

    both = ("tm", "lat")

    def hand_on(current):
        def moved(values, of):
            pairs = [
                (t * lat_size + i, (t + 1) * lat_size + j)
                for t in range(tm_size - 1)
                for i, j in enumerate(of)
                if 0 <= j < lat_size
            ]
            return lax.ppermute(values, both, pairs)

        return moved(current, range(lat_size)), moved(current[:, 0], near_of), moved(current[:, -1], far_of)

    previous = outcome
    incoming = hand_on(passed)
    (natural,) = call(natural_kernel, [array(*starts.shape)], [vmem] * 4)(
        early_rows, late_rows, mean_depths, jnp.asarray(fine_order.T, bf16)
    )
    for turn in range(1, tm_size - 1):
        outcome = middle_turn(*incoming, coarse_wet, mean_depth, coupling, Place(rows))
        previous = jnp.where(tm == turn, outcome, previous)
        incoming = hand_on(delta + outcome)

    new_ends, coarse_new = call(
        final_kernel,
        [array(*starts.shape), array(*coarse_old.shape)],
        [vmem] * 11,
        [buffer(3, coarse_rows + 2, 8, half)]
        + [buffer(coarse_rows + 2, 8, half)] * 2
        + [buffer(3, coarse_rows, 8, half)],
    )(
        *incoming, previous, coarse_wet, coarse_before, mean_depths, coupling, natural,
        jnp.asarray(coarse_order.T, bf16), jnp.asarray(prolong_matrix(width), bf16),
    )
    return (
        from_tiles(new_ends, layers, rows, width)[None],
        from_tiles(coarse_new, layers, coarse_rows, half)[None],
    )


def solution(mesh):
    in_specs = (
        P("tm", None, None, "lat", None),
        P("tm", None, None, "lat", None),
        P(),
        P(),
        P("lat", None),
    )
    out_specs = (P("tm", None, None, "lat", None), P("tm", None, None, "lat", None))
    return jax.shard_map(local, mesh=mesh, in_specs=in_specs, out_specs=out_specs, check_vma=False)
```

time: 56.7 us -> 41.1 us (0.72)
  Pallas kernels: 37.9 us -> 22.5 us
  waiting for transfers between devices: 0.01 us -> 1.72 us
  starting transfers between devices: 13.7 us -> 12.6 us
    pallas_call x6 -> x5, Pallas kernels: 37.9 us -> 22.5 us  [the longest x1 8.92 us: local(): call(near_kernel, [array(3, rows - HALO, 8, width), array(HALO, 3, 3, 8,...]
    ppermute x2, starting transfers between devices: 6.43 us -> 4.61 us  [the longest x1 4.52 us: local(): far = lax.ppermute(to_far, 'lat', neighbours(far_of))]
    ppermute x2, waiting for transfers between devices: 0.01 us -> 1.71 us  [the longest x1 1.71 us: local(): far = lax.ppermute(to_far, 'lat', neighbours(far_of))]
    ppermute x3, starting transfers between devices: 7.28 us -> 8.02 us  [moved(): return lax.ppermute(values, both, pairs)]
    unnamed x23 -> x14, local copies, waits for them, and re-layouts: 3.04 us -> 3.18 us
  transfers between devices with their start and end apart: 5 -> 5, of which waited for: 0 -> 1; matrix products, arithmetic and copies ran while one was open for 1% -> 0% of each run, Pallas kernels for 34% -> 27%
where the time goes in v2:
time: 41.1 us; the launch traced here: 40.8 us
  Pallas kernels  22.5 us (55%)
  starting transfers between devices  12.6 us (31%)
  local copies, waits for them, and re-layouts  3.18 us (8%)
  waiting for transfers between devices  1.72 us (4%)
  between operations  0.76 us (2%)
    pallas_call x1, Pallas kernels, local(): call(near_kernel, [array(3, rows - HALO, 8, width), array(HALO, 3, 3, 8,...  8.92 us
    ppermute x3, starting transfers between devices, moved(): return lax.ppermute(values, both, pairs)  8.02 us
    pallas_call x1, Pallas kernels, local(): call(far_kernel, [array(3, HALO, 8, width)] + [array(3, coarse_rows, 8, h...  6.64 us
    ppermute x1, starting transfers between devices, local(): far = lax.ppermute(to_far, 'lat', neighbours(far_of))  4.52 us
    unnamed x14, local copies, waits for them, and re-layouts  3.18 us
    pallas_call x1, Pallas kernels, local(): call(final_kernel, [array(*starts.shape), array(*coarse_old.shape)], [vme...  2.49 us
    pallas_call x1, Pallas kernels, local(): call(pack_kernel, [array(planes, 8, width)] * 2, [hbm] * 2, [buffer(*star...  2.35 us
    pallas_call x1, Pallas kernels, local(): call(natural_kernel, [array(*starts.shape)], [vmem] * 4)  2.13 us
  transfers between devices with their start and end apart: 5, of which 1 were waited for; matrix products, arithmetic and copies ran while one was open for 0% of the time, Pallas kernels for 27%

profile of v2, /device:TPU:1, one launch (start us, length us, event | category | flops | bytes accessed | tf_op | source)
XLA Modules:
  0.0 40.8 jit_solution(5347861654996196556)
XLA Ops:
  0.6 2.4 %shard_map.104 = (f32[38,8,512]{2,1,0:T(8,128)S(1)}, f32[38,8,512]{2,1,0:T(8,128)S(1)}) custom-call(f32[3,512,128]{2,1,0:T(8,128)} %bitcast.30, s32[16,512]{1,0:T(8,128)} %wet_hbm.1), custom_call_target="tpu_custom_call" | custom-call | tf_op jit(solution)/shard_map/pallas_call | solution.py:560
  3.0 0.1 collective-permute-start.1
  3.1 4.5 %collective-permute-start = (f32[38,8,512]{2,1,0:T(8,128)S(1)}, f32[38,8,512]{2,1,0:T(8,128)S(1)}, u32[]{:S(2)}, u32[]{:S(2)}) collective-permute-start(f32[38,8,512]{2,1,0:T(8,128)S(1)} %get-tuple-element.14.to_far), channel_id=1, source_target_pairs={{1,2},{2,1},{3,4},{4,3},{5,6},{6,5},{7,8},{8,7},{9,10},{10,9},{11,... | collective-permute-start | bytes 1867784 | tf_op jit(solution)/shard_map/ppermute | solution.py:571
  7.6 0.0 collective-permute-done.1.near
  7.6 0.0 copy-start.2
  7.6 0.9 %copy-done.2 = f32[1,3,8,8,256]{4,3,2,1,0:T(8,128)S(1)} copy-done((f32[1,3,8,8,256]{4,3,2,1,0:T(8,128)S(1)}, f32[1,3,8,8,256]{4,3,2,1,0:T(8,128)}, u32[]{:S(2)}) %copy-start.2) | copy-done | bytes 196632
  8.5 0.0 copy-start.4
  8.5 0.9 %copy-done.4 = bf16[256,256]{1,0:T(8,128)(2,1)S(1)} copy-done((bf16[256,256]{1,0:T(8,128)(2,1)S(1)}, bf16[256,256]{1,0:T(8,128)(2,1)}, u32[]{:S(2)}) %copy-start.4) | copy-done | bytes 131096
  9.4 0.0 copy-start.5
  9.5 0.7 %copy-done.5 = f32[8,8]{1,0:T(8,128)S(1)} copy-done((f32[8,8]{1,0:T(8,128)S(1)}, f32[8,8]{1,0:T(8,128)}, u32[]{:S(2)}) %copy-start.5) | copy-done | bytes 280
  10.1 0.0 copy-start.6
  10.1 0.7 %copy-done.6 = f32[8]{0:T(128)S(1)} copy-done((f32[8]{0:T(128)S(1)}, f32[8]{0:T(128)}, u32[]{:S(2)}) %copy-start.6) | copy-done | bytes 56
  10.8 8.9 %shard_map.105 = (f32[3,4,8,512]{3,2,1,0:T(8,128)S(1)}, f32[12,3,3,8,512]{4,3,2,1,0:T(8,128)S(1)}, f32[3,8,8,256]{3,2,1,0:T(8,128)S(1)}, f32[3,8,8,256]{3,2,1,0:T(8,128)S(1)}, f32[8,8,256]{2,1,0:T(8,128)S(1)}) custom-call(f32[38,8,512]{2,1,0:T(8,128)S(1)} %collective-permute-done.1.near, f32[38,8,512]{2,1,0:T(8,128)S(1)} %get-tuple-element.15.to_near, ...), custom_call_target="tpu_custom_call" | custom-call | tf_op jit(solution)/shard_map/pallas_call | solution.py:581
  19.7 1.7 %collective-permute-done.far = f32[38,8,512]{2,1,0:T(8,128)S(1)} collective-permute-done((f32[38,8,512]{2,1,0:T(8,128)S(1)}, f32[38,8,512]{2,1,0:T(8,128)S(1)}, u32[]{:S(2)}, u32[]{:S(2)}) %collective-permute-start) | collective-permute-done | bytes 622624 | tf_op jit(solution)/shard_map/ppermute | solution.py:571
  21.4 0.0 copy-start
  21.4 6.6 %shard_map.106 = (f32[3,12,8,512]{3,2,1,0:T(8,128)S(1)}, f32[3,8,8,256]{3,2,1,0:T(8,128)}, f32[3,8,8,256]{3,2,1,0:T(8,128)S(1)}, f32[3,8,8,256]{3,2,1,0:T(8,128)S(1)}) custom-call(f32[38,8,512]{2,1,0:T(8,128)S(1)} %collective-permute-done.far, f32[38,8,512]{2,1,0:T(8,128)S(1)} %get-tuple-element.14.to_far, f32[38,8,512]{2,1,0:T(8,128)S(1)} %collective-permute-done.1.near, ...), custom_call_target="tpu_custom_call" | custom-call | tf_op jit(solution)/shard_map/pallas_call | solution.py:590
  28.1 0.0 copy-start.1
  28.1 0.0 copy-start.3
  28.1 3.3 %collective-permute-start.2 = (f32[3,8,8,256]{3,2,1,0:T(8,128)S(1)}, f32[3,8,8,256]{3,2,1,0:T(8,128)S(1)}, u32[]{:S(2)}, u32[]{:S(2)}) collective-permute-start(f32[3,8,8,256]{3,2,1,0:T(8,128)S(1)} %get-tuple-element.21), channel_id=1, source_target_pairs={{0,16},{1,17},{2,18},{3,19},{4,20},{5,21},{6,22},{7,23},{8,24},{9,... | collective-permute-start | bytes 589832 | tf_op jit(solution)/shard_map/ppermute | solution.py:607
  31.4 3.5 %collective-permute-start.4 = (f32[3,8,256]{2,1,0:T(8,128)S(1)}, f32[3,8,256]{2,1,0:T(8,128)S(1)}, u32[]{:S(2)}, u32[]{:S(2)}) collective-permute-start(f32[3,8,256]{2,1,0:T(8,128)S(1)} %get-tuple-element.26), channel_id=1, source_target_pairs={{1,18},{2,17},{3,20},{4,19},{5,22},{6,21},{7,24},{8,23},{9,26},{10... | collective-permute-start | bytes 73736 | tf_op jit(solution)/shard_map/ppermute | solution.py:607
  34.8 1.3 %collective-permute-start.3 = (f32[3,8,256]{2,1,0:T(8,128)S(1)}, f32[3,8,256]{2,1,0:T(8,128)S(1)}, u32[]{:S(2)}, u32[]{:S(2)}) collective-permute-start(f32[3,8,256]{2,1,0:T(8,128)S(1)} %get-tuple-element.27), channel_id=1, source_target_pairs={{0,17},{1,16},{2,19},{3,18},{4,21},{5,20},{6,23},{7,22},{8,25},{9,... | collective-permute-start | bytes 73736 | tf_op jit(solution)/shard_map/ppermute | solution.py:607
  36.1 0.0 copy-done
  36.1 2.1 %shard_map.107.natural = f32[3,512,128]{2,1,0:T(8,128)S(1)} custom-call(f32[3,4,8,512]{3,2,1,0:T(8,128)S(1)} %get-tuple-element.17.early_rows, f32[3,12,8,512]{3,2,1,0:T(8,128)S(1)} %get-tuple-element.23.late_rows, f32[1,8]{1,0:T(1,128)S(1)} %bitcast.28, bf16[512,512]{1,0:T(8,128)(2,1)S(1)} %copy-done), custom_call_target="tpu_custom_call" | custom-call | tf_op jit(solution)/shard_map/pallas_call | solution.py:613
  38.3 0.0 collective-permute-done.4.far_edge
  38.3 0.0 collective-permute-done.3.near_edge
  38.3 0.0 collective-permute-done.2.incoming
  38.3 0.0 copy-done.1
  38.3 0.0 copy-done.3
  38.3 2.5 %shard_map.108 = (f32[3,512,128]{2,1,0:T(8,128)}, f32[3,128,128]{2,1,0:T(8,128)}) custom-call(f32[3,8,8,256]{3,2,1,0:T(8,128)S(1)} %collective-permute-done.2.incoming, f32[3,8,256]{2,1,0:T(8,128)S(1)} %collective-permute-done.3.near_edge, f32[3,8,256]{2,1,0:T(8,128)S(1)} %collective-permute-done.4.far_edge, ...), custom_call_target="tpu_custom_call" | custom-call | tf_op jit(solution)/shard_map/pallas_call | solution.py:621
  (1 shorter events, 0.0 us)
Async XLA Ops:
  3.0 4.6 %collective-permute-start.1 = (f32[38,8,512]{2,1,0:T(8,128)S(1)}, f32[38,8,512]{2,1,0:T(8,128)S(1)}, u32[]{:S(2)}, u32[]{:S(2)}) collective-permute-start(f32[38,8,512]{2,1,0:T(8,128)S(1)} %get-tuple-element.15.to_near), channel_id=1, source_target_pairs={{0,1},{1,0},{2,3},{3,2},{4,5},{5,4},{6,7},{7,6},{8,9},{9,8},{10,11... | collective-permute-start | bytes 1867784 | tf_op jit(solution)/shard_map/ppermute | solution.py:572
  3.1 18.4 %collective-permute-start = (f32[38,8,512]{2,1,0:T(8,128)S(1)}, f32[38,8,512]{2,1,0:T(8,128)S(1)}, u32[]{:S(2)}, u32[]{:S(2)}) collective-permute-start(f32[38,8,512]{2,1,0:T(8,128)S(1)} %get-tuple-element.14.to_far), channel_id=1, source_target_pairs={{1,2},{2,1},{3,4},{4,3},{5,6},{6,5},{7,8},{8,7},{9,10},{10,9},{11,... | collective-permute-start | bytes 1867784 | tf_op jit(solution)/shard_map/ppermute | solution.py:571
  7.6 0.9 %copy-start.2 = (f32[1,3,8,8,256]{4,3,2,1,0:T(8,128)S(1)}, f32[1,3,8,8,256]{4,3,2,1,0:T(8,128)}, u32[]{:S(2)}) copy-start(f32[1,3,8,8,256]{4,3,2,1,0:T(8,128)} %param.10) | copy-start | bytes 589828
  8.5 0.9 %copy-start.4 = (bf16[256,256]{1,0:T(8,128)(2,1)S(1)}, bf16[256,256]{1,0:T(8,128)(2,1)}, u32[]{:S(2)}) copy-start(bf16[256,256]{1,0:T(8,128)(2,1)} %constant.8.clone.matrix) | copy-start | bytes 393220
  9.4 0.7 %copy-start.5 = (f32[8,8]{1,0:T(8,128)S(1)}, f32[8,8]{1,0:T(8,128)}, u32[]{:S(2)}) copy-start(f32[8,8]{1,0:T(8,128)} %coupling.5) | copy-start | bytes 772
  10.1 0.7 %copy-start.6 = (f32[8]{0:T(128)S(1)}, f32[8]{0:T(128)}, u32[]{:S(2)}) copy-start(f32[8]{0:T(128)} %param.11) | copy-start | bytes 100
  21.4 14.7 %copy-start = (bf16[512,512]{1,0:T(8,128)(2,1)S(1)}, bf16[512,512]{1,0:T(8,128)(2,1)}, u32[]{:S(2)}) copy-start(bf16[512,512]{1,0:T(8,128)(2,1)} %constant.9.clone.matrix) | copy-start | bytes 1572868
  28.1 10.2 %copy-start.1 = (bf16[256,512]{1,0:T(8,128)(2,1)S(1)}, bf16[256,512]{1,0:T(8,128)(2,1)}, u32[]{:S(2)}) copy-start(bf16[256,512]{1,0:T(8,128)(2,1)} %constant.11.clone.spread) | copy-start | bytes 786436
  28.1 10.2 %copy-start.3 = (bf16[256,256]{1,0:T(8,128)(2,1)S(1)}, bf16[256,256]{1,0:T(8,128)(2,1)}, u32[]{:S(2)}) copy-start(bf16[256,256]{1,0:T(8,128)(2,1)} %constant.10.clone.order) | copy-start | bytes 393220
  28.1 10.2 %collective-permute-start.2 = (f32[3,8,8,256]{3,2,1,0:T(8,128)S(1)}, f32[3,8,8,256]{3,2,1,0:T(8,128)S(1)}, u32[]{:S(2)}, u32[]{:S(2)}) collective-permute-start(f32[3,8,8,256]{3,2,1,0:T(8,128)S(1)} %get-tuple-element.21), channel_id=1, source_target_pairs={{0,16},{1,17},{2,18},{3,19},{4,20},{5,21},{6,22},{7,23},{8,24},{9,... | collective-permute-start | bytes 589832 | tf_op jit(solution)/shard_map/ppermute | solution.py:607
  31.4 6.9 %collective-permute-start.4 = (f32[3,8,256]{2,1,0:T(8,128)S(1)}, f32[3,8,256]{2,1,0:T(8,128)S(1)}, u32[]{:S(2)}, u32[]{:S(2)}) collective-permute-start(f32[3,8,256]{2,1,0:T(8,128)S(1)} %get-tuple-element.26), channel_id=1, source_target_pairs={{1,18},{2,17},{3,20},{4,19},{5,22},{6,21},{7,24},{8,23},{9,26},{10... | collective-permute-start | bytes 73736 | tf_op jit(solution)/shard_map/ppermute | solution.py:607
  34.8 3.5 %collective-permute-start.3 = (f32[3,8,256]{2,1,0:T(8,128)S(1)}, f32[3,8,256]{2,1,0:T(8,128)S(1)}, u32[]{:S(2)}, u32[]{:S(2)}) collective-permute-start(f32[3,8,256]{2,1,0:T(8,128)S(1)} %get-tuple-element.27), channel_id=1, source_target_pairs={{0,17},{1,16},{2,19},{3,18},{4,21},{5,20},{6,23},{7,22},{8,25},{9,... | collective-permute-start | bytes 73736 | tf_op jit(solution)/shard_map/ppermute | solution.py:607

commit v3 on v2

--- a/solution.py
+++ b/solution.py
@@ -11,6 +11,7 @@
 
 STEPS = 4
 HALO = 3 * STEPS
+NEAR = HALO + 2
 GROUP = 6
 CHUNK = GROUP + 2
 LANES = 128
@@ -64,11 +65,6 @@
     return jnp.concatenate([tiles[field, part, :] for part in tile_slices(rows, width, r)], axis=1)
 
 
-def store_row(tiles, field, rows, width, r, value):
-    for c, part in enumerate(tile_slices(rows, width, r)):
-        tiles[field, part, :] = value[:, c * LANES : (c + 1) * LANES]
-
-
 def blocks_of(x):
     return [x[:, c : c + LANES] for c in range(0, x.shape[1], LANES)]
 
@@ -99,6 +95,26 @@
 
 def select(x, matrix, parts):
     return sum(dot(part, matrix) for part in split(x, parts))
+
+
+def select_blocks(x, matrix, parts, block=2 * LANES):
+    terms = split(x, parts)
+    for c in range(0, matrix.shape[1], block):
+        yield c, sum(dot(part, matrix[:, c : c + block]) for part in terms)
+
+
+def layer_major(place, rows, source_rows):
+    repeat = rows // source_rows
+    shape = (8 * rows, 8 * source_rows)
+    target = lax.broadcasted_iota(jnp.int32, shape, 0)
+    source = lax.broadcasted_iota(jnp.int32, shape, 1)
+    layer = lax.div(target, rows)
+    row = lax.div(place.own_row(rows, target - rows * layer), repeat)
+    return jnp.where(source == 8 * row + layer, 1.0, 0.0).astype(bf16)
+
+
+def reorder(matrix, x, parts=2):
+    return sum(dot(matrix, part) for part in split(x, parts))
 
 
 def coupling_parts(coupling, count):
@@ -222,23 +238,23 @@
     lax.fori_loop(0, rest, two, 0)
 
 
-def coarse_update(state, hv, press, wet, rows, kron_parts, first_coriolis, coriolis_step, emit):
+def coarse_update(state, hv, press, wet_of, size, rows, kron_parts, coriolis_of, emit, inside=1.0):
     scale = STEPS * time_step / 4.0
     start = 0
-    while start < rows + 2:
-        pressure_rows(state, hv, press, min(start, rows + 2 - CHUNK), CHUNK, kron_parts)
+    while start < size:
+        pressure_rows(state, hv, press, min(start, size - CHUNK), CHUNK, kron_parts)
         start += CHUNK
-    for i in range(rows):
-        coriolis = first_coriolis + coriolis_step * i
-        (h, u, v), (dh, du, dv) = row_tendency(state, hv, press, i + 1, viscosity, coriolis)
-        mask = wet[i] * scale
+    for i in rows:
+        (h, u, v), (dh, du, dv) = row_tendency(state, hv, press, i, viscosity, coriolis_of(i))
+        mask = wet_of(i) * scale
         keep = 1.0 - 4.0 * viscosity * mask
-        emit(i, (h - scale * dh, keep * u + mask * du, keep * v + mask * dv))
-
-
-def wet_row(halo, i):
-    plane, row = (0, i) if i < 8 else (1, i - HALO + 8)
-    return halo[3 * HALO + plane, pl.ds(row, 1), :]
+        step = scale * inside if i == rows[0] else scale
+        emit(i, (h - step * dh, keep * u + mask * du, keep * v + mask * dv))
+
+
+def wet_row(halo, count, i):
+    plane, row = (0, i) if i < 8 else (1, i - count + 8)
+    return halo[3 * count + plane, pl.ds(row, 1), :]
 
 
 def set_masks(wet, i, mask):
@@ -252,43 +268,58 @@
     return -x if field == 2 else x
 
 
-def pack_kernel(rows, starts_hbm, wet_hbm, to_near, to_far, starts, wet_cells, wet, semaphores):
+def pack_kernel(
+    rows, starts_hbm, wet_hbm, coarse_hbm, coupling_hbm, depth_hbm, order_hbm,
+    to_near, to_far, coarse_old, coupling, mean_depth, coarse_order,
+    starts, wet_cells, wet, semaphores,
+):
     width = wet_cells.shape[-1]
     blocks = width // LANES
-    copies = [
-        pltpu.make_async_copy(source, target, semaphores.at[n])
-        for n, (source, target) in enumerate(
-            [(starts_hbm.at[field], starts.at[field]) for field in range(3)] + [(wet_hbm, wet_cells)]
-        )
-    ]
+    pairs = [(starts_hbm.at[field], starts.at[field]) for field in range(3)] + [(wet_hbm, wet_cells)]
+    pairs += [(coarse_hbm, coarse_old), (coupling_hbm, coupling), (depth_hbm, mean_depth), (order_hbm, coarse_order)]
+    copies = [pltpu.make_async_copy(source, target, semaphores.at[n]) for n, (source, target) in enumerate(pairs)]
     for copy in copies:
         copy.start()
     place = Place(rows)
     column = lax.broadcasted_iota(jnp.int32, (width, LANES), 0)
     column = column - blocks * lax.broadcasted_iota(jnp.int32, (width, LANES), 1)
     order = jnp.concatenate([jnp.where(column == c, 1.0, 0.0).astype(bf16) for c in range(blocks)], axis=1)
+    sent = ((to_near, 0, NEAR), (to_far, rows - HALO, HALO))
     for field in range(3):
         copies[field].wait()
         state = [load_row(starts, field, rows, width, place.own_row(rows, i)) for i in range(rows)]
         state = jnp.concatenate(state, axis=0)
-        state = select(state * place.sign if field == 2 else state, order, 2).reshape(rows, 8, width)
-        to_near[field * HALO : (field + 1) * HALO] = state[:HALO]
-        to_far[field * HALO : (field + 1) * HALO] = state[rows - HALO :]
+        for c, value in select_blocks(state * place.sign if field == 2 else state, order, 2):
+            value = value.reshape(rows, 8, value.shape[1])
+            for packed, first, count in sent:
+                packed[field * count : (field + 1) * count, :, c : c + value.shape[2]] = value[first : first + count]
     copies[3].wait()
     wet[...] = dot(wet_cells[...].astype(f32).astype(bf16), order)
-    for plane, skip in ((0, 0), (1, HALO - 8)):
-        for i in range(8):
-            for packed, first in ((to_near, 0), (to_far, rows - HALO)):
-                row = place.own_row(rows, first + skip + i)
-                packed[3 * HALO + plane, pl.ds(i, 1), :] = wet[pl.ds(row, 1), :]
+    for packed, first, count in sent:
+        for plane, skip in ((0, 0), (1, count - 8)):
+            if plane == 0 or count > 8:
+                for i in range(min(8, count)):
+                    row = place.own_row(rows, first + skip + i)
+                    packed[3 * count + plane, pl.ds(i, 1), :] = wet[pl.ds(row, 1), :]
+    for copy in copies[4:]:
+        copy.wait()
+    half = width // 2
+    old = [load_row(coarse_old, field, rows // 2, half, place.own_row(rows // 2, 0)) for field in range(3)]
+    old[2] = old[2] * place.sign
+    old = select(jnp.concatenate(old, axis=0), coarse_order[...], 2)
+    to_near[3 * NEAR + 2, :, :half] = old[:8]
+    to_near[3 * NEAR + 2, :, half:] = old[8:16]
+    to_near[3 * NEAR + 3, :, :half] = old[16:]
+    to_near[3 * NEAR + 3, :, half:] = old[16:]
 
 
 def near_kernel(
     rows, near, to_near, to_far, coarse_old, mean_depth, coupling, matrix,
-    early_rows, strips, coarse_before, first, coarse_wet,
+    early_rows, strips, coarse_before, first, outcome, coarse_wet,
     y, a, b, hv, press, wet, short_parts, long_parts,
 ):
     width = y.shape[-1]
+    half = width // 2
     coarse_rows = rows // 2
     place = Place(rows)
     depth = depth_of(mean_depth, width)
@@ -296,51 +327,68 @@
     for count, parts in ((GROUP, short_parts), (CHUNK, long_parts)):
         parts[...] = coupling_parts(coupling[...], count)
         kron_parts[count] = parts
-    for i in range(HALO):
+    for i in range(NEAR):
         for field in range(3):
-            value = turned(near[field * HALO + i], field)
-            y[field, HALO - 1 - i] = value + depth if field == 0 else value
-        set_masks(wet, HALO - 1 - i, jnp.broadcast_to(wet_row(near, i), (8, width)))
+            value = turned(near[field * NEAR + i], field)
+            y[field, NEAR - 1 - i] = value + depth if field == 0 else value
+        set_masks(wet, NEAR - 1 - i, jnp.broadcast_to(wet_row(near, NEAR, i), (8, width)))
     for i in range(rows):
-        sent, at = (to_near, i) if i < HALO else (to_far, i - rows + HALO)
+        sent, at, count = (to_near, i, NEAR) if i < NEAR else (to_far, i - rows + HALO, HALO)
         for field in range(3):
-            value = sent[field * HALO + at]
-            y[field, HALO + i] = value + depth if field == 0 else value
-        set_masks(wet, HALO + i, jnp.broadcast_to(wet_row(sent, at), (8, width)))
-
-    def coriolis_of(r):
-        return place.first + place.step * (r - HALO).astype(f32)
-
-    def inside_of(r):
-        return jnp.where(r < HALO, place.near_inside, 1.0)
+            value = sent[field * count + at]
+            y[field, NEAR + i] = value + depth if field == 0 else value
+        set_masks(wet, NEAR + i, jnp.broadcast_to(wet_row(sent, count, at), (8, width)))
 
     def keep(state, t):
         for field in range(3):
-            strips[t, field] = state[field, pl.ds(HALO + rows - 3 - t, 3)]
+            strips[t, field] = state[field, pl.ds(NEAR + rows - 3 - t, 3)]
 
     keep(y, 0)
-    for i in range(coarse_rows):
-        both = wet[0, HALO + 2 * i] * wet[0, HALO + 2 * i + 1]
+
+    for i in range(coarse_rows + 2):
+        at = NEAR - 4 + 2 * i
+        both = wet[0, at] * wet[0, at + 1]
         blocks = blocks_of(jnp.where(both > 0.0, 1.0, 0.0))
         coarse_wet[i] = jnp.concatenate([p * q for p, q in zip(blocks[0::2], blocks[1::2])], axis=1)
         for field in range(3):
-            first[field, i] = restrict_pair(y[field, HALO + 2 * i], y[field, HALO + 2 * i + 1])
+            first[field, i] = restrict_pair(y[field, at], y[field, at + 1])
+
+    def emit(i, values):
+        for field in range(3):
+            outcome[field, i - 1] = values[field]
+
+    coarse_update(
+        first, hv.at[:, :, pl.ds(0, half)], press.at[:, :, pl.ds(0, half)], lambda i: coarse_wet[i],
+        coarse_rows + 2, range(1, coarse_rows + 1), kron_parts,
+        lambda i: place.coarse_first + place.coarse_step * (i - 2), emit, place.near_inside,
+    )
     order = matrix[...]
+    arrived = ((3 * NEAR + 2, 0), (3 * NEAR + 2, half), (3 * NEAR + 3, 0))
     for field in range(3):
         old = [
-            load_row(coarse_old, field, coarse_rows, width // 2, place.own_row(coarse_rows, i))
+            load_row(coarse_old, field, coarse_rows, half, place.own_row(coarse_rows, i))
             for i in range(coarse_rows)
         ]
-        old = select(jnp.concatenate(old, axis=0), order, 2).reshape(coarse_rows, 8, width // 2)
+        old = select(jnp.concatenate(old, axis=0), order, 2).reshape(coarse_rows, 8, half)
+        plane, at = arrived[field]
+        edge = turned(near[plane, :, at : at + half], field)
         if field == 0:
-            old = old + depth[:, : width // 2]
-        coarse_before[field] = old * place.sign if field == 2 else old
+            old, edge = old + depth[:, :half], edge + depth[:, :half]
+        coarse_before[field, 0] = edge
+        coarse_before[field, 1:] = old * place.sign if field == 2 else old
+
+    def coriolis_of(r):
+        return place.first + place.step * (r - NEAR).astype(f32)
+
+    def inside_of(r):
+        return jnp.where(r < NEAR, place.near_inside, 1.0)
 
     def step(k, unused):
         for which, (source, target) in enumerate(((y, a), (a, b), (b, y))):
             s = 3 * k + which + 1
             run_stage(
-                source, target, y, hv, press, wet, s, HALO + rows - s, HALO + rows - 2 * s, which, kron_parts, coriolis_of, inside_of
+                source, target, y, hv, press, wet, s, NEAR + rows - s, NEAR + rows - 2 * s, which, kron_parts,
+                coriolis_of, inside_of,
             )
 
             @pl.when(s < HALO)
@@ -351,13 +399,12 @@
 
     lax.fori_loop(0, STEPS, step, 0)
     for field in range(3):
-        early_rows[field] = y[field, HALO : HALO + rows - HALO]
+        early_rows[field] = y[field, NEAR - 2 : NEAR + rows - HALO]
 
 
 def far_kernel(
-    rows, far, to_far, near, strips, early_rows, first, coarse_before, coarse_wet,
-    mean_depth, coupling,
-    late_rows, delta, outcome, passed,
+    rows, far, to_far, strips, early_rows, first, outcome, coarse_before, coarse_wet, mean_depth, coupling,
+    late_rows, delta, last_outcome, passed,
     y, a, b, hv, press, wet, short_parts, long_parts, state,
 ):
     width = y.shape[-1]
@@ -374,23 +421,23 @@
         for i in range(HALO):
             value = turned(far[(field + 1) * HALO - 1 - i], field)
             y[field, own + i] = value + depth if field == 0 else value
-        state[field, 1 : coarse_rows + 1] = first[field]
+        state[field, : coarse_rows - 1] = first[field, 3:]
     for i in range(HALO):
-        set_masks(wet, own + i, jnp.broadcast_to(wet_row(far, HALO - 1 - i), (8, width)))
-        set_masks(wet, own - HALO + i, jnp.broadcast_to(wet_row(to_far, i), (8, width)))
-
-    for field in range(3):
-        edge = turned(restrict_pair(near[field * HALO], near[field * HALO + 1]), field)
-        state[field, 0] = edge + depth[:, : width // 2] if field == 0 else edge
-        state[field, coarse_rows + 1] = restrict_pair(y[field, own], y[field, own + 1])
+        set_masks(wet, own + i, jnp.broadcast_to(wet_row(far, HALO, HALO - 1 - i), (8, width)))
+        set_masks(wet, own - HALO + i, jnp.broadcast_to(wet_row(to_far, HALO, i), (8, width)))
+
+    for field in range(3):
+        state[field, coarse_rows - 1] = restrict_pair(y[field, own], y[field, own + 1])
 
     def emit(i, values):
         for field in range(3):
-            outcome[field, i] = values[field]
-
+            last_outcome[field] = values[field]
+
+    half = width // 2
     coarse_update(
-        state, hv.at[:, :, pl.ds(0, width // 2)], press.at[:, :, pl.ds(0, width // 2)], coarse_wet, coarse_rows,
-        kron_parts, place.coarse_first, place.coarse_step, emit,
+        state, hv.at[:, :, pl.ds(0, half)], press.at[:, :, pl.ds(0, half)], lambda i: coarse_wet[coarse_rows + 1],
+        coarse_rows, [coarse_rows - 2], kron_parts,
+        lambda i: place.coarse_first + place.coarse_step * (coarse_rows - 1), emit,
     )
 
     def coriolis_of(r):
@@ -416,37 +463,40 @@
     early = rows - HALO
     for field in range(3):
         late_rows[field] = y[field, own - HALO : own]
-        for i in range(coarse_rows):
+        for i in range(-1, coarse_rows):
             if 2 * i < early:
-                pair = early_rows[field, 2 * i], early_rows[field, 2 * i + 1]
+                pair = early_rows[field, 2 * i + 2], early_rows[field, 2 * i + 3]
             else:
                 pair = y[field, 2 * i - origin], y[field, 2 * i + 1 - origin]
-            difference = restrict_pair(*pair) - coarse_before[field, i]
-            delta[field, i] = difference
-            passed[field, i] = difference + outcome[field, i]
+            difference = restrict_pair(*pair) - coarse_before[field, i + 1]
+            delta[field, i + 1] = difference
+            before = last_outcome[field] if i == coarse_rows - 1 else outcome[field, i + 1]
+            passed[field, i + 1] = difference + before
 
 
 def natural_kernel(rows, early_rows, late_rows, mean_depth, matrix, natural):
     width = late_rows.shape[-1]
-    order = matrix[...]
     place = Place(rows)
     depth = depth_of(mean_depth, width)
     for field in range(3):
-        for part, first in ((early_rows, 0), (late_rows, rows - HALO)):
-            count = part.shape[1]
-            value = part[field] - depth if field == 0 else part[field]
-            if field == 2:
-                value = value * place.sign
-            value = select(value.reshape(count * 8, width), order, 3).reshape(count, 8, width)
-            for i in range(count):
-                store_row(natural, field, rows, width, place.own_row(rows, first + i), value[i])
+        value = jnp.concatenate([part[field] for part in (early_rows.at[:, 2:], late_rows)], axis=0)
+        if field == 0:
+            value = value - depth
+        if field == 2:
+            value = value * place.sign
+        for c, piece in select_blocks(value.reshape(rows * 8, width), matrix, 2):
+            piece = piece.reshape(rows, 8, piece.shape[1])
+            for r in range(rows):
+                slices = tile_slices(rows, width, place.own_row(rows, r))
+                for at in range(0, piece.shape[2], LANES):
+                    natural[field, slices[(c + at) // LANES], :] = piece[r, :, at : at + LANES]
 
 
 def final_kernel(
-    rows, incoming, near_edge, far_edge, previous, coarse_wet, coarse_before, mean_depth, coupling, natural, order,
+    rows, incoming, far_edge, previous, last_previous, coarse_wet, coarse_before, mean_depth, coupling, natural, order,
     spread,
     new_ends, coarse_new,
-    state, hv, press, result,
+    state, hv, press, result, ends, coarse, semaphores,
 ):
     coarse_rows = rows // 2
     half = incoming.shape[-1]
@@ -454,42 +504,54 @@
     place = Place(rows)
     depth = depth_of(mean_depth, half)
     for field in range(3):
-        state[field, 0] = turned(near_edge[field], field)
+        state[field, : coarse_rows + 1] = incoming[field]
         state[field, coarse_rows + 1] = turned(far_edge[field], field)
-        state[field, 1 : coarse_rows + 1] = incoming[field]
-    state[0, 0] += (1.0 - place.near_inside) * depth
     state[0, coarse_rows + 1] += (1.0 - place.far_inside) * depth
     kron_parts = {CHUNK: coupling_parts(coupling[...], CHUNK)}
 
     def emit(i, values):
         for field in range(3):
-            result[field, i] = jnp.where(place.last, values[field], previous[field, i])
+            before = last_previous[field] if i == coarse_rows else previous[field, i]
+            result[field, i - 1] = jnp.where(place.last, values[field], before)
 
     coarse_update(
-        state, hv, press, coarse_wet, coarse_rows, kron_parts, place.coarse_first, place.coarse_step, emit
+        state, hv, press, lambda i: coarse_wet[i + 1], coarse_rows + 2, range(1, coarse_rows + 1), kron_parts,
+        lambda i: place.coarse_first + place.coarse_step * (i - 1), emit,
     )
-    to_natural, to_fine = order[...], spread[...]
+    to_natural = order[...]
+    fine_rows = layer_major(place, rows, coarse_rows)
+    own_rows = layer_major(place, coarse_rows, coarse_rows)
+    copies = []
     for field in range(3):
         value = result[field].reshape(coarse_rows * 8, half)
-        change = value - coarse_before[field].reshape(coarse_rows * 8, half)
+        change = value - coarse_before[field, 1:].reshape(coarse_rows * 8, half)
         if field == 0:
             value = (result[0] - depth).reshape(coarse_rows * 8, half)
         if field == 2:
             value, change = value * place.sign, change * place.sign
-        fine = select(change, to_fine, 2).reshape(coarse_rows, 8, width)
-        value = select(value, to_natural, 2).reshape(coarse_rows, 8, half)
-        for i in range(coarse_rows):
-            store_row(coarse_new, field, coarse_rows, half, place.own_row(coarse_rows, i), value[i])
-            for r in (2 * i, 2 * i + 1):
-                for c, part in enumerate(tile_slices(rows, width, place.own_row(rows, r))):
-                    new_ends[field, part, :] = natural[field, part, :] + fine[i, :, c * LANES : (c + 1) * LANES]
-
-
-def middle_turn(incoming, near_edge, far_edge, coarse_wet, mean_depth, coupling, place):
+        value = select(reorder(own_rows, value), to_natural, 2)
+        for k in range(coarse_rows):
+            for c in range(half // LANES):
+                tile = pl.ds((k * (half // LANES) + c) * 8, 8)
+                coarse[field, tile, :] = value[8 * k : 8 * k + 8, c * LANES : (c + 1) * LANES]
+        copies.append(pltpu.make_async_copy(coarse.at[field], coarse_new.at[field], semaphores.at[3 + field]))
+        copies[-1].start()
+        for c, fine in select_blocks(reorder(fine_rows, change), spread, 2):
+            for k in range(8 * rows // 8):
+                for at in range(0, fine.shape[1], LANES):
+                    tile = pl.ds((k * (width // LANES) + (c + at) // LANES) * 8, 8)
+                    ends[field, tile, :] = natural[field, tile, :] + fine[8 * k : 8 * k + 8, at : at + LANES]
+        copies.append(pltpu.make_async_copy(ends.at[field], new_ends.at[field], semaphores.at[field]))
+        copies[-1].start()
+    for copy in copies:
+        copy.wait()
+
+
+def middle_turn(incoming, far_edge, coarse_wet, mean_depth, coupling, place):
     signs = jnp.asarray([1.0, 1.0, -1.0], f32)[:, None, None]
-    before = (near_edge * signs).at[0].add((1.0 - place.near_inside) * mean_depth[:, None])
     after = (far_edge * signs).at[0].add((1.0 - place.far_inside) * mean_depth[:, None])
-    state = jnp.concatenate([before[:, None], incoming, after[:, None]], axis=1)
+    state = jnp.concatenate([incoming, after[:, None]], axis=1)
+    incoming = incoming[:, 1:]
     h, u, v = state
     e = h - mean_depth[None, :, None]
     rows, layers, half = incoming.shape[1:]
@@ -524,7 +586,7 @@
 def local(starts, coarse_old, mean_depth, coupling, wet_cells):
     layers, rows, width = starts.shape[2:]
     coarse_rows, half = rows // 2, width // 2
-    assert layers == 8 and rows % 8 == 0 and HALO < rows <= 2 * HALO
+    assert layers == 8 and rows % 8 == 0 and NEAR <= rows <= 2 * HALO
     tm, tm_size = lax.axis_index("tm"), lax.axis_size("tm")
     lat_size = lax.axis_size("lat")
     starts = tiles_of(starts[0])
@@ -533,7 +595,6 @@
     hbm = pl.BlockSpec(memory_space=pltpu.HBM)
     fine_order = interleave_matrix(width)
     coarse_order = interleave_matrix(half)
-    planes = 3 * HALO + 2
 
     def array(*shape):
         return jax.ShapeDtypeStruct(shape, f32)
@@ -541,12 +602,12 @@
     def buffer(*shape):
         return pltpu.VMEM(shape, f32)
 
-    def call(kernel, outs, in_specs, scratch=()):
+    def call(kernel, outs, in_specs, scratch=(), out_specs=None):
         return pl.pallas_call(
             functools.partial(kernel, rows),
             out_shape=outs,
             in_specs=in_specs,
-            out_specs=[vmem] * len(outs),
+            out_specs=out_specs or [vmem] * len(outs),
             scratch_shapes=list(scratch),
             compiler_params=pltpu.CompilerParams(vmem_limit_bytes=16 * 2**20),
         )
@@ -557,20 +618,23 @@
     def neighbours(of):
         return [(i, j) for i, j in enumerate(of) if 0 <= j < lat_size]
 
-    to_near, to_far = call(
+    operands = (
+        starts, wet_cells, coarse_old, coupling, mean_depth.reshape(1, layers), jnp.asarray(coarse_order, bf16)
+    )
+    to_near, to_far, coarse_old, coupling_kept, mean_depths, order = call(
         pack_kernel,
-        [array(planes, 8, width)] * 2,
-        [hbm] * 2,
+        [array(3 * NEAR + 4, 8, width), array(3 * HALO + 2, 8, width)]
+        + [jax.ShapeDtypeStruct(x.shape, x.dtype) for x in operands[2:]],
+        [hbm] * 6,
         [
             buffer(*starts.shape),
             pltpu.VMEM((rows, width), jnp.int32),
             buffer(rows, width),
-            pltpu.SemaphoreType.DMA((4,)),
+            pltpu.SemaphoreType.DMA((8,)),
         ],
-    )(*[pltpu.with_memory_space_constraint(x, pltpu.HBM) for x in (starts, wet_cells)])
+    )(*[pltpu.with_memory_space_constraint(x, pltpu.HBM) for x in operands])
     far = lax.ppermute(to_far, "lat", neighbours(far_of))
     near = lax.ppermute(to_near, "lat", neighbours(near_of))
-    mean_depths = mean_depth.reshape(1, layers)
 
     def stage_scratch(count):
         return [buffer(3, count, 8, width)] * 3 + [buffer(count, 8, width)] * 2 + [
@@ -578,21 +642,22 @@
             *[pltpu.VMEM((n * 8, 3 * n * 8), bf16) for n in (GROUP, CHUNK)],
         ]
 
-    early_rows, strips, coarse_before, first, coarse_wet = call(
+    early_rows, strips, coarse_before, first, outcome, coarse_wet = call(
         near_kernel,
-        [array(3, rows - HALO, 8, width), array(HALO, 3, 3, 8, width)]
-        + [array(3, coarse_rows, 8, half)] * 2
-        + [array(coarse_rows, 8, half)],
+        [array(3, rows - HALO + 2, 8, width), array(HALO, 3, 3, 8, width)]
+        + [array(3, coarse_rows + n, 8, half) for n in (1, 2, 0)]
+        + [array(coarse_rows + 2, 8, half)],
         [vmem] * 7,
-        stage_scratch(HALO + rows),
-    )(near, to_near, to_far, coarse_old, mean_depths, coupling, jnp.asarray(coarse_order, bf16))
-
-    late_rows, delta, outcome, passed = call(
+        stage_scratch(NEAR + rows),
+    )(near, to_near, to_far, coarse_old, mean_depths, coupling_kept, order)
+
+    late_rows, delta, last_outcome, passed = call(
         far_kernel,
-        [array(3, HALO, 8, width)] + [array(3, coarse_rows, 8, half)] * 3,
+        [array(3, HALO, 8, width), array(3, coarse_rows + 1, 8, half), array(3, 8, half)]
+        + [array(3, coarse_rows + 1, 8, half)],
         [vmem] * 10,
-        stage_scratch(2 * HALO + 1) + [buffer(3, coarse_rows + 2, 8, half)],
-    )(far, to_far, near, strips, early_rows, first, coarse_before, coarse_wet, mean_depths, coupling)
+        stage_scratch(2 * HALO + 1) + [buffer(3, coarse_rows, 8, half)],
+    )(far, to_far, strips, early_rows, first, outcome, coarse_before, coarse_wet, mean_depths, coupling_kept)
 
     both = ("tm", "lat")
 
@@ -606,17 +671,23 @@
             ]
             return lax.ppermute(values, both, pairs)
 
-        return moved(current, range(lat_size)), moved(current[:, 0], near_of), moved(current[:, -1], far_of)
-
-    previous = outcome
+        main, far_edge = moved(current, range(lat_size)), moved(current[:, -1], far_of)
+        if current.shape[1] > coarse_rows:
+            return main, far_edge
+        near_edge = moved(current[:, 0], near_of) * jnp.asarray([1.0, 1.0, -1.0], f32)[:, None, None]
+        near_edge = near_edge.at[0].add((1.0 - Place(rows).near_inside) * mean_depth[:, None])
+        return jnp.concatenate([near_edge[:, None], main], axis=1), far_edge
+
+    previous, last_previous = outcome, last_outcome
     incoming = hand_on(passed)
     (natural,) = call(natural_kernel, [array(*starts.shape)], [vmem] * 4)(
         early_rows, late_rows, mean_depths, jnp.asarray(fine_order.T, bf16)
     )
     for turn in range(1, tm_size - 1):
-        outcome = middle_turn(*incoming, coarse_wet, mean_depth, coupling, Place(rows))
-        previous = jnp.where(tm == turn, outcome, previous)
-        incoming = hand_on(delta + outcome)
+        result = middle_turn(*incoming, coarse_wet[2:], mean_depth, coupling, Place(rows))
+        previous = jnp.where(tm == turn, jnp.concatenate([previous[:, :1], result[:, :-1]], axis=1), previous)
+        last_previous = jnp.where(tm == turn, result[:, -1], last_previous)
+        incoming = hand_on(delta[:, 1:] + result)
 
     new_ends, coarse_new = call(
         final_kernel,
@@ -624,9 +695,11 @@
         [vmem] * 11,
         [buffer(3, coarse_rows + 2, 8, half)]
         + [buffer(coarse_rows + 2, 8, half)] * 2
-        + [buffer(3, coarse_rows, 8, half)],
+        + [buffer(3, coarse_rows, 8, half), buffer(*starts.shape), buffer(*coarse_old.shape)]
+        + [pltpu.SemaphoreType.DMA((6,))],
+        [hbm, hbm],
     )(
-        *incoming, previous, coarse_wet, coarse_before, mean_depths, coupling, natural,
+        *incoming, previous, last_previous, coarse_wet, coarse_before, mean_depths, coupling_kept, natural,
         jnp.asarray(coarse_order.T, bf16), jnp.asarray(prolong_matrix(width), bf16),
     )
     return (

time: 41.1 us -> 39.5 us (0.961)
  the two profiles are of different devices: /device:TPU:1 before, /device:TPU:3 now
where the time goes in v3:
time: 39.5 us; the launch traced here: 39.3 us
  Pallas kernels  22 us (56%)
  waiting for transfers between devices  10.2 us (26%)
  starting transfers between devices  6.49 us (16%)
  between operations  0.71 us (2%)
    pallas_call x1, Pallas kernels, local(): call(near_kernel, [array(3, rows - HALO + 2, 8, width), array(HALO, 3, 3,...  9.7 us
    pallas_call x1, Pallas kernels, local(): call(far_kernel, [array(3, HALO, 8, width), array(3, coarse_rows + 1, 8,...  6.62 us
    ppermute x2, waiting for transfers between devices, moved(): return lax.ppermute(values, both, pairs)  6.05 us
    ppermute x1, waiting for transfers between devices, local(): far = lax.ppermute(to_far, 'lat', neighbours(far_of))  4.11 us
    ppermute x1, starting transfers between devices, local(): far = lax.ppermute(to_far, 'lat', neighbours(far_of))  3.05 us
    ppermute x2, starting transfers between devices, moved(): return lax.ppermute(values, both, pairs)  2.7 us
    pallas_call x1, Pallas kernels, local(): call(pack_kernel, [array(3 * NEAR + 4, 8, width), array(3 * HALO + 2, 8,...  2.64 us
    pallas_call x1, Pallas kernels, local(): call(final_kernel, [array(*starts.shape), array(*coarse_old.shape)], [vme...  1.95 us
  transfers between devices with their start and end apart: 4, of which 2 were waited for; matrix products, arithmetic and copies ran while one was open for 0% of the time, Pallas kernels for 27%

profile of v3, /device:TPU:3, one launch (start us, length us, event | category | flops | bytes accessed | tf_op | source)
XLA Modules:
  0.0 39.3 jit_solution(4219652733173818163)
XLA Ops:
  0.6 2.6 %shard_map.104 = (f32[46,8,512]{2,1,0:T(8,128)S(1)}, f32[38,8,512]{2,1,0:T(8,128)S(1)}, f32[3,128,128]{2,1,0:T(8,128)S(1)}, f32[8,8]{1,0:T(8,128)S(1)}, f32[1,8]...) custom-call(f32[3,512,128]{2,1,0:T(8,128)} %bitcast.23, s32[16,512]{1,0:T(8,128)} %wet_hbm.1, f32[3,128,128]{2,1,0:T(8,128)} %bitcast.24, ...), custom_call_target="tpu_custom_call" | custom-call | tf_op jit(solution)/shard_map/pallas_call | solution.py:624
  3.3 0.7 %collective-permute-start.1 = (f32[46,8,512]{2,1,0:T(8,128)S(1)}, f32[46,8,512]{2,1,0:T(8,128)S(1)}, u32[]{:S(2)}, u32[]{:S(2)}) collective-permute-start(f32[46,8,512]{2,1,0:T(8,128)S(1)} %get-tuple-element.20.to_near), channel_id=1, source_target_pairs={{0,1},{1,0},{2,3},{3,2},{4,5},{5,4},{6,7},{7,6},{8,9},{9,8},{10,11... | collective-permute-start | bytes 2261000 | tf_op jit(solution)/shard_map/ppermute | solution.py:637
  4.0 3.0 %collective-permute-start = (f32[38,8,512]{2,1,0:T(8,128)S(1)}, f32[38,8,512]{2,1,0:T(8,128)S(1)}, u32[]{:S(2)}, u32[]{:S(2)}) collective-permute-start(f32[38,8,512]{2,1,0:T(8,128)S(1)} %get-tuple-element.19.to_far), channel_id=1, source_target_pairs={{1,2},{2,1},{3,4},{4,3},{5,6},{6,5},{7,8},{8,7},{9,10},{10,9},{11,... | collective-permute-start | bytes 1867784 | tf_op jit(solution)/shard_map/ppermute | solution.py:636
  7.1 0.0 collective-permute-done.1.near
  7.1 9.7 %shard_map.105 = (f32[3,6,8,512]{3,2,1,0:T(8,128)S(1)}, f32[12,3,3,8,512]{4,3,2,1,0:T(8,128)S(1)}, f32[3,9,8,256]{3,2,1,0:T(8,128)S(1)}, f32[3,10,8,256]{3,2,1,0...) custom-call(f32[46,8,512]{2,1,0:T(8,128)S(1)} %collective-permute-done.1.near, ...), custom_call_target="tpu_custom_call" | custom-call | tf_op jit(solution)/shard_map/pallas_call | solution.py:645
  16.8 4.1 %collective-permute-done.far = f32[38,8,512]{2,1,0:T(8,128)S(1)} collective-permute-done((f32[38,8,512]{2,1,0:T(8,128)S(1)}, f32[38,8,512]{2,1,0:T(8,128)S(1)}, u32[]{:S(2)}, u32[]{:S(2)}) %collective-permute-start) | collective-permute-done | bytes 622624 | tf_op jit(solution)/shard_map/ppermute | solution.py:636
  20.9 0.0 copy-start
  20.9 6.6 %shard_map.106 = (f32[3,12,8,512]{3,2,1,0:T(8,128)S(1)}, f32[3,9,8,256]{3,2,1,0:T(8,128)}, f32[3,8,256]{2,1,0:T(8,128)S(1)}, f32[3,9,8,256]{3,2,1,0:T(8,128)S(1)}) custom-call(f32[38,8,512]{2,1,0:T(8,128)S(1)} %collective-permute-done.far, f32[38,8,512]{2,1,0:T(8,128)S(1)} %get-tuple-element.19.to_far, f32[12,3,3,8,512]{4,3,2,1,0:T(8,128)S(1)} %get-tuple-element.25.strips, ...), custom_call_target="tpu_custom_call" | custom-call | tf_op jit(solution)/shard_map/pallas_call | solution.py:654
  27.5 0.0 copy-start.1
  27.5 0.0 copy-start.2
  27.5 1.4 %collective-permute-start.2 = (f32[3,9,8,256]{3,2,1,0:T(8,128)S(1)}, f32[3,9,8,256]{3,2,1,0:T(8,128)S(1)}, u32[]{:S(2)}, u32[]{:S(2)}) collective-permute-start(f32[3,9,8,256]{3,2,1,0:T(8,128)S(1)} %get-tuple-element.31), channel_id=1, source_target_pairs={{0,16},{1,17},{2,18},{3,19},{4,20},{5,21},{6,22},{7,23},{8,24},{9,... | collective-permute-start | bytes 663560 | tf_op jit(solution)/shard_map/ppermute | solution.py:672
  29.0 1.3 %collective-permute-start.3 = (f32[3,8,256]{2,1,0:T(8,128)S(1)}, f32[3,8,256]{2,1,0:T(8,128)S(1)}, u32[]{:S(2)}, u32[]{:S(2)}) collective-permute-start(f32[3,8,256]{2,1,0:T(8,128)S(1)} %slice_bitcast_fusion), channel_id=1, source_target_pairs={{1,18},{2,17},{3,20},{4,19},{5,22},{6,21},{7,24},{8,23},{9,26},{10... | collective-permute-start | bytes 73736 | tf_op jit(solution)/shard_map/ppermute | solution.py:672
  30.3 0.0 copy-done
  30.3 1.0 %shard_map.107.natural = f32[3,512,128]{2,1,0:T(8,128)S(1)} custom-call(f32[3,6,8,512]{3,2,1,0:T(8,128)S(1)} %get-tuple-element.26.early_rows, f32[3,12,8,512]{3,2,1,0:T(8,128)S(1)} %get-tuple-element.33.late_rows, f32[1,8]{1,0:T(1,128)S(1)} %get-tuple-element.22.mean_depth, bf16[512,512]{1,0:T(8,128)(2,1)S(1)} %copy-done), custom_call_target="tpu_custom_call" | custom-call | tf_op jit(solution)/shard_map/pallas_call | solution.py:683
  31.3 6.0 %collective-permute-done.3.far_edge = f32[3,8,256]{2,1,0:T(8,128)S(1)} collective-permute-done((f32[3,8,256]{2,1,0:T(8,128)S(1)}, f32[3,8,256]{2,1,0:T(8,128)S(1)}, u32[]{:S(2)}, u32[]{:S(2)}) %collective-permute-start.3) | collective-permute-done | bytes 24608 | tf_op jit(solution)/shard_map/ppermute | solution.py:672
  37.4 0.0 collective-permute-done.2.incoming
  37.4 0.0 copy-done.1
  37.4 0.0 copy-done.2
  37.4 2.0 %shard_map.108 = (f32[3,512,128]{2,1,0:T(8,128)}, f32[3,128,128]{2,1,0:T(8,128)}) custom-call(f32[3,9,8,256]{3,2,1,0:T(8,128)S(1)} %collective-permute-done.2.incoming, f32[3,8,256]{2,1,0:T(8,128)S(1)} %collective-permute-done.3.far_edge, f32[3,8,8,256]{3,2,1,0:T(8,128)S(1)} %get-tuple-element.28.outcome.previous, ...), custom_call_target="tpu_custom_call" | custom-call | tf_op jit(solution)/shard_map/pallas_call | solution.py:692
  (1 shorter events, 0.0 us)
Async XLA Ops:
  3.3 3.8 %collective-permute-start.1 = (f32[46,8,512]{2,1,0:T(8,128)S(1)}, f32[46,8,512]{2,1,0:T(8,128)S(1)}, u32[]{:S(2)}, u32[]{:S(2)}) collective-permute-start(f32[46,8,512]{2,1,0:T(8,128)S(1)} %get-tuple-element.20.to_near), channel_id=1, source_target_pairs={{0,1},{1,0},{2,3},{3,2},{4,5},{5,4},{6,7},{7,6},{8,9},{9,8},{10,11... | collective-permute-start | bytes 2261000 | tf_op jit(solution)/shard_map/ppermute | solution.py:637
  4.0 16.9 %collective-permute-start = (f32[38,8,512]{2,1,0:T(8,128)S(1)}, f32[38,8,512]{2,1,0:T(8,128)S(1)}, u32[]{:S(2)}, u32[]{:S(2)}) collective-permute-start(f32[38,8,512]{2,1,0:T(8,128)S(1)} %get-tuple-element.19.to_far), channel_id=1, source_target_pairs={{1,2},{2,1},{3,4},{4,3},{5,6},{6,5},{7,8},{8,7},{9,10},{10,9},{11,... | collective-permute-start | bytes 1867784 | tf_op jit(solution)/shard_map/ppermute | solution.py:636
  20.9 9.4 %copy-start = (bf16[512,512]{1,0:T(8,128)(2,1)S(1)}, bf16[512,512]{1,0:T(8,128)(2,1)}, u32[]{:S(2)}) copy-start(bf16[512,512]{1,0:T(8,128)(2,1)} %constant.9.clone.matrix) | copy-start | bytes 1572868
  27.5 9.8 %copy-start.1 = (bf16[256,512]{1,0:T(8,128)(2,1)S(1)}, bf16[256,512]{1,0:T(8,128)(2,1)}, u32[]{:S(2)}) copy-start(bf16[256,512]{1,0:T(8,128)(2,1)} %constant.11.clone.spread) | copy-start | bytes 786436
  27.5 9.8 %copy-start.2 = (bf16[256,256]{1,0:T(8,128)(2,1)S(1)}, bf16[256,256]{1,0:T(8,128)(2,1)}, u32[]{:S(2)}) copy-start(bf16[256,256]{1,0:T(8,128)(2,1)} %constant.10.clone.order) | copy-start | bytes 393220
  27.5 9.8 %collective-permute-start.2 = (f32[3,9,8,256]{3,2,1,0:T(8,128)S(1)}, f32[3,9,8,256]{3,2,1,0:T(8,128)S(1)}, u32[]{:S(2)}, u32[]{:S(2)}) collective-permute-start(f32[3,9,8,256]{3,2,1,0:T(8,128)S(1)} %get-tuple-element.31), channel_id=1, source_target_pairs={{0,16},{1,17},{2,18},{3,19},{4,20},{5,21},{6,22},{7,23},{8,24},{9,... | collective-permute-start | bytes 663560 | tf_op jit(solution)/shard_map/ppermute | solution.py:672
  29.0 8.4 %collective-permute-start.3 = (f32[3,8,256]{2,1,0:T(8,128)S(1)}, f32[3,8,256]{2,1,0:T(8,128)S(1)}, u32[]{:S(2)}, u32[]{:S(2)}) collective-permute-start(f32[3,8,256]{2,1,0:T(8,128)S(1)} %slice_bitcast_fusion), channel_id=1, source_target_pairs={{1,18},{2,17},{3,20},{4,19},{5,22},{6,21},{7,24},{8,23},{9,26},{10... | collective-permute-start | bytes 73736 | tf_op jit(solution)/shard_map/ppermute | solution.py:672

commit v4 on v3

--- a/solution.py
+++ b/solution.py
@@ -268,40 +268,69 @@
     return -x if field == 2 else x
 
 
-def pack_kernel(
-    rows, starts_hbm, wet_hbm, coarse_hbm, coupling_hbm, depth_hbm, order_hbm,
-    to_near, to_far, coarse_old, coupling, mean_depth, coarse_order,
-    starts, wet_cells, wet, semaphores,
-):
+def order_of(width):
+    blocks = width // LANES
+    column = lax.broadcasted_iota(jnp.int32, (width, LANES), 0)
+    column = column - blocks * lax.broadcasted_iota(jnp.int32, (width, LANES), 1)
+    return jnp.concatenate([jnp.where(column == c, 1.0, 0.0).astype(bf16) for c in range(blocks)], axis=1)
+
+
+def packed_rows(place, starts, order, rows, width, chosen):
+    state = [
+        load_row(starts, field, rows, width, place.own_row(rows, i)) * (place.sign if field == 2 else 1.0)
+        for field in range(3)
+        for i in chosen
+    ]
+    count = 8 * len(state)
+    terms = jnp.concatenate(split(jnp.concatenate(state, axis=0), 2), axis=0)
+    for c in range(0, width, 2 * LANES):
+        value = dot(terms, order[:, c : c + 2 * LANES])
+        yield c, (value[:count] + value[count:]).reshape(3, len(chosen), 8, 2 * LANES)
+
+
+def pack_wet(place, packed, wet, rows, first, count):
+    for plane, skip in ((0, 0), (1, count - 8)):
+        for i in range(8):
+            row = place.own_row(rows, first + skip + i)
+            packed[3 * count + plane, pl.ds(i, 1), :] = wet[pl.ds(row, 1), :]
+
+
+def pack_far_kernel(rows, starts_hbm, wet_hbm, to_far, starts, order, wet, wet_cells, semaphores):
     width = wet_cells.shape[-1]
-    blocks = width // LANES
     pairs = [(starts_hbm.at[field], starts.at[field]) for field in range(3)] + [(wet_hbm, wet_cells)]
-    pairs += [(coarse_hbm, coarse_old), (coupling_hbm, coupling), (depth_hbm, mean_depth), (order_hbm, coarse_order)]
     copies = [pltpu.make_async_copy(source, target, semaphores.at[n]) for n, (source, target) in enumerate(pairs)]
     for copy in copies:
         copy.start()
     place = Place(rows)
-    column = lax.broadcasted_iota(jnp.int32, (width, LANES), 0)
-    column = column - blocks * lax.broadcasted_iota(jnp.int32, (width, LANES), 1)
-    order = jnp.concatenate([jnp.where(column == c, 1.0, 0.0).astype(bf16) for c in range(blocks)], axis=1)
-    sent = ((to_near, 0, NEAR), (to_far, rows - HALO, HALO))
-    for field in range(3):
-        copies[field].wait()
-        state = [load_row(starts, field, rows, width, place.own_row(rows, i)) for i in range(rows)]
-        state = jnp.concatenate(state, axis=0)
-        for c, value in select_blocks(state * place.sign if field == 2 else state, order, 2):
-            value = value.reshape(rows, 8, value.shape[1])
-            for packed, first, count in sent:
-                packed[field * count : (field + 1) * count, :, c : c + value.shape[2]] = value[first : first + count]
-    copies[3].wait()
-    wet[...] = dot(wet_cells[...].astype(f32).astype(bf16), order)
-    for packed, first, count in sent:
-        for plane, skip in ((0, 0), (1, count - 8)):
-            if plane == 0 or count > 8:
-                for i in range(min(8, count)):
-                    row = place.own_row(rows, first + skip + i)
-                    packed[3 * count + plane, pl.ds(i, 1), :] = wet[pl.ds(row, 1), :]
-    for copy in copies[4:]:
+    order[...] = order_of(width)
+    for copy in copies:
+        copy.wait()
+    for c, value in packed_rows(place, starts, order, rows, width, range(rows - HALO, rows)):
+        for field in range(3):
+            to_far[field * HALO : (field + 1) * HALO, :, c : c + value.shape[3]] = value[field]
+    wet[...] = dot(wet_cells[...].astype(f32).astype(bf16), order[...])
+    pack_wet(place, to_far, wet, rows, rows - HALO, HALO)
+
+
+def pack_near_kernel(
+    rows, starts, order, wet, to_far, coarse_hbm, coupling_hbm, depth_hbm, order_hbm,
+    to_near, coarse_old, coupling, mean_depth, coarse_order,
+    semaphores,
+):
+    width = wet.shape[-1]
+    pairs = [(coarse_hbm, coarse_old), (coupling_hbm, coupling), (depth_hbm, mean_depth), (order_hbm, coarse_order)]
+    copies = [pltpu.make_async_copy(source, target, semaphores.at[n]) for n, (source, target) in enumerate(pairs)]
+    for copy in copies:
+        copy.start()
+    place = Place(rows)
+    early = rows - HALO
+    for c, value in packed_rows(place, starts, order, rows, width, range(early)):
+        for field in range(3):
+            to_near[field * NEAR : field * NEAR + early, :, c : c + value.shape[3]] = value[field]
+    for field in range(3):
+        to_near[field * NEAR + early : (field + 1) * NEAR] = to_far[field * HALO : field * HALO + NEAR - early]
+    pack_wet(place, to_near, wet, rows, 0, NEAR)
+    for copy in copies:
         copy.wait()
     half = width // 2
     old = [load_row(coarse_old, field, rows // 2, half, place.own_row(rows // 2, 0)) for field in range(3)]
@@ -315,14 +344,15 @@
 
 def near_kernel(
     rows, near, to_near, to_far, coarse_old, mean_depth, coupling, matrix,
-    early_rows, strips, coarse_before, first, outcome, coarse_wet,
-    y, a, b, hv, press, wet, short_parts, long_parts,
+    early_rows, strips, coarse_before, first, outcome, coarse_wet, short_parts, long_parts, depths,
+    y, a, b, hv, press, wet,
 ):
     width = y.shape[-1]
     half = width // 2
     coarse_rows = rows // 2
     place = Place(rows)
     depth = depth_of(mean_depth, width)
+    depths[...] = depth
     kron_parts = {}
     for count, parts in ((GROUP, short_parts), (CHUNK, long_parts)):
         parts[...] = coupling_parts(coupling[...], count)
@@ -403,20 +433,18 @@
 
 
 def far_kernel(
-    rows, far, to_far, strips, early_rows, first, outcome, coarse_before, coarse_wet, mean_depth, coupling,
+    rows, far, to_far, strips, early_rows, first, outcome, coarse_before, coarse_wet, short_parts, long_parts,
+    depths,
     late_rows, delta, last_outcome, passed,
-    y, a, b, hv, press, wet, short_parts, long_parts, state,
+    y, a, b, hv, press, wet, state,
 ):
     width = y.shape[-1]
     origin = rows - HALO - 1
     own = rows - origin
     coarse_rows = rows // 2
     place = Place(rows)
-    depth = depth_of(mean_depth, width)
-    kron_parts = {}
-    for count, parts in ((GROUP, short_parts), (CHUNK, long_parts)):
-        parts[...] = coupling_parts(coupling[...], count)
-        kron_parts[count] = parts
+    depth = depths[...]
+    kron_parts = {GROUP: short_parts, CHUNK: long_parts}
     for field in range(3):
         for i in range(HALO):
             value = turned(far[(field + 1) * HALO - 1 - i], field)
@@ -474,10 +502,10 @@
             passed[field, i + 1] = difference + before
 
 
-def natural_kernel(rows, early_rows, late_rows, mean_depth, matrix, natural):
+def natural_kernel(rows, early_rows, late_rows, depths, matrix, natural):
     width = late_rows.shape[-1]
     place = Place(rows)
-    depth = depth_of(mean_depth, width)
+    depth = depths[...]
     for field in range(3):
         value = jnp.concatenate([part[field] for part in (early_rows.at[:, 2:], late_rows)], axis=0)
         if field == 0:
@@ -493,7 +521,7 @@
 
 
 def final_kernel(
-    rows, incoming, far_edge, previous, last_previous, coarse_wet, coarse_before, mean_depth, coupling, natural, order,
+    rows, incoming, far_edge, previous, last_previous, coarse_wet, coarse_before, depths, long_parts, natural, order,
     spread,
     new_ends, coarse_new,
     state, hv, press, result, ends, coarse, semaphores,
@@ -502,12 +530,12 @@
     half = incoming.shape[-1]
     width = 2 * half
     place = Place(rows)
-    depth = depth_of(mean_depth, half)
+    depth = depths[:, :half]
     for field in range(3):
         state[field, : coarse_rows + 1] = incoming[field]
         state[field, coarse_rows + 1] = turned(far_edge[field], field)
     state[0, coarse_rows + 1] += (1.0 - place.far_inside) * depth
-    kron_parts = {CHUNK: coupling_parts(coupling[...], CHUNK)}
+    kron_parts = {CHUNK: long_parts}
 
     def emit(i, values):
         for field in range(3):
@@ -618,35 +646,40 @@
     def neighbours(of):
         return [(i, j) for i, j in enumerate(of) if 0 <= j < lat_size]
 
-    operands = (
-        starts, wet_cells, coarse_old, coupling, mean_depth.reshape(1, layers), jnp.asarray(coarse_order, bf16)
-    )
-    to_near, to_far, coarse_old, coupling_kept, mean_depths, order = call(
-        pack_kernel,
-        [array(3 * NEAR + 4, 8, width), array(3 * HALO + 2, 8, width)]
-        + [jax.ShapeDtypeStruct(x.shape, x.dtype) for x in operands[2:]],
-        [hbm] * 6,
+    def in_hbm(*operands):
+        return [pltpu.with_memory_space_constraint(x, pltpu.HBM) for x in operands]
+
+    to_far, starts_kept, fine_matrix, wet = call(
+        pack_far_kernel,
         [
-            buffer(*starts.shape),
-            pltpu.VMEM((rows, width), jnp.int32),
-            buffer(rows, width),
-            pltpu.SemaphoreType.DMA((8,)),
+            array(3 * HALO + 2, 8, width),
+            array(*starts.shape),
+            jax.ShapeDtypeStruct((width, width), bf16),
+            array(rows, width),
         ],
-    )(*[pltpu.with_memory_space_constraint(x, pltpu.HBM) for x in operands])
+        [hbm] * 2,
+        [pltpu.VMEM((rows, width), jnp.int32), pltpu.SemaphoreType.DMA((4,))],
+    )(*in_hbm(starts, wet_cells))
+    operands = (coarse_old, coupling, mean_depth.reshape(1, layers), jnp.asarray(coarse_order, bf16))
     far = lax.ppermute(to_far, "lat", neighbours(far_of))
+    to_near, coarse_old, coupling_kept, mean_depths, order = call(
+        pack_near_kernel,
+        [array(3 * NEAR + 4, 8, width)] + [jax.ShapeDtypeStruct(x.shape, x.dtype) for x in operands],
+        [vmem] * 4 + [hbm] * 4,
+        [pltpu.SemaphoreType.DMA((4,))],
+    )(starts_kept, fine_matrix, wet, to_far, *in_hbm(*operands))
     near = lax.ppermute(to_near, "lat", neighbours(near_of))
 
     def stage_scratch(count):
-        return [buffer(3, count, 8, width)] * 3 + [buffer(count, 8, width)] * 2 + [
-            buffer(6, count, 8, width),
-            *[pltpu.VMEM((n * 8, 3 * n * 8), bf16) for n in (GROUP, CHUNK)],
-        ]
-
-    early_rows, strips, coarse_before, first, outcome, coarse_wet = call(
+        return [buffer(3, count, 8, width)] * 3 + [buffer(count, 8, width)] * 2 + [buffer(6, count, 8, width)]
+
+    early_rows, strips, coarse_before, first, outcome, coarse_wet, *shared = call(
         near_kernel,
         [array(3, rows - HALO + 2, 8, width), array(HALO, 3, 3, 8, width)]
         + [array(3, coarse_rows + n, 8, half) for n in (1, 2, 0)]
-        + [array(coarse_rows + 2, 8, half)],
+        + [array(coarse_rows + 2, 8, half)]
+        + [jax.ShapeDtypeStruct((n * 8, 3 * n * 8), bf16) for n in (GROUP, CHUNK)]
+        + [array(8, width)],
         [vmem] * 7,
         stage_scratch(NEAR + rows),
     )(near, to_near, to_far, coarse_old, mean_depths, coupling_kept, order)
@@ -655,9 +688,9 @@
         far_kernel,
         [array(3, HALO, 8, width), array(3, coarse_rows + 1, 8, half), array(3, 8, half)]
         + [array(3, coarse_rows + 1, 8, half)],
-        [vmem] * 10,
+        [vmem] * 11,
         stage_scratch(2 * HALO + 1) + [buffer(3, coarse_rows, 8, half)],
-    )(far, to_far, strips, early_rows, first, outcome, coarse_before, coarse_wet, mean_depths, coupling_kept)
+    )(far, to_far, strips, early_rows, first, outcome, coarse_before, coarse_wet, *shared)
 
     both = ("tm", "lat")
 
@@ -681,7 +714,7 @@
     previous, last_previous = outcome, last_outcome
     incoming = hand_on(passed)
     (natural,) = call(natural_kernel, [array(*starts.shape)], [vmem] * 4)(
-        early_rows, late_rows, mean_depths, jnp.asarray(fine_order.T, bf16)
+        early_rows, late_rows, shared[2], jnp.asarray(fine_order.T, bf16)
     )
     for turn in range(1, tm_size - 1):
         result = middle_turn(*incoming, coarse_wet[2:], mean_depth, coupling, Place(rows))
@@ -699,7 +732,7 @@
         + [pltpu.SemaphoreType.DMA((6,))],
         [hbm, hbm],
     )(
-        *incoming, previous, last_previous, coarse_wet, coarse_before, mean_depths, coupling_kept, natural,
+        *incoming, previous, last_previous, coarse_wet, coarse_before, shared[2], shared[1], natural,
         jnp.asarray(coarse_order.T, bf16), jnp.asarray(prolong_matrix(width), bf16),
     )
     return (

time: 39.5 us -> 40 us (1.013)
  the two profiles are of different devices: /device:TPU:3 before, /device:TPU:19 now
where the time goes in v4:
time: 40 us; the launch traced here: 39.8 us
  Pallas kernels  22.4 us (56%)
  waiting for transfers between devices  10.2 us (25%)
  starting transfers between devices  6.49 us (16%)
  between operations  0.72 us (2%)
    pallas_call x1, Pallas kernels, local(): call(near_kernel, [array(3, rows - HALO + 2, 8, width), array(HALO, 3, 3,...  9.76 us
    pallas_call x1, Pallas kernels, local(): call(far_kernel, [array(3, HALO, 8, width), array(3, coarse_rows + 1, 8,...  6.52 us
    ppermute x1, waiting for transfers between devices, local(): far = lax.ppermute(to_far, 'lat', neighbours(far_of))  5.38 us
    ppermute x2, waiting for transfers between devices, moved(): return lax.ppermute(values, both, pairs)  4.81 us
    ppermute x1, starting transfers between devices, local(): far = lax.ppermute(to_far, 'lat', neighbours(far_of))  3.05 us
    ppermute x2, starting transfers between devices, moved(): return lax.ppermute(values, both, pairs)  2.7 us
    pallas_call x1, Pallas kernels, local(): call(final_kernel, [array(*starts.shape), array(*coarse_old.shape)], [vme...  1.9 us
    pallas_call x1, Pallas kernels, local(): call(pack_far_kernel, [array(3 * HALO + 2, 8, width), array(*starts.shape...  1.85 us
  transfers between devices with their start and end apart: 4, of which 2 were waited for; matrix products, arithmetic and copies ran while one was open for 0% of the time, Pallas kernels for 27%

profile of v4, /device:TPU:19, one launch (start us, length us, event | category | flops | bytes accessed | tf_op | source)
XLA Modules:
  0.0 39.8 jit_solution(513737137264044086)
XLA Ops:
  0.6 1.8 %shard_map.104 = (f32[38,8,512]{2,1,0:T(8,128)S(1)}, f32[3,512,128]{2,1,0:T(8,128)S(1)}, bf16[512,512]{1,0:T(8,128)(2,1)S(1)}, f32[16,512]{1,0:T(8,128)S(1)}) custom-call(f32[3,512,128]{2,1,0:T(8,128)} %bitcast.23, s32[16,512]{1,0:T(8,128)} %wet_hbm.1), custom_call_target="tpu_custom_call" | custom-call | tf_op jit(solution)/shard_map/pallas_call | solution.py:652
  2.5 1.4 %shard_map.105 = (f32[46,8,512]{2,1,0:T(8,128)S(1)}, f32[3,128,128]{2,1,0:T(8,128)S(1)}, f32[8,8]{1,0:T(8,128)S(1)}, f32[1,8]{1,0:T(1,128)S(1)}, bf16[256,256]{1,0:T(8,128)(2,1)S(1)}) custom-call(f32[3,512,128]{2,1,0:T(8,128)S(1)} %get-tuple-element.26.starts, bf16[512,512]{1,0:T(8,128)(2,1)S(1)} %get-tuple-element.27.order, ...), custom_call_target="tpu_custom_call" | custom-call | tf_op jit(solution)/shard_map/pallas_call | solution.py:665
  3.9 0.7 %collective-permute-start.1 = (f32[46,8,512]{2,1,0:T(8,128)S(1)}, f32[46,8,512]{2,1,0:T(8,128)S(1)}, u32[]{:S(2)}, u32[]{:S(2)}) collective-permute-start(f32[46,8,512]{2,1,0:T(8,128)S(1)} %get-tuple-element.29.to_near), channel_id=1, source_target_pairs={{0,1},{1,0},{2,3},{3,2},{4,5},{5,4},{6,7},{7,6},{8,9},{9,8},{10,11... | collective-permute-start | bytes 2261000 | tf_op jit(solution)/shard_map/ppermute | solution.py:671
  4.6 3.0 %collective-permute-start = (f32[38,8,512]{2,1,0:T(8,128)S(1)}, f32[38,8,512]{2,1,0:T(8,128)S(1)}, u32[]{:S(2)}, u32[]{:S(2)}) collective-permute-start(f32[38,8,512]{2,1,0:T(8,128)S(1)} %get-tuple-element.25.to_far), channel_id=1, source_target_pairs={{1,2},{2,1},{3,4},{4,3},{5,6},{6,5},{7,8},{8,7},{9,10},{10,9},{11,... | collective-permute-start | bytes 1867784 | tf_op jit(solution)/shard_map/ppermute | solution.py:664
  7.7 0.0 collective-permute-done.1.near
  7.7 9.8 %shard_map.106 = (f32[3,6,8,512]{3,2,1,0:T(8,128)S(1)}, f32[12,3,3,8,512]{4,3,2,1,0:T(8,128)S(1)}, f32[3,9,8,256]{3,2,1,0:T(8,128)S(1)}, f32[3,10,8,256]{3,2,1,0...) custom-call(f32[46,8,512]{2,1,0:T(8,128)S(1)} %collective-permute-do, ...), custom_call_target="tpu_custom_call" | custom-call | tf_op jit(solution)/shard_map/pallas_call | solution.py:676
  17.5 5.4 %collective-permute-done.far = f32[38,8,512]{2,1,0:T(8,128)S(1)} collective-permute-done((f32[38,8,512]{2,1,0:T(8,128)S(1)}, f32[38,8,512]{2,1,0:T(8,128)S(1)}, u32[]{:S(2)}, u32[]{:S(2)}) %collective-permute-start) | collective-permute-done | bytes 622624 | tf_op jit(solution)/shard_map/ppermute | solution.py:664
  22.9 0.0 copy-start
  22.9 6.5 %shard_map.107 = (f32[3,12,8,512]{3,2,1,0:T(8,128)S(1)}, f32[3,9,8,256]{3,2,1,0:T(8,128)}, f32[3,8,256]{2,1,0:T(8,128)S(1)}, f32[3,9,8,256]{3,2,1,0:T(8,128)S(1)}) custom-call(f32[38,8,512]{2,1,0:T(8,128)S(1)} %collective-permute-done.far, f32[38,8,512]{2,1,0:T(8,128)S(1)} %get-tuple-element.25.to_far, f32[12,3,3,8,512]{4,3,2,1,0:T(8,128)S(1)} %get-tuple-element.34.strips, ...), custom_call_target="tpu_custom_call" | custom-call | tf_op jit(solution)/shard_map/pallas_call | solution.py:687
  29.4 0.0 copy-start.1
  29.4 0.0 copy-start.2
  29.4 1.4 %collective-permute-start.2 = (f32[3,9,8,256]{3,2,1,0:T(8,128)S(1)}, f32[3,9,8,256]{3,2,1,0:T(8,128)S(1)}, u32[]{:S(2)}, u32[]{:S(2)}) collective-permute-start(f32[3,9,8,256]{3,2,1,0:T(8,128)S(1)} %get-tuple-element.43), channel_id=1, source_target_pairs={{0,16},{1,17},{2,18},{3,19},{4,20},{5,21},{6,22},{7,23},{8,24},{9,... | collective-permute-start | bytes 663560 | tf_op jit(solution)/shard_map/ppermute | solution.py:705
  30.8 1.3 %collective-permute-start.3 = (f32[3,8,256]{2,1,0:T(8,128)S(1)}, f32[3,8,256]{2,1,0:T(8,128)S(1)}, u32[]{:S(2)}, u32[]{:S(2)}) collective-permute-start(f32[3,8,256]{2,1,0:T(8,128)S(1)} %slice_bitcast_fusion), channel_id=1, source_target_pairs={{1,18},{2,17},{3,20},{4,19},{5,22},{6,21},{7,24},{8,23},{9,26},{10... | collective-permute-start | bytes 73736 | tf_op jit(solution)/shard_map/ppermute | solution.py:705
  32.1 0.0 copy-done
  32.1 1.0 %shard_map.108.natural = f32[3,512,128]{2,1,0:T(8,128)S(1)} custom-call(f32[3,6,8,512]{3,2,1,0:T(8,128)S(1)} %get-tuple-element.35.early_rows, f32[3,12,8,512]{3,2,1,0:T(8,128)S(1)} %get-tuple-element.45.late_rows, f32[8,512]{1,0:T(8,128)S(1)} %get-tuple-element.42.depths, bf16[512,512]{1,0:T(8,128)(2,1)S(1)} %copy-done), custom_call_target="tpu_custom_call" | custom-call | tf_op jit(solution)/shard_map/pallas_call | solution.py:716
  33.1 4.8 %collective-permute-done.3.far_edge = f32[3,8,256]{2,1,0:T(8,128)S(1)} collective-permute-done((f32[3,8,256]{2,1,0:T(8,128)S(1)}, f32[3,8,256]{2,1,0:T(8,128)S(1)}, u32[]{:S(2)}, u32[]{:S(2)}) %collective-permute-start.3) | collective-permute-done | bytes 24608 | tf_op jit(solution)/shard_map/ppermute | solution.py:705
  37.9 0.0 collective-permute-done.2.incoming
  37.9 0.0 copy-done.1
  37.9 0.0 copy-done.2
  37.9 1.9 %shard_map.109 = (f32[3,512,128]{2,1,0:T(8,128)}, f32[3,128,128]{2,1,0:T(8,128)}) custom-call(f32[3,9,8,256]{3,2,1,0:T(8,128)S(1)} %collective-permute-done.2.incoming, f32[3,8,256]{2,1,0:T(8,128)S(1)} %collective-permute-done.3.far_edge, f32[3,8,8,256]{3,2,1,0:T(8,128)S(1)} %get-tuple-element.37.outcome.previous, ...), custom_call_target="tpu_custom_call" | custom-call | tf_op jit(solution)/shard_map/pallas_call | solution.py:725
  (1 shorter events, 0.0 us)
Async XLA Ops:
  3.9 3.8 %collective-permute-start.1 = (f32[46,8,512]{2,1,0:T(8,128)S(1)}, f32[46,8,512]{2,1,0:T(8,128)S(1)}, u32[]{:S(2)}, u32[]{:S(2)}) collective-permute-start(f32[46,8,512]{2,1,0:T(8,128)S(1)} %get-tuple-element.29.to_near), channel_id=1, source_target_pairs={{0,1},{1,0},{2,3},{3,2},{4,5},{5,4},{6,7},{7,6},{8,9},{9,8},{10,11... | collective-permute-start | bytes 2261000 | tf_op jit(solution)/shard_map/ppermute | solution.py:671
  4.6 18.2 %collective-permute-start = (f32[38,8,512]{2,1,0:T(8,128)S(1)}, f32[38,8,512]{2,1,0:T(8,128)S(1)}, u32[]{:S(2)}, u32[]{:S(2)}) collective-permute-start(f32[38,8,512]{2,1,0:T(8,128)S(1)} %get-tuple-element.25.to_far), channel_id=1, source_target_pairs={{1,2},{2,1},{3,4},{4,3},{5,6},{6,5},{7,8},{8,7},{9,10},{10,9},{11,... | collective-permute-start | bytes 1867784 | tf_op jit(solution)/shard_map/ppermute | solution.py:664
  22.9 9.3 %copy-start = (bf16[512,512]{1,0:T(8,128)(2,1)S(1)}, bf16[512,512]{1,0:T(8,128)(2,1)}, u32[]{:S(2)}) copy-start(bf16[512,512]{1,0:T(8,128)(2,1)} %constant.9.clone.matrix) | copy-start | bytes 1572868
  29.4 8.5 %copy-start.1 = (bf16[256,512]{1,0:T(8,128)(2,1)S(1)}, bf16[256,512]{1,0:T(8,128)(2,1)}, u32[]{:S(2)}) copy-start(bf16[256,512]{1,0:T(8,128)(2,1)} %constant.11.clone.spread) | copy-start | bytes 786436
  29.4 8.5 %copy-start.2 = (bf16[256,256]{1,0:T(8,128)(2,1)S(1)}, bf16[256,256]{1,0:T(8,128)(2,1)}, u32[]{:S(2)}) copy-start(bf16[256,256]{1,0:T(8,128)(2,1)} %constant.10.clone.order) | copy-start | bytes 393220
  29.4 8.5 %collective-permute-start.2 = (f32[3,9,8,256]{3,2,1,0:T(8,128)S(1)}, f32[3,9,8,256]{3,2,1,0:T(8,128)S(1)}, u32[]{:S(2)}, u32[]{:S(2)}) collective-permute-start(f32[3,9,8,256]{3,2,1,0:T(8,128)S(1)} %get-tuple-element.43), channel_id=1, source_target_pairs={{0,16},{1,17},{2,18},{3,19},{4,20},{5,21},{6,22},{7,23},{8,24},{9,... | collective-permute-start | bytes 663560 | tf_op jit(solution)/shard_map/ppermute | solution.py:705
  30.8 7.1 %collective-permute-start.3 = (f32[3,8,256]{2,1,0:T(8,128)S(1)}, f32[3,8,256]{2,1,0:T(8,128)S(1)}, u32[]{:S(2)}, u32[]{:S(2)}) collective-permute-start(f32[3,8,256]{2,1,0:T(8,128)S(1)} %slice_bitcast_fusion), channel_id=1, source_target_pairs={{1,18},{2,17},{3,20},{4,19},{5,22},{6,21},{7,24},{8,23},{9,26},{10... | collective-permute-start | bytes 73736 | tf_op jit(solution)/shard_map/ppermute | solution.py:705

commit v5 on v4

--- a/solution.py
+++ b/solution.py
@@ -344,8 +344,8 @@
 
 def near_kernel(
     rows, near, to_near, to_far, coarse_old, mean_depth, coupling, matrix,
-    early_rows, strips, coarse_before, first, outcome, coarse_wet, short_parts, long_parts, depths,
-    y, a, b, hv, press, wet,
+    early_rows, strips, coarse_before, first, outcome, coarse_wet, short_parts, long_parts, depths, wet,
+    y, a, b, hv, press,
 ):
     width = y.shape[-1]
     half = width // 2
@@ -434,13 +434,14 @@
 
 def far_kernel(
     rows, far, to_far, strips, early_rows, first, outcome, coarse_before, coarse_wet, short_parts, long_parts,
-    depths,
-    late_rows, delta, last_outcome, passed,
-    y, a, b, hv, press, wet, state,
+    depths, near_wet,
+    late_rows, delta, last_outcome, passed, all_wet,
+    y, a, b, hv, press, state,
 ):
     width = y.shape[-1]
     origin = rows - HALO - 1
     own = rows - origin
+    wet = all_wet.at[:, pl.ds(NEAR + origin, 2 * HALO + 1)]
     coarse_rows = rows // 2
     place = Place(rows)
     depth = depths[...]
@@ -452,7 +453,6 @@
         state[field, : coarse_rows - 1] = first[field, 3:]
     for i in range(HALO):
         set_masks(wet, own + i, jnp.broadcast_to(wet_row(far, HALO, HALO - 1 - i), (8, width)))
-        set_masks(wet, own - HALO + i, jnp.broadcast_to(wet_row(to_far, HALO, i), (8, width)))
 
     for field in range(3):
         state[field, coarse_rows - 1] = restrict_pair(y[field, own], y[field, own + 1])
@@ -630,13 +630,14 @@
     def buffer(*shape):
         return pltpu.VMEM(shape, f32)
 
-    def call(kernel, outs, in_specs, scratch=(), out_specs=None):
+    def call(kernel, outs, in_specs, scratch=(), out_specs=None, aliases=None):
         return pl.pallas_call(
             functools.partial(kernel, rows),
             out_shape=outs,
             in_specs=in_specs,
             out_specs=out_specs or [vmem] * len(outs),
             scratch_shapes=list(scratch),
+            input_output_aliases=aliases or {},
             compiler_params=pltpu.CompilerParams(vmem_limit_bytes=16 * 2**20),
         )
 
@@ -671,7 +672,7 @@
     near = lax.ppermute(to_near, "lat", neighbours(near_of))
 
     def stage_scratch(count):
-        return [buffer(3, count, 8, width)] * 3 + [buffer(count, 8, width)] * 2 + [buffer(6, count, 8, width)]
+        return [buffer(3, count, 8, width)] * 3 + [buffer(count, 8, width)] * 2
 
     early_rows, strips, coarse_before, first, outcome, coarse_wet, *shared = call(
         near_kernel,
@@ -679,17 +680,18 @@
         + [array(3, coarse_rows + n, 8, half) for n in (1, 2, 0)]
         + [array(coarse_rows + 2, 8, half)]
         + [jax.ShapeDtypeStruct((n * 8, 3 * n * 8), bf16) for n in (GROUP, CHUNK)]
-        + [array(8, width)],
+        + [array(8, width), array(6, NEAR + rows + HALO, 8, width)],
         [vmem] * 7,
         stage_scratch(NEAR + rows),
     )(near, to_near, to_far, coarse_old, mean_depths, coupling_kept, order)
 
-    late_rows, delta, last_outcome, passed = call(
+    late_rows, delta, last_outcome, passed, _ = call(
         far_kernel,
         [array(3, HALO, 8, width), array(3, coarse_rows + 1, 8, half), array(3, 8, half)]
-        + [array(3, coarse_rows + 1, 8, half)],
-        [vmem] * 11,
+        + [array(3, coarse_rows + 1, 8, half), array(6, NEAR + rows + HALO, 8, width)],
+        [vmem] * 12,
         stage_scratch(2 * HALO + 1) + [buffer(3, coarse_rows, 8, half)],
+        aliases={11: 4},
     )(far, to_far, strips, early_rows, first, outcome, coarse_before, coarse_wet, *shared)
 
     both = ("tm", "lat")

time: 40 us -> 39.9 us (level)
  transfers between devices with their start and end apart: 4 -> 4, of which waited for: 2 -> 2; matrix products, arithmetic and copies ran while one was open for 0% -> 0% of each run, Pallas kernels for 27% -> 28%
where the time goes in v5:
time: 39.9 us; the launch traced here: 39.7 us
  Pallas kernels  22.7 us (57%)
  waiting for transfers between devices  9.96 us (25%)
  starting transfers between devices  6.36 us (16%)
  between operations  0.72 us (2%)
    pallas_call x1, Pallas kernels, local(): call(near_kernel, [array(3, rows - HALO + 2, 8, width), array(HALO, 3, 3,...  9.98 us
    pallas_call x1, Pallas kernels, local(): call(far_kernel, [array(3, HALO, 8, width), array(3, coarse_rows + 1, 8,...  6.61 us
    ppermute x1, waiting for transfers between devices, local(): far = lax.ppermute(to_far, 'lat', neighbours(far_of))  5.16 us
    ppermute x2, waiting for transfers between devices, moved(): return lax.ppermute(values, both, pairs)  4.8 us
    ppermute x1, starting transfers between devices, local(): far = lax.ppermute(to_far, 'lat', neighbours(far_of))  3.05 us
    ppermute x2, starting transfers between devices, moved(): return lax.ppermute(values, both, pairs)  2.57 us
    pallas_call x1, Pallas kernels, local(): call(final_kernel, [array(*starts.shape), array(*coarse_old.shape)], [vme...  1.9 us
    pallas_call x1, Pallas kernels, local(): call(pack_far_kernel, [array(3 * HALO + 2, 8, width), array(*starts.shape...  1.85 us
  transfers between devices with their start and end apart: 4, of which 2 were waited for; matrix products, arithmetic and copies ran while one was open for 0% of the time, Pallas kernels for 28%

profile of v5, /device:TPU:19, one launch (start us, length us, event | category | flops | bytes accessed | tf_op | source)
XLA Modules:
  0.0 39.7 jit_solution(2080468006280636476)
XLA Ops:
  0.6 1.8 %shard_map.104 = (f32[38,8,512]{2,1,0:T(8,128)S(1)}, f32[3,512,128]{2,1,0:T(8,128)S(1)}, bf16[512,512]{1,0:T(8,128)(2,1)S(1)}, f32[16,512]{1,0:T(8,128)S(1)}) custom-call(f32[3,512,128]{2,1,0:T(8,128)} %bitcast.23, s32[16,512]{1,0:T(8,128)} %wet_hbm.1), custom_call_target="tpu_custom_call" | custom-call | tf_op jit(solution)/shard_map/pallas_call | solution.py:653
  2.5 1.4 %shard_map.105 = (f32[46,8,512]{2,1,0:T(8,128)S(1)}, f32[3,128,128]{2,1,0:T(8,128)S(1)}, f32[8,8]{1,0:T(8,128)S(1)}, f32[1,8]{1,0:T(1,128)S(1)}, bf16[256,256]{1,0:T(8,128)(2,1)S(1)}) custom-call(f32[3,512,128]{2,1,0:T(8,128)S(1)} %get-tuple-element.27.starts, bf16[512,512]{1,0:T(8,128)(2,1)S(1)} %get-tuple-element.28.order, ...), custom_call_target="tpu_custom_call" | custom-call | tf_op jit(solution)/shard_map/pallas_call | solution.py:666
  3.9 0.7 %collective-permute-start.1 = (f32[46,8,512]{2,1,0:T(8,128)S(1)}, f32[46,8,512]{2,1,0:T(8,128)S(1)}, u32[]{:S(2)}, u32[]{:S(2)}) collective-permute-start(f32[46,8,512]{2,1,0:T(8,128)S(1)} %get-tuple-element.30.to_near), channel_id=1, source_target_pairs={{0,1},{1,0},{2,3},{3,2},{4,5},{5,4},{6,7},{7,6},{8,9},{9,8},{10,11... | collective-permute-start | bytes 2261000 | tf_op jit(solution)/shard_map/ppermute | solution.py:672
  4.6 3.0 %collective-permute-start = (f32[38,8,512]{2,1,0:T(8,128)S(1)}, f32[38,8,512]{2,1,0:T(8,128)S(1)}, u32[]{:S(2)}, u32[]{:S(2)}) collective-permute-start(f32[38,8,512]{2,1,0:T(8,128)S(1)} %get-tuple-element.26.to_far), channel_id=1, source_target_pairs={{1,2},{2,1},{3,4},{4,3},{5,6},{6,5},{7,8},{8,7},{9,10},{10,9},{11,... | collective-permute-start | bytes 1867784 | tf_op jit(solution)/shard_map/ppermute | solution.py:665
  7.7 0.0 collective-permute-done.1.near
  7.7 10.0 %shard_map.106 = (f32[3,6,8,512]{3,2,1,0:T(8,128)S(1)}, f32[12,3,3,8,512]{4,3,2,1,0:T(8,128)S(1)}, f32[3,9,8,256]{3,2,1,0:T(8,128)S(1)}, f32[3,10,8,256]{3,2,1,0...) custom-call(f32[46,8,512]{2,1,0:T(8,128)S(1)} %collective-permute-do, ...), custom_call_target="tpu_custom_call" | custom-call | tf_op jit(solution)/shard_map/pallas_call | solution.py:677
  17.7 5.2 %collective-permute-done.far = f32[38,8,512]{2,1,0:T(8,128)S(1)} collective-permute-done((f32[38,8,512]{2,1,0:T(8,128)S(1)}, f32[38,8,512]{2,1,0:T(8,128)S(1)}, u32[]{:S(2)}, u32[]{:S(2)}) %collective-permute-start) | collective-permute-done | bytes 622624 | tf_op jit(solution)/shard_map/ppermute | solution.py:665
  22.9 0.0 copy-start
  22.9 0.0 copy-start.1
  22.9 0.0 copy-start.2
  22.9 6.6 %shard_map.107 = (f32[3,12,8,512]{3,2,1,0:T(8,128)S(1)}, f32[3,9,8,256]{3,2,1,0:T(8,128)}, f32[3,8,256]{2,1,0:T(8,128)S(1)}, f32[3,9,8,256]{3,2,1,0:T(8,128)S(1)}, f32[6,42,8,512]{3,2,1,0:T(8,128)S(1)}) custom-call(f32[38,8,512]{2,1,0:T(8,128)S(1)} %collective-permute-done.far, ...), custom_call_target="tpu_custom_call", output_to_operand_aliasing={{4}: (11, {})} | custom-call | tf_op jit(solution)/shard_map/pallas_call | solution.py:688
  29.5 1.3 %collective-permute-start.2 = (f32[3,9,8,256]{3,2,1,0:T(8,128)S(1)}, f32[3,9,8,256]{3,2,1,0:T(8,128)S(1)}, u32[]{:S(2)}, u32[]{:S(2)}) collective-permute-start(f32[3,9,8,256]{3,2,1,0:T(8,128)S(1)} %get-tuple-element.45), channel_id=1, source_target_pairs={{0,16},{1,17},{2,18},{3,19},{4,20},{5,21},{6,22},{7,23},{8,24},{9,... | collective-permute-start | bytes 663560 | tf_op jit(solution)/shard_map/ppermute | solution.py:707
  30.8 1.3 %collective-permute-start.3 = (f32[3,8,256]{2,1,0:T(8,128)S(1)}, f32[3,8,256]{2,1,0:T(8,128)S(1)}, u32[]{:S(2)}, u32[]{:S(2)}) collective-permute-start(f32[3,8,256]{2,1,0:T(8,128)S(1)} %slice_bitcast_fusion), channel_id=1, source_target_pairs={{1,18},{2,17},{3,20},{4,19},{5,22},{6,21},{7,24},{8,23},{9,26},{10... | collective-permute-start | bytes 73736 | tf_op jit(solution)/shard_map/ppermute | solution.py:707
  32.1 0.0 copy-done
  32.1 1.0 %shard_map.108.natural = f32[3,512,128]{2,1,0:T(8,128)S(1)} custom-call(f32[3,6,8,512]{3,2,1,0:T(8,128)S(1)} %get-tuple-element.36.early_rows, f32[3,12,8,512]{3,2,1,0:T(8,128)S(1)} %get-tuple-element.47.late_rows, f32[8,512]{1,0:T(8,128)S(1)} %get-tuple-element.43.depths, bf16[512,512]{1,0:T(8,128)(2,1)S(1)} %copy-done), custom_call_target="tpu_custom_call" | custom-call | tf_op jit(solution)/shard_map/pallas_call | solution.py:718
  33.0 4.8 %collective-permute-done.3.far_edge = f32[3,8,256]{2,1,0:T(8,128)S(1)} collective-permute-done((f32[3,8,256]{2,1,0:T(8,128)S(1)}, f32[3,8,256]{2,1,0:T(8,128)S(1)}, u32[]{:S(2)}, u32[]{:S(2)}) %collective-permute-start.3) | collective-permute-done | bytes 24608 | tf_op jit(solution)/shard_map/ppermute | solution.py:707
  37.8 0.0 collective-permute-done.2.incoming
  37.8 0.0 copy-done.1
  37.8 0.0 copy-done.2
  37.8 1.9 %shard_map.109 = (f32[3,512,128]{2,1,0:T(8,128)}, f32[3,128,128]{2,1,0:T(8,128)}) custom-call(f32[3,9,8,256]{3,2,1,0:T(8,128)S(1)} %collective-permute-done.2.incoming, f32[3,8,256]{2,1,0:T(8,128)S(1)} %collective-permute-done.3.far_edge, f32[3,8,8,256]{3,2,1,0:T(8,128)S(1)} %get-tuple-element.38.outcome.previous, ...), custom_call_target="tpu_custom_call" | custom-call | tf_op jit(solution)/shard_map/pallas_call | solution.py:727
  (1 shorter events, 0.0 us)
Async XLA Ops:
  3.9 3.8 %collective-permute-start.1 = (f32[46,8,512]{2,1,0:T(8,128)S(1)}, f32[46,8,512]{2,1,0:T(8,128)S(1)}, u32[]{:S(2)}, u32[]{:S(2)}) collective-permute-start(f32[46,8,512]{2,1,0:T(8,128)S(1)} %get-tuple-element.30.to_near), channel_id=1, source_target_pairs={{0,1},{1,0},{2,3},{3,2},{4,5},{5,4},{6,7},{7,6},{8,9},{9,8},{10,11... | collective-permute-start | bytes 2261000 | tf_op jit(solution)/shard_map/ppermute | solution.py:672
  4.6 18.2 %collective-permute-start = (f32[38,8,512]{2,1,0:T(8,128)S(1)}, f32[38,8,512]{2,1,0:T(8,128)S(1)}, u32[]{:S(2)}, u32[]{:S(2)}) collective-permute-start(f32[38,8,512]{2,1,0:T(8,128)S(1)} %get-tuple-element.26.to_far), channel_id=1, source_target_pairs={{1,2},{2,1},{3,4},{4,3},{5,6},{6,5},{7,8},{8,7},{9,10},{10,9},{11,... | collective-permute-start | bytes 1867784 | tf_op jit(solution)/shard_map/ppermute | solution.py:665
  22.9 9.2 %copy-start = (bf16[512,512]{1,0:T(8,128)(2,1)S(1)}, bf16[512,512]{1,0:T(8,128)(2,1)}, u32[]{:S(2)}) copy-start(bf16[512,512]{1,0:T(8,128)(2,1)} %constant.9.clone.matrix) | copy-start | bytes 1572868
  22.9 15.0 %copy-start.1 = (bf16[256,512]{1,0:T(8,128)(2,1)S(1)}, bf16[256,512]{1,0:T(8,128)(2,1)}, u32[]{:S(2)}) copy-start(bf16[256,512]{1,0:T(8,128)(2,1)} %constant.11.clone.spread) | copy-start | bytes 786436
  22.9 15.0 %copy-start.2 = (bf16[256,256]{1,0:T(8,128)(2,1)S(1)}, bf16[256,256]{1,0:T(8,128)(2,1)}, u32[]{:S(2)}) copy-start(bf16[256,256]{1,0:T(8,128)(2,1)} %constant.10.clone.order) | copy-start | bytes 393220
  29.5 8.4 %collective-permute-start.2 = (f32[3,9,8,256]{3,2,1,0:T(8,128)S(1)}, f32[3,9,8,256]{3,2,1,0:T(8,128)S(1)}, u32[]{:S(2)}, u32[]{:S(2)}) collective-permute-start(f32[3,9,8,256]{3,2,1,0:T(8,128)S(1)} %get-tuple-element.45), channel_id=1, source_target_pairs={{0,16},{1,17},{2,18},{3,19},{4,20},{5,21},{6,22},{7,23},{8,24},{9,... | collective-permute-start | bytes 663560 | tf_op jit(solution)/shard_map/ppermute | solution.py:707
  30.8 7.1 %collective-permute-start.3 = (f32[3,8,256]{2,1,0:T(8,128)S(1)}, f32[3,8,256]{2,1,0:T(8,128)S(1)}, u32[]{:S(2)}, u32[]{:S(2)}) collective-permute-start(f32[3,8,256]{2,1,0:T(8,128)S(1)} %slice_bitcast_fusion), channel_id=1, source_target_pairs={{1,18},{2,17},{3,20},{4,19},{5,22},{6,21},{7,24},{8,23},{9,26},{10... | collective-permute-start | bytes 73736 | tf_op jit(solution)/shard_map/ppermute | solution.py:707
